TPU v7x, 256 devices: a whole 4x4x8 slice. The times are simulated.
256 devices in a mesh: req: 32 (over x, y, core), tp: 8 (over z).
Axes of the slice: x: 4, y: 4, z: 8, core: 2. Of those that a mesh axis runs over, the one named last changes fastest.
Arguments:
- hidden: bfloat16 [1024, 24, 2560], P('req', None, 'tp'), may hold values from -6 to 6
- norm_gain: float32 [2560], replicated, may hold values from 0.25 to 1.75
- w_query: bfloat16 [2560, 2560], P(None, 'tp'), may hold values from -0.125 to 0.125
- w_keyval: bfloat16 [1280, 2560], P('tp'), may hold values from -0.125 to 0.125
- w_out: bfloat16 [2560, 2560], P('tp'), may hold values from -0.25 to 0.25
- kv_cache: bfloat16 [1024, 1280, 512], P('req', 'tp'), as said below
- lengths: int32 [1024], P('req'), may hold values from 2 to 508, as said below
- parents: int32 [1024, 24], P('req'), may hold values from 0 to 22, as said below
- accepted: int32 [1024, 4], P('req'), may hold values from 0 to 6, as said below
- slot_of: int32 [1024], P('req'), may hold values from 0 to 1023, as said below
Outputs:
- out_rows: bfloat16 [1024, 24, 2560], P('req', None, 'tp')
- new_cache: bfloat16 [1024, 1280, 512], P('req', 'tp')
Inputs may be any that keep to these rules, and one draw needn't show every extreme that they name: `lengths`: some request has exactly 508 cached tokens. parents[r, 0] = 0 and parents[r, t] is t - 1 or max(t - 2, 0) for t >= 1. accepted[r, m] is the tree token at depth m on the path from token 0 to one token of request r, so accepted[r, 0] = 0. A permutation; the 32 requests held by req index i go to 32 different req indices, one to each: a request of index i lands in slot d * 32 + i, where d = slot_of // 32. `kv_cache`: keys and values of cached tokens; positions at or past a request's length are not read.
All inputs are finite; a program needn't handle non-finite values.
Results may differ from a plain program's by a relative error of at most 0.012.
Values may be sent and summed in bfloat16 or wider, within the bound.
No kernel may reach another device: no remote copies, remote signals or barrier semaphores. Data moves between devices by JAX's collectives and lax.ppermute only.
A program may use at most 128 MiB of HBM per device.

v0:
```python
import math

import jax
import jax.numpy as jnp
from jax import lax
from jax.sharding import PartitionSpec as P

H = 32
KVH = 8
HD = 80


def ancestry(parents):
    tree_size = parents.shape[-1]
    tokens = jnp.arange(tree_size, dtype=jnp.int32)

    def follow(index_step, state):
        marks, depths, current = state
        marks = jnp.logical_or(marks, current[..., :, None] == tokens)
        depths = depths + (current != 0).astype(jnp.int32)
        current = jnp.take_along_axis(parents, current, axis=-1)
        return (marks, depths, current)

    start = jnp.broadcast_to(tokens, parents.shape)
    marks = jnp.zeros(parents.shape + (tree_size,), jnp.bool_)
    marks, depths, finished = lax.fori_loop(
        0, tree_size, follow, (marks, jnp.zeros(parents.shape, jnp.int32), start)
    )
    return (marks, depths)


def rope_tables(positions):
    frequency = 10000.0 ** (-2.0 * jnp.arange(HD // 2, dtype=jnp.float32) / HD)
    angles = positions.astype(jnp.float32)[..., None] * frequency
    return (jnp.cos(angles), jnp.sin(angles))


def rotate_pairs(values, cosines, sines):
    half_size = values.shape[-1] // 2
    first_half = values[..., :half_size]
    second_half = values[..., half_size:]
    return jnp.concatenate(
        [first_half * cosines - second_half * sines, second_half * cosines + first_half * sines],
        axis=-1,
    )


def place_columns(kept_rows, new_columns, start):
    return lax.dynamic_update_slice(kept_rows, new_columns, (jnp.zeros((), jnp.int32), start))


def verify_layer(rows, norm_gain, w_query, w_keyval, w_out, kv_cache, lengths, parents, accepted):
    requests, tree_size, shard_width = rows.shape
    cache_len = kv_cache.shape[2]
    group_size = H // KVH
    kv_local = w_keyval.shape[0] // (2 * HD)
    score_scale = 1.0 / math.sqrt(HD)
    full_rows = lax.all_gather(rows, "tp", axis=2, tiled=True)
    values = full_rows.astype(jnp.float32)
    spread = jnp.mean(values * values, axis=-1, keepdims=True)
    normed = (values * lax.rsqrt(spread + 1e-05) * norm_gain).astype(jnp.bfloat16)
    flat_rows = normed.reshape(requests * tree_size, -1)
    query = jnp.dot(flat_rows, w_query, preferred_element_type=jnp.float32).reshape(
        requests, tree_size, kv_local, group_size, HD
    )
    keyval = lax.dot_general(
        flat_rows, w_keyval, (((1,), (1,)), ((), ())), preferred_element_type=jnp.float32
    ).reshape(requests, tree_size, kv_local, 2, HD)
    ancestors, depths = ancestry(parents)
    cosines, sines = rope_tables(lengths[:, None] + depths)
    query = rotate_pairs(query, cosines[:, :, None, None], sines[:, :, None, None]).astype(
        jnp.bfloat16
    )
    keys = rotate_pairs(keyval[:, :, :, 0], cosines[:, :, None], sines[:, :, None]).astype(
        jnp.bfloat16
    )
    tree_values = keyval[:, :, :, 1].astype(jnp.bfloat16)
    cached = kv_cache.reshape(requests, kv_local, 2, HD, cache_len)
    cache_scores = (
        jnp.einsum("rtgqe,rgec->rgqtc", query, cached[:, :, 0], preferred_element_type=jnp.float32)
        * score_scale
    )
    tree_scores = (
        jnp.einsum("rtgqe,rsge->rgqts", query, keys, preferred_element_type=jnp.float32)
        * score_scale
    )
    positions = jnp.arange(cache_len, dtype=jnp.int32)
    live_rows = positions[None, :] < lengths[:, None]
    cache_scores = jnp.where(live_rows[:, None, None, None, :], cache_scores, -jnp.inf)
    tree_scores = jnp.where(ancestors[:, None, None, :, :], tree_scores, -jnp.inf)
    row_max = jnp.maximum(jnp.max(cache_scores, axis=-1), jnp.max(tree_scores, axis=-1))[..., None]
    cache_weights = jnp.exp(cache_scores - row_max)
    tree_weights = jnp.exp(tree_scores - row_max)
    denominator = (jnp.sum(cache_weights, axis=-1) + jnp.sum(tree_weights, axis=-1))[..., None]
    cache_probs = (cache_weights / denominator).astype(jnp.bfloat16)
    tree_probs = (tree_weights / denominator).astype(jnp.bfloat16)
    context = jnp.einsum(
        "rgqtc,rgec->rtgqe", cache_probs, cached[:, :, 1], preferred_element_type=jnp.float32
    )
    context = context + jnp.einsum(
        "rgqts,rsge->rtgqe", tree_probs, tree_values, preferred_element_type=jnp.float32
    )
    context = context.astype(jnp.bfloat16).reshape(requests * tree_size, -1)
    partial_value = jnp.dot(context, w_out, preferred_element_type=jnp.float32).reshape(
        requests, tree_size, -1
    )
    summed = lax.psum_scatter(
        partial_value.astype(jnp.bfloat16), "tp", scatter_dimension=2, tiled=True
    ).astype(jnp.float32)
    out_rows = (rows.astype(jnp.float32) + summed).astype(jnp.bfloat16)
    tree_kv = jnp.stack([keys, tree_values], axis=3).reshape(requests, tree_size, -1)
    accepted_kv = jnp.transpose(
        jnp.take_along_axis(tree_kv, accepted[:, :, None], axis=1), (0, 2, 1)
    )
    kept = jnp.where(live_rows[:, None, :], kv_cache, jnp.zeros((), jnp.bfloat16))
    compacted = jax.vmap(place_columns)(kept, accepted_kv, lengths)
    return (out_rows, compacted)


def per_device(
    hidden, norm_gain, w_query, w_keyval, w_out, kv_cache, lengths, parents, accepted, slot_of
):
    held_count = hidden.shape[0]
    destination = slot_of // held_count
    peer_index = jnp.arange(held_count, dtype=jnp.int32)
    matches = (destination[None, :] == peer_index[:, None]).astype(jnp.int32)
    send_order = jnp.sum(matches * peer_index[None, :], axis=1)
    out_rows, compacted = verify_layer(
        hidden, norm_gain, w_query, w_keyval, w_out, kv_cache, lengths, parents, accepted
    )
    new_cache = lax.all_to_all(
        jnp.take(compacted, send_order, axis=0), "req", split_axis=0, concat_axis=0, tiled=True
    )
    return (out_rows, new_cache)


def solution(mesh):
    in_specs = (
        P("req", None, "tp"),
        P(),
        P(None, "tp"),
        P("tp", None),
        P("tp", None),
        P("req", "tp", None),
        P("req"),
        P("req", None),
        P("req", None),
        P("req"),
    )
    out_specs = (P("req", None, "tp"), P("req", "tp", None))
    return jax.shard_map(
        per_device, mesh=mesh, in_specs=in_specs, out_specs=out_specs, check_vma=False
    )
```

profile of v0, /device:TPU:1, one launch (start us, length us, event | category | flops | bytes accessed | tf_op | source)
XLA Modules:
  0.0 669.3 jit_solution(16635566112242576531)
XLA Ops:
  7.2 4.1 copy.62
  11.5 142.3 %while.17 = (s32[]{:T(128)}, pred[32,24,24]{2,1,0:T(8,128)(4,1)S(1)}, s32[32,24]{1,0:T(8,128)S(1)}, s32[32,24]{1,0:T(8,128)S(1)}, s32[32,24]{0,1:T(8,128)S(1)}, /*index=5*/s32[]{:T(128)}, s32[]{:T(128)}) while((s32[]{:T(128)}, pred[32,24,24]{2,1,0:T(8,128)(4,1)S(1)}, s32[32,24]{1,0:T(8,128)S(1)}, s32[32,24]{1,0:T(8,128)S(1)}, ...), condition=%wide.region_2.3_spmd.clone, body=%wide.region_1.2_spmd.clone.sunk | while | flops 69891 | bytes 86104 | solution.py:26
  12.0 5.3 gather_fusion
  17.9 5.3 gather_fusion
  23.8 5.3 gather_fusion
  29.8 5.3 gather_fusion
  35.7 5.3 gather_fusion
  41.6 5.3 gather_fusion
  47.5 5.3 gather_fusion
  53.5 5.3 gather_fusion
  59.4 5.3 gather_fusion
  65.3 5.3 gather_fusion
  71.3 5.3 gather_fusion
  77.2 5.3 gather_fusion
  83.1 5.3 gather_fusion
  89.0 5.3 gather_fusion
  95.0 5.3 gather_fusion
  100.9 5.3 gather_fusion
  106.8 5.3 gather_fusion
  112.8 5.3 gather_fusion
  118.7 5.3 gather_fusion
  124.6 5.3 gather_fusion
  130.6 5.3 gather_fusion
  136.5 5.3 gather_fusion
  142.4 5.3 gather_fusion
  148.3 5.3 gather_fusion
  156.2 5.3 broadcast_select_fusion.1
  161.5 16.7 %all-gather.2.cloned.1.call-done = bf16[32,24,2560]{0,1,2:T(8,128)(2,1)} async-done(((bf16[32,24,320]{0,1,2:T(8,128)(2,1)}), bf16[32,24,2560]{0,1,2:T(8,128)(2,1)}) %all-gather.2.cloned.1.call-update) | async-done | bytes 3932176 | tf_op jit(solution)/shard_map/all_gather | solution.py:58
  178.2 18.6 %copy.63 = bf16[32,24,2560]{2,1,0:T(8,128)(2,1)} copy(bf16[32,24,2560]{0,1,2:T(8,128)(2,1)} %all-gather.2.cloned.1.call-done) | data formatting | bytes 7864320 | tf_op jit(solution)/shard_map/all_gather | solution.py:58
  196.9 3.1 fusion.3
  218.7 5.1 convolution_convert_fusion
  223.8 18.5 %copy.81 = bf16[32,24,2560]{1,0,2:T(8,128)(2,1)} copy(bf16[32,24,2560]{2,1,0:T(8,128)(2,1)} %convolution_convert_fusion) | data formatting | bytes 7864320
  242.3 29.8 %reshape.345 = bf16[2560,768]{1,0:T(8,128)(2,1)} reshape(bf16[2560,32,24]{2,1,0:T(8,128)(2,1)} %bitcast.178) | data formatting | bytes 7864320
  274.1 293.6 %while.16 = (s32[]{:T(128)}, bf16[32,160,512]{2,1,0:T(8,128)(2,1)}, s32[32,3]{0,1:T(4,128)S(1)}, bf16[32,160,4]{1,2,0:T(4,128)(2,1)S(1)}, s32[]{:T(128)}, /*index=5*/s32[3]{0:T(128)S(1)}, s32[]{:T(128)}) while((s32[]{:T(128)}, bf16[32,160,512]{2,1,0:T(8,128)(2,1)}, s32[32,3]{0,1:T(4,128)S(1)}, bf16[32,160,4]{1,2,0:T(4,128)(2,1)S(1)}, s32[]{:T(128)}, ...), condition=%wide.while_cond, body=%wide.while_body.sunk | while | flops 659 | bytes 11691 | solution.py:49
  280.3 3.0 dynamic-update-slice.3
  289.5 3.0 dynamic-update-slice.3
  298.7 3.0 dynamic-update-slice.3
  307.9 3.0 dynamic-update-slice.3
  317.1 3.0 dynamic-update-slice.3
  326.2 3.0 dynamic-update-slice.3
  344.6 3.0 dynamic-update-slice.3
  353.8 3.0 dynamic-update-slice.3
  567.7 5.7 gather_fusion.1
  573.3 3.1 broadcast_select_fusion
  576.4 69.3 %all_to_all.5 = bf16[32,160,512]{2,1,0:T(8,128)(2,1)} all-to-all(bf16[32,160,512]{2,1,0:T(8,128)(2,1)S(1)} %broadcast_select_fusion), channel_id=1, replica_groups=mesh['req'=32,'tp'=8] {'req'}, dimensions={0} | all-to-all | bytes 10485760 | tf_op jit(solution)/shard_map/all_to_all | solution.py:131
  645.7 6.1 reshape.346
  651.8 4.3 copy.82
  657.1 5.4 copy.109
  (413 shorter events, 306.7 us)
Async XLA Ops:
  7.2 211.5 %copy-start = (bf16[320,2560]{1,0:T(8,128)(2,1)S(1)}, bf16[320,2560]{1,0:T(8,128)(2,1)}, u32[]{:S(2)}) copy-start(bf16[320,2560]{1,0:T(8,128)(2,1)} %param.16) | copy-start | bytes 4915204
  7.2 4.2 copy-start.1
  7.2 171.1 %all-gather.2.cloned.1.call-start = ((), (), s32[]{:S(2)}) async-start(), calls=%async_computation.2 | async-start | bytes 17694720 | tf_op jit(solution)/shard_map/all_gather | solution.py:58
  11.3 634.4 %reduce-scatter.4.cloned.1.call-start = ((), (), s32[]{:S(2)}) async-start(), calls=%async_computation.3 | async-start | bytes 4423680
  11.4 142.6 %copy-start.5 = (s32[32,4]{0,1:T(4,128)S(1)}, s32[32,4]{0,1:T(4,128)}, u32[]{:S(2)}) copy-start(s32[32,4]{0,1:T(4,128)} %param.20) | copy-start | bytes 1540
  11.4 142.9 %copy-start.6 = (s32[32]{0:T(128)S(1)}, s32[32]{0:T(128)}, u32[]{:S(2)}) copy-start(s32[32]{0:T(128)} %param.18) | copy-start | bytes 388
  11.5 143.0 %copy-start.9 = (s32[32]{0:T(128)S(1)}, s32[32]{0:T(128)}, u32[]{:S(2)}) copy-start(s32[32]{0:T(128)} %param.21) | copy-start | bytes 388
  196.9 3.3 copy-start.2
  196.9 3.3 copy-start.8
  200.2 2.9 copy-start.7
  203.0 4.8 slice-start
  203.0 4.8 slice-start.1
  272.1 2.0 copy-start.4
  645.7 10.4 %copy-start.3 = (bf16[32,24,320]{2,1,0:T(8,128)(2,1)S(1)}, bf16[32,24,320]{2,1,0:T(8,128)(2,1)}, u32[]{:S(2)}) copy-start(bf16[32,24,320]{2,1,0:T(8,128)(2,1)} %param.12) | copy-start | bytes 1474564
Sparse Core Ops, SparseCore 0:
  11.5 166.7 all-gather.1
  272.2 51.5 reduce-scatter.3
where the time goes:
time: 677 us; the launch traced here: 669 us
  local copies, waits for them, and re-layouts  349 us (52%)
  other arithmetic  202 us (30%)
  blocking collectives  69.3 us (10%)
  waiting for transfers between devices  16.7 us (2%)
  matrix products  16.5 us (2%)
  between operations  14.4 us (2%)
    scatter x64, other arithmetic  172 us
    gather x72, local copies, waits for them, and re-layouts, follow(): current = jnp.take_along_axis(parents, current, axis=-1)  132 us
    scatter x160, local copies, waits for them, and re-layouts  121 us
    all_to_all x1, blocking collectives, per_device(): lax.all_to_all(jnp.take(compacted, send_order, axis=0), 'req', split_axis...  69.3 us
    unnamed x31, local copies, waits for them, and re-layouts  68.3 us
    all_gather x1, local copies, waits for them, and re-layouts, verify_layer(): full_rows = lax.all_gather(rows, 'tp', axis=2, tiled=True)  18.6 us
    all_gather x1, waiting for transfers between devices, verify_layer(): full_rows = lax.all_gather(rows, 'tp', axis=2, tiled=True)  16.7 us
  transfers between devices with their start and end apart: 2, of which 1 were waited for; matrix products, arithmetic and copies ran while one was open for 68% of the time, Pallas kernels for 0%

commit v1 on v0

v1 whole, which is shorter than its diff:
```python
import math

import jax
import jax.numpy as jnp
from jax import lax
from jax.experimental import pallas as pl
from jax.experimental.pallas import tpu as pltpu
from jax.sharding import PartitionSpec as P

H = 32
KVH = 8
HD = 80
D = 2560
TREE = 24
CACHE = 512
DEPTH = 4
N_TP = 8
GROUP = H // KVH
LANES = 128
REQ_BLOCK = 8
ROWS = REQ_BLOCK * TREE
HALF = ROWS // 2
PACKED = 2 * ROWS + HALF
WIDTH = D // N_TP
NEG = -1e30
EXTRA = 16
BF = jnp.bfloat16
F32 = jnp.float32
VMEM_LIMIT = 56 * 1024 * 1024


def lane_index(shape):
    return lax.broadcasted_iota(jnp.int32, shape, len(shape) - 1)


def swap_halves(tile):
    return pltpu.roll(tile, 64, 1)


def pack_kernel(parity, x_ref, o_ref):
    x = x_ref[...].astype(F32)
    t0 = x[:, 0:128]
    t1 = x[:, 128:256]
    t2 = jnp.concatenate([x[:, 256:320], jnp.zeros((ROWS, 64), F32)], axis=1)
    low = lane_index((ROWS, LANES)) < 64
    low_half = lane_index((HALF, LANES)) < 64
    even = jnp.bitwise_and(parity[0], 1) == 0

    @pl.when(even)
    def _():
        o_ref[0, 0:ROWS] = t0.astype(BF)
        o_ref[0, ROWS : 2 * ROWS] = t1.astype(BF)
        o_ref[0, 2 * ROWS : PACKED] = jnp.where(
            low_half, t2[:HALF], swap_halves(t2[HALF:])
        ).astype(BF)

    @pl.when(jnp.logical_not(even))
    def _():
        s0, s1, s2 = swap_halves(t0), swap_halves(t1), swap_halves(t2)
        o_ref[0, 0:ROWS] = jnp.where(low, s0, s1).astype(BF)
        o_ref[0, ROWS : 2 * ROWS] = jnp.where(low, s1, s2).astype(BF)
        o_ref[0, 2 * ROWS : PACKED] = jnp.where(low_half, t0[:HALF], s0[HALF:]).astype(BF)


def pack_rows(rows, parity):
    blocks = rows.shape[0] // ROWS
    return pl.pallas_call(
        pack_kernel,
        out_shape=jax.ShapeDtypeStruct((blocks, PACKED, LANES), BF),
        grid_spec=pltpu.PrefetchScalarGridSpec(
            num_scalar_prefetch=1,
            grid=(blocks,),
            in_specs=[pl.BlockSpec((ROWS, WIDTH), lambda b, p: (b, 0))],
            out_specs=pl.BlockSpec((1, PACKED, LANES), lambda b, p: (b, 0, 0)),
        ),
        name="pack_rows",
    )(parity, rows)


def finish_kernel(parity, s_ref, x_ref, o_ref):
    m0 = s_ref[0, 0:ROWS].astype(F32)
    m1 = s_ref[0, ROWS : 2 * ROWS].astype(F32)
    packed_tail = s_ref[0, 2 * ROWS : PACKED].astype(F32)
    tail = jnp.concatenate([packed_tail, swap_halves(packed_tail)], axis=0)
    low = lane_index((ROWS, LANES)) < 64
    even = jnp.bitwise_and(parity[0], 1) == 0

    @pl.when(even)
    def _():
        total = jnp.concatenate([m0, m1, tail], axis=1)[:, :WIDTH]
        o_ref[...] = (x_ref[...].astype(F32) + total).astype(BF)

    @pl.when(jnp.logical_not(even))
    def _():
        s0, s1 = swap_halves(m0), swap_halves(m1)
        total = jnp.concatenate(
            [jnp.where(low, tail, s0), jnp.where(low, s0, s1), s1], axis=1
        )[:, :WIDTH]
        o_ref[...] = (x_ref[...].astype(F32) + total).astype(BF)


def finish_rows(summed, rows, parity):
    blocks = rows.shape[0] // ROWS
    return pl.pallas_call(
        finish_kernel,
        out_shape=jax.ShapeDtypeStruct(rows.shape, BF),
        grid_spec=pltpu.PrefetchScalarGridSpec(
            num_scalar_prefetch=1,
            grid=(blocks,),
            in_specs=[
                pl.BlockSpec((1, PACKED, LANES), lambda b, p: (b, 0, 0)),
                pl.BlockSpec((ROWS, WIDTH), lambda b, p: (b, 0)),
            ],
            out_specs=pl.BlockSpec((ROWS, WIDTH), lambda b, p: (b, 0)),
        ),
        name="finish_rows",
    )(parity, summed, rows)


def prep_kernel(parents_ref, cos_ref, sin_ref, step_ref, bias_out, cos_out, sin_out):
    requests = parents_ref.shape[0]
    lane = lane_index((requests, LANES))
    step_cos = step_ref[0:1, :]
    step_sin = step_ref[1:2, :]
    sign = step_ref[2:3, :]
    parents = parents_ref[...]
    marks = jnp.where(lane == 0, 1.0, 0.0)
    cosines, sines = cos_ref[...], sin_ref[...]
    older = (marks, cosines, sines)
    newer = older
    for t in range(TREE):
        if t > 0:
            near = jnp.broadcast_to(parents[:, t : t + 1], (requests, LANES)) == t - 1
            marks, cosines, sines = (jnp.where(near, a, b) for a, b in zip(newer, older))
            marks = jnp.where(lane == t, 1.0, marks)
            if t > 0:
                cosines, sines = (
                    cosines * step_cos - sines * step_sin,
                    sines * step_cos + cosines * step_sin,
                )
            older, newer = newer, (marks, cosines, sines)
        bias_out[:, t, :] = jnp.where(marks > 0.5, 0.0, NEG)
        cos_out[:, t, :] = cosines
        sin_out[:, t, :] = sines * sign


def prepare_tables(parents, lengths):
    requests = parents.shape[0]
    lane = jnp.arange(LANES)
    pair = jnp.where(lane < HD // 2, lane, lane - HD // 2)
    frequency = 10000.0 ** (-2.0 * pair.astype(F32) / HD)
    angles = lengths.astype(F32)[:, None] * frequency[None, :]
    sign = jnp.where(lane < HD // 2, -1.0, jnp.where(lane < HD, 1.0, 0.0))
    steps = jnp.stack([jnp.cos(frequency), jnp.sin(frequency), sign] + [sign] * 5)
    table = jax.ShapeDtypeStruct((requests, TREE, LANES), F32)
    return pl.pallas_call(
        prep_kernel, out_shape=(table, table, table), name="prepare_tables"
    )(parents, jnp.cos(angles), jnp.sin(angles), steps)


def order_kernel(order, cache_ref, key_ref, value_ref, key_sems, value_sems):
    copies = []
    for d in range(cache_ref.shape[0]):
        source = order[d]
        copies.append(
            pltpu.make_async_copy(
                cache_ref.at[source, pl.ds(0, HD)], key_ref.at[d], key_sems.at[d]
            )
        )
        copies.append(
            pltpu.make_async_copy(
                cache_ref.at[source, pl.ds(HD, HD)],
                value_ref.at[d, pl.ds(0, HD)],
                value_sems.at[d],
            )
        )
    for copy in copies:
        copy.start()
    for copy in copies:
        copy.wait()


def order_cache(kv_cache, send_order):
    held = kv_cache.shape[0]
    return pl.pallas_call(
        order_kernel,
        out_shape=(
            jax.ShapeDtypeStruct((held, HD, CACHE), BF),
            jax.ShapeDtypeStruct((held, HD + EXTRA, CACHE), BF),
        ),
        grid_spec=pltpu.PrefetchScalarGridSpec(
            num_scalar_prefetch=1,
            grid=(1,),
            in_specs=[pl.BlockSpec(memory_space=pl.ANY)],
            out_specs=(pl.BlockSpec(memory_space=pl.ANY), pl.BlockSpec(memory_space=pl.ANY)),
            scratch_shapes=[
                pltpu.SemaphoreType.DMA((held,)),
                pltpu.SemaphoreType.DMA((held,)),
            ],
        ),
        name="order_cache",
    )(send_order, kv_cache)


def layer_kernel(
    lengths,
    accepted,
    destination,
    x_ref,
    wq_ref,
    wkv_ref,
    wo_ref,
    cache_ref,
    bias_ref,
    cos_ref,
    sin_ref,
    send_in,
    out_ref,
    send_out,
    xs,
    qkv,
    ctx,
    wo,
    extra,
    sems,
    *,
    first_block,
):
    b = pl.program_id(0)

    @pl.when(b == 0)
    def _():
        wo[...] = jnp.zeros_like(wo)
        for h in range(GROUP):
            wo[h * LANES : h * LANES + HD] = wo_ref[h * HD : (h + 1) * HD]
        ctx[...] = jnp.zeros_like(ctx)
        extra[...] = jnp.zeros_like(extra)

    low_half = lane_index((HALF, LANES)) < 64
    squares = jnp.zeros((ROWS, LANES), F32)
    for j in range(N_TP // 2):
        base = j * 5 * LANES
        for device, at in ((2 * j, base), (2 * j + 1, base + 3 * LANES)):
            for part in range(2):
                piece = x_ref[device, 0, part * ROWS : (part + 1) * ROWS]
                xs[:, at + part * LANES : at + (part + 1) * LANES] = piece
                wide = piece.astype(F32)
                squares = squares + wide * wide
        even_tail = x_ref[2 * j, 0, 2 * ROWS : PACKED].astype(F32)
        odd_tail = x_ref[2 * j + 1, 0, 2 * ROWS : PACKED].astype(F32)
        tail = jnp.concatenate(
            [
                jnp.where(low_half, even_tail, swap_halves(odd_tail)),
                jnp.where(low_half, swap_halves(even_tail), odd_tail),
            ],
            axis=0,
        )
        xs[:, base + 2 * LANES : base + 3 * LANES] = tail.astype(BF)
        squares = squares + tail * tail
    scale = lax.rsqrt(jnp.sum(squares, axis=1, keepdims=True) * (1.0 / D) + 1e-05)
    flat = xs[...]
    query = jnp.dot(flat, wq_ref[...], preferred_element_type=F32) * scale
    keyval = jnp.dot(flat, wkv_ref[...], preferred_element_type=F32) * scale
    cosines = cos_ref[...].reshape(ROWS, LANES)
    sines = sin_ref[...].reshape(ROWS, LANES)
    first = lane_index((ROWS, LANES)) < HD // 2

    def rotate(tile):
        other = jnp.where(
            first, pltpu.roll(tile, LANES - HD // 2, 1), pltpu.roll(tile, HD // 2, 1)
        )
        return tile * cosines + other * sines

    for h in range(GROUP):
        qkv[:, h * LANES : (h + 1) * LANES] = rotate(query[:, h * LANES : (h + 1) * LANES])
    qkv[:, GROUP * LANES : (GROUP + 1) * LANES] = rotate(keyval[:, :LANES])
    qkv[:, (GROUP + 1) * LANES :] = keyval[:, LANES:]

    factor = math.log2(math.e) / math.sqrt(HD)
    column = lane_index((GROUP * TREE, CACHE))
    extra_row = lax.broadcasted_iota(jnp.int32, (EXTRA, LANES), 0)
    pick_row = lax.broadcasted_iota(jnp.int32, (EXTRA, TREE), 0)
    pick_column = lane_index((EXTRA, TREE))
    copies = []
    for i in range(REQ_BLOCK):
        r = (first_block + b) * REQ_BLOCK + i
        length = lengths[r]
        rows = slice(i * TREE, (i + 1) * TREE)
        q = jnp.concatenate(
            [qkv[rows, h * LANES : (h + 1) * LANES] for h in range(GROUP)], axis=0
        ).astype(BF)
        k = qkv[rows, GROUP * LANES : (GROUP + 1) * LANES].astype(BF)
        v = qkv[rows, (GROUP + 1) * LANES :].astype(BF)
        cached = jnp.dot(q[:, :HD], cache_ref[i, 0:HD], preferred_element_type=F32)
        cached = jnp.where(column < length, cached * factor, NEG)
        fresh = lax.dot_general(q, k, (((1,), (1,)), ((), ())), preferred_element_type=F32)
        bias = bias_ref[i][:, :TREE]
        fresh = fresh * factor + jnp.concatenate([bias] * GROUP, axis=0)
        top = jnp.maximum(
            jnp.max(cached, axis=1, keepdims=True), jnp.max(fresh, axis=1, keepdims=True)
        )
        cached = jnp.exp2(cached - top)
        fresh = jnp.exp2(fresh - top)
        total = jnp.sum(cached, axis=1, keepdims=True) + jnp.sum(fresh, axis=1, keepdims=True)
        mixed = lax.dot_general(
            cached.astype(BF),
            cache_ref[i, HD : 2 * HD],
            (((1,), (1,)), ((), ())),
            preferred_element_type=F32,
        ) + jnp.dot(fresh.astype(BF), v[:, :HD], preferred_element_type=F32)
        mixed = mixed / total
        for h in range(GROUP):
            ctx[rows, h * LANES : h * LANES + HD] = mixed[h * TREE : (h + 1) * TREE]

        wanted = jnp.full((EXTRA, TREE), -1, jnp.int32)
        for m in range(DEPTH):
            wanted = jnp.where(pick_row == m, accepted[r * DEPTH + m], wanted)
        pick = jnp.where(pick_column == wanted, 1.0, 0.0).astype(BF)
        new_keys = jnp.dot(pick, k, preferred_element_type=F32)
        new_values = jnp.dot(pick, v, preferred_element_type=F32)
        coarse = (length // 16).astype(F32)
        fine = (length % 16).astype(F32)
        new_keys = jnp.where(extra_row == 8, coarse, jnp.where(extra_row == 9, fine, new_keys))
        extra[i, :, 0:LANES] = new_keys.astype(BF)
        extra[i, :, LANES : 2 * LANES] = new_values.astype(BF)
        copies.append(
            pltpu.make_async_copy(
                extra.at[i], send_out.at[destination[r], pl.ds(HD, EXTRA)], sems.at[i]
            )
        )
        copies[-1].start()

    partial = jnp.dot(ctx[...].astype(BF), wo[...], preferred_element_type=F32)
    for j in range(N_TP // 2):
        base = j * 5 * LANES
        for device, at in ((2 * j, base), (2 * j + 1, base + 3 * LANES)):
            for part in range(2):
                out_ref[device, 0, part * ROWS : (part + 1) * ROWS] = partial[
                    :, at + part * LANES : at + (part + 1) * LANES
                ].astype(BF)
        tail = partial[:, base + 2 * LANES : base + 3 * LANES]
        out_ref[2 * j, 0, 2 * ROWS : PACKED] = jnp.where(
            low_half, tail[:HALF], swap_halves(tail[HALF:])
        ).astype(BF)
        out_ref[2 * j + 1, 0, 2 * ROWS : PACKED] = jnp.where(
            low_half, swap_halves(tail[:HALF]), tail[HALF:]
        ).astype(BF)
    for copy in copies:
        copy.wait()


def verify_layer(
    gathered, wq, wkv, w_out, kv_cache, tables, lengths, accepted, destination, send, first_block
):
    blocks = gathered.shape[1]
    full = lambda b, *_: (0, 0)
    packed = pl.BlockSpec((N_TP, 1, PACKED, LANES), lambda b, *_: (0, b, 0, 0))
    table = pl.BlockSpec((REQ_BLOCK, TREE, LANES), lambda b, *_: (first_block + b, 0, 0))
    anywhere = pl.BlockSpec(memory_space=pl.ANY)

    def body(*refs):
        layer_kernel(*refs, first_block=first_block)

    return pl.pallas_call(
        body,
        out_shape=(
            jax.ShapeDtypeStruct((N_TP, blocks, PACKED, LANES), BF),
            jax.ShapeDtypeStruct(send.shape, BF),
        ),
        grid_spec=pltpu.PrefetchScalarGridSpec(
            num_scalar_prefetch=3,
            grid=(blocks,),
            in_specs=[
                packed,
                pl.BlockSpec(wq.shape, full),
                pl.BlockSpec(wkv.shape, full),
                pl.BlockSpec(w_out.shape, full),
                pl.BlockSpec(
                    (REQ_BLOCK, 2 * HD, CACHE), lambda b, *_: (first_block + b, 0, 0)
                ),
                table,
                table,
                table,
                anywhere,
            ],
            out_specs=(packed, anywhere),
            scratch_shapes=[
                pltpu.VMEM((ROWS, D), BF),
                pltpu.VMEM((ROWS, (GROUP + 2) * LANES), F32),
                pltpu.VMEM((ROWS, GROUP * LANES), F32),
                pltpu.VMEM((GROUP * LANES, D), BF),
                pltpu.VMEM((REQ_BLOCK, EXTRA, CACHE), BF),
                pltpu.SemaphoreType.DMA((REQ_BLOCK,)),
            ],
        ),
        input_output_aliases={11: 1},
        compiler_params=pltpu.CompilerParams(vmem_limit_bytes=VMEM_LIMIT),
        name="verify_layer",
    )(
        lengths,
        accepted,
        destination,
        gathered,
        wq,
        wkv,
        w_out,
        kv_cache,
        *tables,
        send,
    )


def assemble_kernel(key_ref, value_ref, o_ref):
    column = lane_index((HD, CACHE))
    place_row = lax.broadcasted_iota(jnp.int32, (EXTRA, CACHE), 0)
    place_column = lane_index((EXTRA, CACHE))
    for i in range(key_ref.shape[0]):
        extra = value_ref[i, HD : HD + EXTRA]
        wide = extra[:, :LANES].astype(F32)
        length = (wide[8:9] * 16.0 + wide[9:10]).astype(jnp.int32)
        length = jnp.concatenate([length] * (CACHE // LANES), axis=1)
        place = jnp.where(
            jnp.logical_and(place_column == length + place_row, place_row < DEPTH), 1.0, 0.0
        ).astype(BF)
        live = column < length
        for part, ref in ((0, key_ref), (1, value_ref)):
            new = lax.dot_general(
                extra[:, part * LANES : part * LANES + LANES],
                place,
                (((0,), (0,)), ((), ())),
                preferred_element_type=F32,
            )[:HD]
            o_ref[i, part * HD : (part + 1) * HD] = jnp.where(
                live, ref[i, 0:HD].astype(F32), new
            ).astype(BF)


def assemble_cache(keys, values):
    held = keys.shape[0]
    step = 4
    return pl.pallas_call(
        assemble_kernel,
        out_shape=jax.ShapeDtypeStruct((held, 2 * HD, CACHE), BF),
        grid=(held // step,),
        in_specs=[
            pl.BlockSpec((step, HD, CACHE), lambda s: (s, 0, 0)),
            pl.BlockSpec((step, HD + EXTRA, CACHE), lambda s: (s, 0, 0)),
        ],
        out_specs=pl.BlockSpec((step, 2 * HD, CACHE), lambda s: (s, 0, 0)),
        name="assemble_cache",
    )(keys, values)


def spread_heads(heads):
    source = jnp.arange(heads * HD)[:, None]
    target = jnp.arange(heads * LANES)[None, :]
    return (source // HD * LANES + source % HD == target).astype(BF)


def exchange(values):
    return lax.all_to_all(values, "req", split_axis=0, concat_axis=0, tiled=True)


def per_device(
    hidden, norm_gain, w_query, w_keyval, w_out, kv_cache, lengths, parents, accepted, slot_of
):
    held = hidden.shape[0]
    rows = hidden.reshape(held * TREE, WIDTH)
    parity = lax.axis_index("tp").astype(jnp.int32).reshape(1)
    packed = pack_rows(rows, parity)
    gathered = lax.all_gather(packed, "tp", axis=0, tiled=False)

    destination = slot_of // held
    peer_index = jnp.arange(held, dtype=jnp.int32)
    matches = (destination[None, :] == peer_index[:, None]).astype(jnp.int32)
    send_order = jnp.sum(matches * peer_index[None, :], axis=1)
    key_send, value_send = order_cache(kv_cache, send_order)
    key_received = exchange(key_send)

    tables = prepare_tables(parents, lengths)
    gain = norm_gain[:, None]
    wq = (jnp.dot(w_query, spread_heads(GROUP), preferred_element_type=F32) * gain).astype(BF)
    wkv = lax.dot_general(
        w_keyval, spread_heads(2), (((0,), (0,)), ((), ())), preferred_element_type=F32
    )
    wkv = (wkv * gain).astype(BF)

    key_received, value_send = lax.optimization_barrier((key_received, value_send))
    partial, value_send = verify_layer(
        gathered,
        wq,
        wkv,
        w_out,
        kv_cache,
        tables,
        lengths,
        accepted.reshape(-1),
        destination,
        value_send,
        0,
    )
    summed = lax.psum_scatter(partial, "tp", scatter_dimension=0, tiled=True)
    value_received = exchange(value_send)
    new_cache = assemble_cache(key_received, value_received)
    out_rows = finish_rows(summed.reshape(-1, PACKED, LANES), rows, parity)
    return (out_rows.reshape(hidden.shape), new_cache)


def solution(mesh):
    in_specs = (
        P("req", None, "tp"),
        P(),
        P(None, "tp"),
        P("tp", None),
        P("tp", None),
        P("req", "tp", None),
        P("req"),
        P("req", None),
        P("req", None),
        P("req"),
    )
    out_specs = (P("req", None, "tp"), P("req", "tp", None))
    return jax.shard_map(
        per_device, mesh=mesh, in_specs=in_specs, out_specs=out_specs, check_vma=False
    )
```

time: 677 us -> 305 us (0.45); the launches traced: 669 us -> 304 us
  local copies, waits for them, and re-layouts: 349 us -> 2.06 us
  Pallas kernels: 0 us -> 204 us
  other arithmetic: 202 us -> 2.19 us
  blocking collectives: 69.3 us -> 44.9 us
  matrix products: 16.5 us -> 5.15 us
  starting transfers between devices: 0.08 us -> 8.86 us
    pallas_call x0 -> x6, Pallas kernels: none -> 204 us  [the longest x1 161 us: order_cache(): pl.pallas_call(order_kernel, out_shape=(jax.ShapeDtypeStruct((held, HD, C...]
    scatter x65 -> x0, other arithmetic: 172 us -> none
    gather x77 -> x0, local copies, waits for them, and re-layouts: 139 us -> none  [the longest x72 132 us: follow(): current = jnp.take_along_axis(parents, current, axis=-1)]
    scatter x160 -> x0, local copies, waits for them, and re-layouts: 121 us -> none
    unnamed x31 -> x16, local copies, waits for them, and re-layouts: 68.3 us -> 0.8 us
    all_to_all x1, blocking collectives: 69.3 us -> 44.9 us  [exchange(): lax.all_to_all(values, 'req', split_axis=0, concat_axis=0, tiled=True)]
    all_to_all x0 -> x1, waiting for transfers between devices: none -> 23.2 us  [exchange(): lax.all_to_all(values, 'req', split_axis=0, concat_axis=0, tiled=True)]
    all_gather x1 -> x0, local copies, waits for them, and re-layouts: 18.6 us -> none  [verify_layer(): full_rows = lax.all_gather(rows, 'tp', axis=2, tiled=True)]
  transfers between devices with their start and end apart: 2 -> 3, of which waited for: 1 -> 1; matrix products, arithmetic and copies ran while one was open for 68% -> 3% of each run, Pallas kernels for 0% -> 57%
where the time goes in v1:
time: 305 us; the launch traced here: 304 us
  Pallas kernels  204 us (67%)
  blocking collectives  44.9 us (15%)
  waiting for transfers between devices  23.2 us (8%)
  between operations  14.2 us (5%)
  starting transfers between devices  8.86 us (3%)
  matrix products  5.15 us (2%)
    pallas_call x1, Pallas kernels, order_cache(): pl.pallas_call(order_kernel, out_shape=(jax.ShapeDtypeStruct((held, HD, C...  161 us
    all_to_all x1, blocking collectives, exchange(): lax.all_to_all(values, 'req', split_axis=0, concat_axis=0, tiled=True)  44.9 us
    pallas_call x1, Pallas kernels, verify_layer(): pl.pallas_call(body, out_shape=(jax.ShapeDtypeStruct((N_TP, blocks, PACKE...  24.4 us
    all_to_all x1, waiting for transfers between devices, exchange(): lax.all_to_all(values, 'req', split_axis=0, concat_axis=0, tiled=True)  23.2 us
    all_to_all x1, starting transfers between devices, exchange(): lax.all_to_all(values, 'req', split_axis=0, concat_axis=0, tiled=True)  8.78 us
    pallas_call x1, Pallas kernels, assemble_cache(): pl.pallas_call(assemble_kernel, out_shape=jax.ShapeDtypeStruct((held, 2 *...  8.5 us
  transfers between devices with their start and end apart: 3, of which 1 were waited for; matrix products, arithmetic and copies ran while one was open for 3% of the time, Pallas kernels for 57%

profile of v1, /device:TPU:1, one launch (start us, length us, event | category | flops | bytes accessed | tf_op | source)
XLA Modules:
  0.0 304.2 jit_solution(1607093339687047697)
XLA Ops:
  7.2 0.0 copy-start
  7.2 0.0 all-gather.3.cloned.1.call-start
  7.2 3.4 %pack_rows.1 = bf16[4,480,128]{2,1,0:T(8,128)(2,1)} custom-call(s32[1]{0:T(128)} %bitcast.parity, bf16[768,320]{1,0:T(8,128)(2,1)} %bitcast.12), custom_call_target="tpu_custom_call" | custom-call | tf_op jit(solution)/shard_map/pack_rows/pallas_call | solution.py:67
  10.7 0.0 all-gather.3.cloned.1.call-update
  10.7 0.7 and_select_fusion.2.refs_2_
  11.3 0.0 copy-start.6
  11.3 0.6 select_reduce_fusion.order
  12.0 161.2 %order_cache.1 = (bf16[32,80,512]{2,1,0:T(8,128)(2,1)}, bf16[32,96,512]{2,1,0:T(8,128)(2,1)}) custom-call(s32[32]{0:T(128)} %select_reduce_fusion.order, bf16[32,160,512]{2,1,0:T(8,128)(2,1)} %refs_7_.1), custom_call_target="tpu_custom_call" | custom-call | tf_op jit(solution)/shard_map/order_cache/pallas_call | solution.py:185
  173.2 0.0 copy-done.6
  173.2 0.0 copy-start.5
  173.2 0.0 copy-start.3
  173.2 0.0 copy-start.4
  173.2 0.0 copy-start.1
  173.2 0.0 copy-start.2
  173.2 8.8 %all-to-all-start = ((bf16[32,80,512]{2,1,0:T(8,128)(2,1)}), bf16[32,80,512]{2,1,0:T(8,128)(2,1)}, u32[]{:S(2)}, u32[]{:S(2)}) async-start(bf16[32,80,512]{2,1,0:T(8,128)(2,1)} %get-tuple-element.14), calls=%async_computation | async-start | bytes 5242880 | tf_op jit(solution)/shard_map/all_to_all | solution.py:461
  182.0 0.0 reduce-scatter.2.cloned.1.call-start
  182.1 0.0 copy-done.5
  182.1 0.0 copy-done.3
  182.1 0.7 copy.28.parents_ref
  182.8 0.0 copy-done.4
  182.8 0.1 copy.25
  182.9 0.6 reshape.149.refs_1_
  183.6 0.1 compare_select_fusion.1
  183.6 0.6 stack.2.step_ref
  184.2 0.8 multiply_sine_fusion
  185.0 2.6 prepare_tables.1
  187.6 0.0 copy-done.1
  187.6 0.0 copy-done.2
  187.7 1.9 fusion.2.refs_5_
  189.6 0.0 copy-done
  189.6 3.2 %fusion.refs_4_ = bf16[2560,512]{1,0:T(8,128)(2,1)} fusion(bf16[2560,320]{0,1:T(8,128)(2,1)S(1)} %copy-done, f32[2560]{0:T(1024)S(1)} %copy-done.2, s32[320]{0:T(512)S(1)} %fusion.10), kind=kOutput, calls=%fused_computation.2 | convolution fusion | flops 841646080 | bytes 4271360 | tf_op jit(solution)/shard_map/dot_general | solution.py:482
  192.8 23.2 %all-to-all-done.key_ref = bf16[32,80,512]{2,1,0:T(8,128)(2,1)} async-done(((bf16[32,80,512]{2,1,0:T(8,128)(2,1)}), bf16[32,80,512]{2,1,0:T(8,128)(2,1)}, u32[]{:S(2)}, u32[]{:S(2)}) %all-to-all-start) | async-done | bytes 2621472 | tf_op jit(solution)/shard_map/all_to_all | solution.py:461
  216.0 0.0 all-gather.3.cloned.1.call-done
  216.0 24.4 %verify_layer.1 = (bf16[8,4,480,128]{3,2,1,0:T(8,128)(2,1)}, bf16[32,96,512]{2,1,0:T(8,128)(2,1)}) custom-call(s32[32]{0:T(128)} %refs_0_.1, s32[128]{0:T(128)} %reshape.149.refs_1_, s32[32]{0:T(128)} %copy-done.6, bf16[8,4,480,128]{3,2,1,0:T(8,128)(2,1)} %bitcast.11, bf16[2560,512]{1,0:T(8,128)(2,1)} %fusion.refs_4_, ...), custom_call_target="tpu_custom_call", output_to_operand_aliasing={{1}: (11, {})} | custom-call | tf_op jit(solution)/shard_map/verify_layer/pallas_call | solution.py:364
  240.4 0.0 reduce-scatter.2.cloned.1.call-update
  240.4 44.9 %all_to_all.10.value_ref = bf16[32,96,512]{2,1,0:T(8,128)(2,1)} all-to-all(bf16[32,96,512]{2,1,0:T(8,128)(2,1)} %get-tuple-element.19), channel_id=1, replica_groups=mesh['req'=32,'tp'=8] {'req'}, dimensions={0} | all-to-all | bytes 6291456 | tf_op jit(solution)/shard_map/all_to_all | solution.py:461
  285.3 8.5 %assemble_cache.1 = bf16[32,160,512]{2,1,0:T(8,128)(2,1)} custom-call(bf16[32,80,512]{2,1,0:T(8,128)(2,1)} %all-to-all-done.key_ref, bf16[32,96,512]{2,1,0:T(8,128)(2,1)} %all_to_all.10.value_ref), custom_call_target="tpu_custom_call" | custom-call | tf_op jit(solution)/shard_map/assemble_cache/pallas_call | solution.py:441
  293.8 0.0 reduce-scatter.2.cloned.1.call-done
  293.8 3.5 %finish_rows.1 = bf16[768,320]{1,0:T(8,128)(2,1)} custom-call(s32[1]{0:T(128)} %bitcast.parity, bf16[4,480,128]{2,1,0:T(8,128)(2,1)} %bitcast.15, bf16[768,320]{1,0:T(8,128)(2,1)} %bitcast.13), custom_call_target="tpu_custom_call" | custom-call | tf_op jit(solution)/shard_map/finish_rows/pallas_call | solution.py:104
  (5 shorter events, 0.1 us)
Async XLA Ops:
  7.2 182.4 %copy-start = (bf16[2560,320]{0,1:T(8,128)(2,1)S(1)}, bf16[2560,320]{0,1:T(8,128)(2,1)}, u32[]{:S(2)}) copy-start(bf16[2560,320]{0,1:T(8,128)(2,1)} %param.12) | copy-start | bytes 4915204
  7.2 208.8 %all-gather.3.cloned.1.call-start = ((), (), s32[]{:S(2)}) async-start(), calls=%async_computation.4 | async-start | bytes 4423680 | tf_op jit(solution)/shard_map/all_gather | solution.py:471
  11.3 161.8 %copy-start.6 = (s32[32]{0:T(128)}, s32[32]{0:T(128)S(1)}, u32[]{:S(2)}) copy-start(s32[32]{0:T(128)S(1)} %and_select_fusion.2.refs_2_) | copy-start | bytes 388
  173.2 8.9 %copy-start.5 = (s32[32]{0:T(128)S(1)}, s32[32]{0:T(128)}, u32[]{:S(2)}) copy-start(s32[32]{0:T(128)} %refs_0_.1) | copy-start | bytes 388
  173.2 8.9 %copy-start.3 = (s32[32,24]{0,1:T(8,128)S(1)}, s32[32,24]{0,1:T(8,128)}, u32[]{:S(2)}) copy-start(s32[32,24]{0,1:T(8,128)} %param.17) | copy-start | bytes 9220
  173.2 9.6 %copy-start.4 = (s32[32,4]{0,1:T(4,128)S(1)}, s32[32,4]{0,1:T(4,128)}, u32[]{:S(2)}) copy-start(s32[32,4]{0,1:T(4,128)} %param.18) | copy-start | bytes 1540
  173.2 14.4 %copy-start.1 = (bf16[160,2560]{1,0:T(8,128)(2,1)S(1)}, bf16[160,2560]{1,0:T(8,128)(2,1)}, u32[]{:S(2)}) copy-start(bf16[160,2560]{1,0:T(8,128)(2,1)} %param.13) | copy-start | bytes 2457604
  173.2 14.4 %copy-start.2 = (f32[2560]{0:T(1024)S(1)}, f32[2560]{0:T(1024)}, u32[]{:S(2)}) copy-start(f32[2560]{0:T(1024)} %param.11) | copy-start | bytes 30724
  173.2 42.7 %all-to-all-start = ((bf16[32,80,512]{2,1,0:T(8,128)(2,1)}), bf16[32,80,512]{2,1,0:T(8,128)(2,1)}, u32[]{:S(2)}, u32[]{:S(2)}) async-start(bf16[32,80,512]{2,1,0:T(8,128)(2,1)} %get-tuple-element.14), calls=%async_computation | async-start | bytes 5242880 | tf_op jit(solution)/shard_map/all_to_all | solution.py:461
  182.0 111.8 %reduce-scatter.2.cloned.1.call-start = ((), (), s32[]{:S(2)}) async-start(), calls=%async_computation.3 | async-start | bytes 4423680 | tf_op jit(solution)/shard_map/reduce_scatter | solution.py:502
Sparse Core Ops, SparseCore 0:
  10.8 176.9 all-gather.2
  240.5 52.3 reduce-scatter.1

commit v2 on v1

--- a/solution.py
+++ b/solution.py
@@ -158,26 +158,27 @@
     )(parents, jnp.cos(angles), jnp.sin(angles), steps)
 
 
-def order_kernel(order, cache_ref, key_ref, value_ref, key_sems, value_sems):
-    copies = []
+def order_kernel(order, cache_ref, key_ref, value_ref, buffer, load_sems, key_sems, value_sems):
+    loads, stores = [], []
     for d in range(cache_ref.shape[0]):
-        source = order[d]
-        copies.append(
+        loads.append(
+            pltpu.make_async_copy(cache_ref.at[order[d]], buffer.at[d], load_sems.at[d])
+        )
+        loads[-1].start()
+    for d, load in enumerate(loads):
+        load.wait()
+        stores.append(
+            pltpu.make_async_copy(buffer.at[d, pl.ds(0, HD)], key_ref.at[d], key_sems.at[d])
+        )
+        stores.append(
             pltpu.make_async_copy(
-                cache_ref.at[source, pl.ds(0, HD)], key_ref.at[d], key_sems.at[d]
+                buffer.at[d, pl.ds(HD, HD)], value_ref.at[d, pl.ds(0, HD)], value_sems.at[d]
             )
         )
-        copies.append(
-            pltpu.make_async_copy(
-                cache_ref.at[source, pl.ds(HD, HD)],
-                value_ref.at[d, pl.ds(0, HD)],
-                value_sems.at[d],
-            )
-        )
-    for copy in copies:
-        copy.start()
-    for copy in copies:
-        copy.wait()
+        stores[-2].start()
+        stores[-1].start()
+    for store in stores:
+        store.wait()
 
 
 def order_cache(kv_cache, send_order):
@@ -194,10 +195,13 @@
             in_specs=[pl.BlockSpec(memory_space=pl.ANY)],
             out_specs=(pl.BlockSpec(memory_space=pl.ANY), pl.BlockSpec(memory_space=pl.ANY)),
             scratch_shapes=[
+                pltpu.VMEM(kv_cache.shape, BF),
+                pltpu.SemaphoreType.DMA((held,)),
                 pltpu.SemaphoreType.DMA((held,)),
                 pltpu.SemaphoreType.DMA((held,)),
             ],
         ),
+        compiler_params=pltpu.CompilerParams(vmem_limit_bytes=VMEM_LIMIT),
         name="order_cache",
     )(send_order, kv_cache)
 

time: 305 us -> 158 us (0.52)
  Pallas kernels: 204 us -> 48.6 us
  waiting for transfers between devices: 23.2 us -> 29.3 us
    pallas_call x1, Pallas kernels: 161 us -> 6.11 us  [order_cache(): pl.pallas_call(order_kernel, out_shape=(jax.ShapeDtypeStruct((held, HD, C...]
    all_gather x1, waiting for transfers between devices: 0.01 us -> 6.09 us  [per_device(): gathered = lax.all_gather(packed, 'tp', axis=0, tiled=False)]
  transfers between devices with their start and end apart: 3 -> 3, of which waited for: 1 -> 2; matrix products, arithmetic and copies ran while one was open for 3% -> 6% of each run, Pallas kernels for 57% -> 11%
where the time goes in v2:
time: 158 us; the launch traced here: 157 us
  Pallas kernels  48.6 us (31%)
  blocking collectives  47 us (30%)
  waiting for transfers between devices  29.3 us (19%)
  between operations  14.2 us (9%)
  starting transfers between devices  8.86 us (6%)
  matrix products  5.15 us (3%)
  other arithmetic  2.19 us (1%)
  local copies, waits for them, and re-layouts  2.06 us (1%)
    all_to_all x1, blocking collectives, exchange(): lax.all_to_all(values, 'req', split_axis=0, concat_axis=0, tiled=True)  47 us
    pallas_call x1, Pallas kernels, verify_layer(): pl.pallas_call(body, out_shape=(jax.ShapeDtypeStruct((N_TP, blocks, PACKE...  24.4 us
    all_to_all x1, waiting for transfers between devices, exchange(): lax.all_to_all(values, 'req', split_axis=0, concat_axis=0, tiled=True)  23.2 us
    all_to_all x1, starting transfers between devices, exchange(): lax.all_to_all(values, 'req', split_axis=0, concat_axis=0, tiled=True)  8.78 us
    pallas_call x1, Pallas kernels, assemble_cache(): pl.pallas_call(assemble_kernel, out_shape=jax.ShapeDtypeStruct((held, 2 *...  8.5 us
    pallas_call x1, Pallas kernels, order_cache(): pl.pallas_call(order_kernel, out_shape=(jax.ShapeDtypeStruct((held, HD, C...  6.11 us
    all_gather x1, waiting for transfers between devices, per_device(): gathered = lax.all_gather(packed, 'tp', axis=0, tiled=False)  6.09 us
    pallas_call x1, Pallas kernels, finish_rows(): pl.pallas_call(finish_kernel, out_shape=jax.ShapeDtypeStruct(rows.shape,...  3.51 us
  transfers between devices with their start and end apart: 3, of which 2 were waited for; matrix products, arithmetic and copies ran while one was open for 6% of the time, Pallas kernels for 11%

profile of v2, /device:TPU:1, one launch (start us, length us, event | category | flops | bytes accessed | tf_op | source)
XLA Modules:
  0.0 157.3 jit_solution(384328290400909638)
XLA Ops:
  7.2 0.0 copy-start
  7.2 0.0 all-gather.3.cloned.1.call-start
  7.2 3.4 %pack_rows.1 = bf16[4,480,128]{2,1,0:T(8,128)(2,1)} custom-call(s32[1]{0:T(128)} %bitcast.parity, bf16[768,320]{1,0:T(8,128)(2,1)} %bitcast.12), custom_call_target="tpu_custom_call" | custom-call | tf_op jit(solution)/shard_map/pack_rows/pallas_call | solution.py:67
  10.7 0.0 all-gather.3.cloned.1.call-update
  10.7 0.7 and_select_fusion.2.refs_2_
  11.3 0.0 copy-start.6
  11.3 0.6 select_reduce_fusion.order
  12.0 6.1 %order_cache.1 = (bf16[32,80,512]{2,1,0:T(8,128)(2,1)}, bf16[32,96,512]{2,1,0:T(8,128)(2,1)}) custom-call(s32[32]{0:T(128)} %select_reduce_fusion.order, bf16[32,160,512]{2,1,0:T(8,128)(2,1)} %refs_7_.1), custom_call_target="tpu_custom_call" | custom-call | tf_op jit(solution)/shard_map/order_cache/pallas_call | solution.py:186
  18.1 0.0 copy-done.6
  18.1 0.0 copy-start.5
  18.1 0.0 copy-start.3
  18.1 0.0 copy-start.4
  18.1 0.0 copy-start.1
  18.2 0.0 copy-start.2
  18.2 8.8 %all-to-all-start = ((bf16[32,80,512]{2,1,0:T(8,128)(2,1)}), bf16[32,80,512]{2,1,0:T(8,128)(2,1)}, u32[]{:S(2)}, u32[]{:S(2)}) async-start(bf16[32,80,512]{2,1,0:T(8,128)(2,1)} %get-tuple-element.14), calls=%async_computation | async-start | bytes 5242880 | tf_op jit(solution)/shard_map/all_to_all | solution.py:465
  27.0 0.0 reduce-scatter.2.cloned.1.call-start
  27.0 0.0 copy-done.5
  27.0 0.0 copy-done.3
  27.0 0.7 copy.28.parents_ref
  27.7 0.0 copy-done.4
  27.7 0.1 copy.25
  27.8 0.6 reshape.149.refs_1_
  28.5 0.1 compare_select_fusion.1
  28.5 0.6 stack.2.step_ref
  29.2 0.8 multiply_sine_fusion
  29.9 2.6 %prepare_tables.1 = (f32[32,24,128]{2,1,0:T(8,128)}, f32[32,24,128]{2,1,0:T(8,128)}, f32[32,24,128]{2,1,0:T(8,128)}) custom-call(s32[32,24]{1,0:T(8,128)} %copy.28.parents_ref, f32[32,128]{1,0:T(8,128)} %get-tuple-element.21.cos_ref, f32[32,128]{1,0:T(8,128)} %get-tuple-element.20.sin_ref, f32[8,128]{1,0:T(8,128)} %stack.2.step_ref), custom_call_target="tpu_custom_call" | custom-call | tf_op jit(solution)/shard_map/prepare_tables/pallas_call | solution.py:156
  32.6 0.0 copy-done.1
  32.6 0.0 copy-done.2
  32.6 1.9 %fusion.2.refs_5_ = bf16[2560,256]{1,0:T(8,128)(2,1)} fusion(bf16[160,2560]{1,0:T(8,128)(2,1)S(1)} %copy-done.1, f32[2560]{0:T(1024)S(1)} %copy-done.2, s32[160]{0:T(256)S(1)} %fusion.16), kind=kOutput, calls=%fused_computation.4 | convolution fusion | flops 211066880 | bytes 2140800 | tf_op jit(solution)/shard_map/dot_general | solution.py:487
  34.5 0.0 copy-done
  34.5 3.2 %fusion.refs_4_ = bf16[2560,512]{1,0:T(8,128)(2,1)} fusion(bf16[2560,320]{0,1:T(8,128)(2,1)S(1)} %copy-done, f32[2560]{0:T(1024)S(1)} %copy-done.2, s32[320]{0:T(512)S(1)} %fusion.10), kind=kOutput, calls=%fused_computation.2 | convolution fusion | flops 841646080 | bytes 4271360 | tf_op jit(solution)/shard_map/dot_general | solution.py:486
  37.8 23.2 %all-to-all-done.key_ref = bf16[32,80,512]{2,1,0:T(8,128)(2,1)} async-done(((bf16[32,80,512]{2,1,0:T(8,128)(2,1)}), bf16[32,80,512]{2,1,0:T(8,128)(2,1)}, u32[]{:S(2)}, u32[]{:S(2)}) %all-to-all-start) | async-done | bytes 2621472 | tf_op jit(solution)/shard_map/all_to_all | solution.py:465
  60.9 6.1 %all-gather.3.cloned.1.call-done = bf16[32,480,128]{2,1,0:T(8,128)(2,1)} async-done(((bf16[4,480,128]{2,1,0:T(8,128)(2,1)}), bf16[32,480,128]{2,1,0:T(8,128)(2,1)}) %all-gather.3.cloned.1.call-update) | async-done | bytes 3932176 | tf_op jit(solution)/shard_map/all_gather | solution.py:475
  67.0 24.4 %verify_layer.1 = (bf16[8,4,480,128]{3,2,1,0:T(8,128)(2,1)}, bf16[32,96,512]{2,1,0:T(8,128)(2,1)}) custom-call(s32[32]{0:T(128)} %refs_0_.1, s32[128]{0:T(128)} %reshape.149.refs_1_, s32[32]{0:T(128)} %copy-done.6, bf16[8,4,480,128]{3,2,1,0:T(8,128)(2,1)} %bitcast.11, bf16[2560,512]{1,0:T(8,128)(2,1)} %fusion.refs_4_, ...), custom_call_target="tpu_custom_call", output_to_operand_aliasing={{1}: (11, {})} | custom-call | tf_op jit(solution)/shard_map/verify_layer/pallas_call | solution.py:368
  91.4 0.0 reduce-scatter.2.cloned.1.call-update
  91.4 47.0 %all_to_all.10.value_ref = bf16[32,96,512]{2,1,0:T(8,128)(2,1)} all-to-all(bf16[32,96,512]{2,1,0:T(8,128)(2,1)} %get-tuple-element.19), channel_id=1, replica_groups=mesh['req'=32,'tp'=8] {'req'}, dimensions={0} | all-to-all | bytes 6291456 | tf_op jit(solution)/shard_map/all_to_all | solution.py:465
  138.4 8.5 %assemble_cache.1 = bf16[32,160,512]{2,1,0:T(8,128)(2,1)} custom-call(bf16[32,80,512]{2,1,0:T(8,128)(2,1)} %all-to-all-done.key_ref, bf16[32,96,512]{2,1,0:T(8,128)(2,1)} %all_to_all.10.value_ref), custom_call_target="tpu_custom_call" | custom-call | tf_op jit(solution)/shard_map/assemble_cache/pallas_call | solution.py:445
  146.9 0.0 reduce-scatter.2.cloned.1.call-done
  146.9 3.5 %finish_rows.1 = bf16[768,320]{1,0:T(8,128)(2,1)} custom-call(s32[1]{0:T(128)} %bitcast.parity, bf16[4,480,128]{2,1,0:T(8,128)(2,1)} %bitcast.15, bf16[768,320]{1,0:T(8,128)(2,1)} %bitcast.13), custom_call_target="tpu_custom_call" | custom-call | tf_op jit(solution)/shard_map/finish_rows/pallas_call | solution.py:104
  (5 shorter events, 0.1 us)
Async XLA Ops:
  7.2 27.4 %copy-start = (bf16[2560,320]{0,1:T(8,128)(2,1)S(1)}, bf16[2560,320]{0,1:T(8,128)(2,1)}, u32[]{:S(2)}) copy-start(bf16[2560,320]{0,1:T(8,128)(2,1)} %param.12) | copy-start | bytes 4915204
  7.2 59.8 %all-gather.3.cloned.1.call-start = ((), (), s32[]{:S(2)}) async-start(), calls=%async_computation.4 | async-start | bytes 4423680 | tf_op jit(solution)/shard_map/all_gather | solution.py:475
  11.3 6.8 %copy-start.6 = (s32[32]{0:T(128)}, s32[32]{0:T(128)S(1)}, u32[]{:S(2)}) copy-start(s32[32]{0:T(128)S(1)} %and_select_fusion.2.refs_2_) | copy-start | bytes 388
  18.1 8.9 %copy-start.5 = (s32[32]{0:T(128)S(1)}, s32[32]{0:T(128)}, u32[]{:S(2)}) copy-start(s32[32]{0:T(128)} %refs_0_.1) | copy-start | bytes 388
  18.1 8.9 %copy-start.3 = (s32[32,24]{0,1:T(8,128)S(1)}, s32[32,24]{0,1:T(8,128)}, u32[]{:S(2)}) copy-start(s32[32,24]{0,1:T(8,128)} %param.17) | copy-start | bytes 9220
  18.1 9.6 %copy-start.4 = (s32[32,4]{0,1:T(4,128)S(1)}, s32[32,4]{0,1:T(4,128)}, u32[]{:S(2)}) copy-start(s32[32,4]{0,1:T(4,128)} %param.18) | copy-start | bytes 1540
  18.1 14.4 %copy-start.1 = (bf16[160,2560]{1,0:T(8,128)(2,1)S(1)}, bf16[160,2560]{1,0:T(8,128)(2,1)}, u32[]{:S(2)}) copy-start(bf16[160,2560]{1,0:T(8,128)(2,1)} %param.13) | copy-start | bytes 2457604
  18.2 14.4 %copy-start.2 = (f32[2560]{0:T(1024)S(1)}, f32[2560]{0:T(1024)}, u32[]{:S(2)}) copy-start(f32[2560]{0:T(1024)} %param.11) | copy-start | bytes 30724
  18.2 42.7 %all-to-all-start = ((bf16[32,80,512]{2,1,0:T(8,128)(2,1)}), bf16[32,80,512]{2,1,0:T(8,128)(2,1)}, u32[]{:S(2)}, u32[]{:S(2)}) async-start(bf16[32,80,512]{2,1,0:T(8,128)(2,1)} %get-tuple-element.14), calls=%async_computation | async-start | bytes 5242880 | tf_op jit(solution)/shard_map/all_to_all | solution.py:465
  27.0 120.0 %reduce-scatter.2.cloned.1.call-start = ((), (), s32[]{:S(2)}) async-start(), calls=%async_computation.3 | async-start | bytes 4423680 | tf_op jit(solution)/shard_map/reduce_scatter | solution.py:506
Sparse Core Ops, SparseCore 0:
  10.8 56.1 all-gather.2
  91.5 51.4 reduce-scatter.1

commit v3 on v2

--- a/solution.py
+++ b/solution.py
@@ -24,6 +24,9 @@
 WIDTH = D // N_TP
 NEG = -1e30
 EXTRA = 16
+EARLY = 112
+LATE = 2 * HD - EARLY
+CHUNKS = 2
 BF = jnp.bfloat16
 F32 = jnp.float32
 VMEM_LIMIT = 56 * 1024 * 1024
@@ -62,15 +65,14 @@
         o_ref[0, 2 * ROWS : PACKED] = jnp.where(low_half, t0[:HALF], s0[HALF:]).astype(BF)
 
 
-def pack_rows(rows, parity):
-    blocks = rows.shape[0] // ROWS
+def pack_rows(rows, parity, blocks, first_block):
     return pl.pallas_call(
         pack_kernel,
         out_shape=jax.ShapeDtypeStruct((blocks, PACKED, LANES), BF),
         grid_spec=pltpu.PrefetchScalarGridSpec(
             num_scalar_prefetch=1,
             grid=(blocks,),
-            in_specs=[pl.BlockSpec((ROWS, WIDTH), lambda b, p: (b, 0))],
+            in_specs=[pl.BlockSpec((ROWS, WIDTH), lambda b, p: (first_block + b, 0))],
             out_specs=pl.BlockSpec((1, PACKED, LANES), lambda b, p: (b, 0, 0)),
         ),
         name="pack_rows",
@@ -99,22 +101,35 @@
         o_ref[...] = (x_ref[...].astype(F32) + total).astype(BF)
 
 
-def finish_rows(summed, rows, parity):
-    blocks = rows.shape[0] // ROWS
+def finish_rows(summed, rows, parity, first_block, done):
+    blocks = summed.shape[0]
+    kernel = finish_kernel
+    operands = (parity, summed, rows)
+    in_specs = [
+        pl.BlockSpec((1, PACKED, LANES), lambda b, p: (b, 0, 0)),
+        pl.BlockSpec((ROWS, WIDTH), lambda b, p: (first_block + b, 0)),
+    ]
+    aliases = {}
+    if done is not None:
+
+        def kernel(parity, s_ref, x_ref, done_ref, o_ref):
+            finish_kernel(parity, s_ref, x_ref, o_ref)
+
+        operands += (done,)
+        in_specs.append(pl.BlockSpec(memory_space=pl.ANY))
+        aliases = {3: 0}
     return pl.pallas_call(
-        finish_kernel,
+        kernel,
         out_shape=jax.ShapeDtypeStruct(rows.shape, BF),
         grid_spec=pltpu.PrefetchScalarGridSpec(
             num_scalar_prefetch=1,
             grid=(blocks,),
-            in_specs=[
-                pl.BlockSpec((1, PACKED, LANES), lambda b, p: (b, 0, 0)),
-                pl.BlockSpec((ROWS, WIDTH), lambda b, p: (b, 0)),
-            ],
-            out_specs=pl.BlockSpec((ROWS, WIDTH), lambda b, p: (b, 0)),
+            in_specs=in_specs,
+            out_specs=pl.BlockSpec((ROWS, WIDTH), lambda b, p: (first_block + b, 0)),
         ),
+        input_output_aliases=aliases,
         name="finish_rows",
-    )(parity, summed, rows)
+    )(*operands)
 
 
 def prep_kernel(parents_ref, cos_ref, sin_ref, step_ref, bias_out, cos_out, sin_out):
@@ -158,7 +173,7 @@
     )(parents, jnp.cos(angles), jnp.sin(angles), steps)
 
 
-def order_kernel(order, cache_ref, key_ref, value_ref, buffer, load_sems, key_sems, value_sems):
+def order_kernel(order, cache_ref, early_ref, late_ref, buffer, load_sems, early_sems, late_sems):
     loads, stores = [], []
     for d in range(cache_ref.shape[0]):
         loads.append(
@@ -168,11 +183,11 @@
     for d, load in enumerate(loads):
         load.wait()
         stores.append(
-            pltpu.make_async_copy(buffer.at[d, pl.ds(0, HD)], key_ref.at[d], key_sems.at[d])
+            pltpu.make_async_copy(buffer.at[d, pl.ds(0, EARLY)], early_ref.at[d], early_sems.at[d])
         )
         stores.append(
             pltpu.make_async_copy(
-                buffer.at[d, pl.ds(HD, HD)], value_ref.at[d, pl.ds(0, HD)], value_sems.at[d]
+                buffer.at[d, pl.ds(EARLY, LATE)], late_ref.at[d, pl.ds(0, LATE)], late_sems.at[d]
             )
         )
         stores[-2].start()
@@ -186,8 +201,8 @@
     return pl.pallas_call(
         order_kernel,
         out_shape=(
-            jax.ShapeDtypeStruct((held, HD, CACHE), BF),
-            jax.ShapeDtypeStruct((held, HD + EXTRA, CACHE), BF),
+            jax.ShapeDtypeStruct((held, EARLY, CACHE), BF),
+            jax.ShapeDtypeStruct((held, LATE + EXTRA, CACHE), BF),
         ),
         grid_spec=pltpu.PrefetchScalarGridSpec(
             num_scalar_prefetch=1,
@@ -283,6 +298,7 @@
     factor = math.log2(math.e) / math.sqrt(HD)
     column = lane_index((GROUP * TREE, CACHE))
     extra_row = lax.broadcasted_iota(jnp.int32, (EXTRA, LANES), 0)
+    extra_lane = lane_index((EXTRA, LANES))
     pick_row = lax.broadcasted_iota(jnp.int32, (EXTRA, TREE), 0)
     pick_column = lane_index((EXTRA, TREE))
     copies = []
@@ -324,12 +340,17 @@
         new_values = jnp.dot(pick, v, preferred_element_type=F32)
         coarse = (length // 16).astype(F32)
         fine = (length % 16).astype(F32)
-        new_keys = jnp.where(extra_row == 8, coarse, jnp.where(extra_row == 9, fine, new_keys))
-        extra[i, :, 0:LANES] = new_keys.astype(BF)
-        extra[i, :, LANES : 2 * LANES] = new_values.astype(BF)
+        shifted = pltpu.roll(new_values, HD, 1)
+        new_keys = jnp.where(extra_lane < HD, new_keys, shifted)
+        extra[i, :, 0:LANES] = jnp.where(
+            extra_row == 8, coarse, jnp.where(extra_row == 9, fine, new_keys)
+        ).astype(BF)
+        extra[i, :, LANES : 2 * LANES] = jnp.where(
+            extra_lane < 2 * HD - LANES, shifted, 0.0
+        ).astype(BF)
         copies.append(
             pltpu.make_async_copy(
-                extra.at[i], send_out.at[destination[r], pl.ds(HD, EXTRA)], sems.at[i]
+                extra.at[i], send_out.at[destination[r], pl.ds(LATE, EXTRA)], sems.at[i]
             )
         )
         copies[-1].start()
@@ -414,45 +435,40 @@
     )
 
 
-def assemble_kernel(key_ref, value_ref, o_ref):
-    column = lane_index((HD, CACHE))
+def assemble_kernel(early_ref, late_ref, o_ref):
     place_row = lax.broadcasted_iota(jnp.int32, (EXTRA, CACHE), 0)
     place_column = lane_index((EXTRA, CACHE))
-    for i in range(key_ref.shape[0]):
-        extra = value_ref[i, HD : HD + EXTRA]
+    for i in range(early_ref.shape[0]):
+        extra = late_ref[i, LATE : LATE + EXTRA, : 2 * LANES]
         wide = extra[:, :LANES].astype(F32)
         length = (wide[8:9] * 16.0 + wide[9:10]).astype(jnp.int32)
         length = jnp.concatenate([length] * (CACHE // LANES), axis=1)
+        offset = place_column - length
         place = jnp.where(
-            jnp.logical_and(place_column == length + place_row, place_row < DEPTH), 1.0, 0.0
-        ).astype(BF)
-        live = column < length
-        for part, ref in ((0, key_ref), (1, value_ref)):
-            new = lax.dot_general(
-                extra[:, part * LANES : part * LANES + LANES],
-                place,
-                (((0,), (0,)), ((), ())),
-                preferred_element_type=F32,
-            )[:HD]
-            o_ref[i, part * HD : (part + 1) * HD] = jnp.where(
-                live, ref[i, 0:HD].astype(F32), new
-            ).astype(BF)
-
-
-def assemble_cache(keys, values):
-    held = keys.shape[0]
+            jnp.logical_and(offset == place_row, place_row < DEPTH), 1.0, 0.0
+        ).astype(BF)
+        live = jnp.where(offset[0:1] < 0, 1.0, 0.0).astype(BF)
+        new = lax.dot_general(
+            extra, place, (((0,), (0,)), ((), ())), preferred_element_type=F32
+        ).astype(BF)
+        o_ref[i, 0:EARLY] = early_ref[i] * live + new[0:EARLY]
+        o_ref[i, EARLY : 2 * HD] = late_ref[i, 0:LATE] * live + new[EARLY : 2 * HD]
+
+
+def assemble_cache(early, late):
+    held = early.shape[0]
     step = 4
     return pl.pallas_call(
         assemble_kernel,
         out_shape=jax.ShapeDtypeStruct((held, 2 * HD, CACHE), BF),
         grid=(held // step,),
         in_specs=[
-            pl.BlockSpec((step, HD, CACHE), lambda s: (s, 0, 0)),
-            pl.BlockSpec((step, HD + EXTRA, CACHE), lambda s: (s, 0, 0)),
+            pl.BlockSpec((step, EARLY, CACHE), lambda s: (s, 0, 0)),
+            pl.BlockSpec((step, LATE + EXTRA, CACHE), lambda s: (s, 0, 0)),
         ],
         out_specs=pl.BlockSpec((step, 2 * HD, CACHE), lambda s: (s, 0, 0)),
         name="assemble_cache",
-    )(keys, values)
+    )(early, late)
 
 
 def spread_heads(heads):
@@ -471,15 +487,18 @@
     held = hidden.shape[0]
     rows = hidden.reshape(held * TREE, WIDTH)
     parity = lax.axis_index("tp").astype(jnp.int32).reshape(1)
-    packed = pack_rows(rows, parity)
-    gathered = lax.all_gather(packed, "tp", axis=0, tiled=False)
+    blocks = held // REQ_BLOCK // CHUNKS
+    gathered = []
+    for c in range(CHUNKS):
+        packed = pack_rows(rows, parity, blocks, c * blocks)
+        gathered.append(lax.all_gather(packed, "tp", axis=0, tiled=False))
 
     destination = slot_of // held
     peer_index = jnp.arange(held, dtype=jnp.int32)
     matches = (destination[None, :] == peer_index[:, None]).astype(jnp.int32)
     send_order = jnp.sum(matches * peer_index[None, :], axis=1)
-    key_send, value_send = order_cache(kv_cache, send_order)
-    key_received = exchange(key_send)
+    early, late = order_cache(kv_cache, send_order)
+    early = exchange(early)
 
     tables = prepare_tables(parents, lengths)
     gain = norm_gain[:, None]
@@ -489,24 +508,31 @@
     )
     wkv = (wkv * gain).astype(BF)
 
-    key_received, value_send = lax.optimization_barrier((key_received, value_send))
-    partial, value_send = verify_layer(
-        gathered,
-        wq,
-        wkv,
-        w_out,
-        kv_cache,
-        tables,
-        lengths,
-        accepted.reshape(-1),
-        destination,
-        value_send,
-        0,
-    )
-    summed = lax.psum_scatter(partial, "tp", scatter_dimension=0, tiled=True)
-    value_received = exchange(value_send)
-    new_cache = assemble_cache(key_received, value_received)
-    out_rows = finish_rows(summed.reshape(-1, PACKED, LANES), rows, parity)
+    summed = []
+    for c in range(CHUNKS):
+        if c == CHUNKS - 1:
+            early, late = lax.optimization_barrier((early, late))
+        partial, late = verify_layer(
+            gathered[c],
+            wq,
+            wkv,
+            w_out,
+            kv_cache,
+            tables,
+            lengths,
+            accepted.reshape(-1),
+            destination,
+            late,
+            c * blocks,
+        )
+        summed.append(lax.psum_scatter(partial, "tp", scatter_dimension=0, tiled=True))
+    late = exchange(late)
+    new_cache = assemble_cache(early, late)
+    out_rows = None
+    for c in range(CHUNKS):
+        out_rows = finish_rows(
+            summed[c].reshape(-1, PACKED, LANES), rows, parity, c * blocks, out_rows
+        )
     return (out_rows.reshape(hidden.shape), new_cache)
 
 

time: 158 us -> 190 us (1.20)
  blocking collectives: 47 us -> 89 us
  starting transfers between devices: 8.86 us -> 0.16 us
  waiting for transfers between devices: 29.3 us -> 22.5 us
  Pallas kernels: 48.6 us -> 54.4 us
    all_to_all x1 -> x2, blocking collectives: 47 us -> 89 us  [exchange(): lax.all_to_all(values, 'req', split_axis=0, concat_axis=0, tiled=True)]
    all_to_all x1 -> x0, waiting for transfers between devices: 23.2 us -> none  [exchange(): lax.all_to_all(values, 'req', split_axis=0, concat_axis=0, tiled=True)]
    all_gather x1 -> x2, waiting for transfers between devices: 6.09 us -> 22.4 us  [per_device(): gathered.append(lax.all_gather(packed, 'tp', axis=0, tiled=False))]
    all_to_all x1 -> x0, starting transfers between devices: 8.78 us -> none  [exchange(): lax.all_to_all(values, 'req', split_axis=0, concat_axis=0, tiled=True)]
    pallas_call x1 -> x2, Pallas kernels: 24.4 us -> 29.8 us  [verify_layer(): pl.pallas_call(body, out_shape=(jax.ShapeDtypeStruct((N_TP, blocks, PACKE...]
    pallas_call x2 -> x3, Pallas kernels: 9.62 us -> 10 us  [the longest x1 6.23 us: order_cache(): pl.pallas_call(order_kernel, out_shape=(jax.ShapeDtypeStruct((held, EARLY...]
  transfers between devices with their start and end apart: 3 -> 4, of which waited for: 2 -> 1; matrix products, arithmetic and copies ran while one was open for 6% -> 5% of each run, Pallas kernels for 11% -> 27%
where the time goes in v3:
time: 190 us; the launch traced here: 189 us
  blocking collectives  89 us (47%)
  Pallas kernels  54.4 us (29%)
  waiting for transfers between devices  22.5 us (12%)
  between operations  13.9 us (7%)
  matrix products  5.1 us (3%)
  local copies, waits for them, and re-layouts  2.05 us (1%)
    all_to_all x2, blocking collectives, exchange(): lax.all_to_all(values, 'req', split_axis=0, concat_axis=0, tiled=True)  89 us
    pallas_call x2, Pallas kernels, verify_layer(): pl.pallas_call(body, out_shape=(jax.ShapeDtypeStruct((N_TP, blocks, PACKE...  29.8 us
    all_gather x2, waiting for transfers between devices, per_device(): gathered.append(lax.all_gather(packed, 'tp', axis=0, tiled=False))  22.4 us
    pallas_call x1, Pallas kernels, assemble_cache(): pl.pallas_call(assemble_kernel, out_shape=jax.ShapeDtypeStruct((held, 2 *...  8.43 us
    pallas_call x1, Pallas kernels, order_cache(): pl.pallas_call(order_kernel, out_shape=(jax.ShapeDtypeStruct((held, EARLY...  6.23 us
  transfers between devices with their start and end apart: 4, of which 1 were waited for; matrix products, arithmetic and copies ran while one was open for 5% of the time, Pallas kernels for 27%

profile of v3, /device:TPU:1, one launch (start us, length us, event | category | flops | bytes accessed | tf_op | source)
XLA Modules:
  0.0 188.6 jit_solution(16640244782985526357)
XLA Ops:
  7.2 0.0 copy-start
  7.2 0.0 copy-start.4
  7.2 0.0 copy-start.3
  7.2 0.0 copy-start.6
  7.2 0.0 copy-start.7
  7.2 0.0 all-gather.7.cloned.1.call-start
  7.3 1.8 pack_rows.3
  9.1 0.0 all-gather.7.cloned.1.call-update
  9.1 0.0 all-gather.5.cloned.1.call-start
  9.2 1.7 pack_rows.2
  10.9 0.0 all-gather.5.cloned.1.call-update
  11.0 0.0 reduce-scatter.5.cloned.1.call-start
  11.0 0.0 copy-done.4
  11.0 0.0 copy-done.3
  11.0 0.7 copy.30.parents_ref
  11.7 0.0 copy-done.6
  11.7 0.1 copy.27
  11.8 0.6 reshape.153.refs_1_
  12.4 0.0 copy-done.7
  12.5 0.0 copy-start.5
  12.5 0.6 select_reduce_fusion.order
  13.1 0.0 copy-start.1
  13.1 0.0 copy-start.2
  13.1 6.2 %order_cache.1 = (bf16[32,112,512]{2,1,0:T(8,128)(2,1)}, bf16[32,64,512]{2,1,0:T(8,128)(2,1)}) custom-call(s32[32]{0:T(128)} %select_reduce_fusion.order, bf16[32,160,512]{2,1,0:T(8,128)(2,1)} %refs_7_.3), custom_call_target="tpu_custom_call" | custom-call | tf_op jit(solution)/shard_map/order_cache/pallas_call | solution.py:201
  19.3 0.0 copy-done.5
  19.4 0.1 compare_select_fusion.1
  19.4 0.6 stack.2.step_ref
  20.1 0.8 multiply_sine_fusion
  20.8 2.6 %prepare_tables.1 = (f32[32,24,128]{2,1,0:T(8,128)}, f32[32,24,128]{2,1,0:T(8,128)}, f32[32,24,128]{2,1,0:T(8,128)}) custom-call(s32[32,24]{1,0:T(8,128)} %copy.30.parents_ref, f32[32,128]{1,0:T(8,128)} %get-tuple-element.25.cos_ref, f32[32,128]{1,0:T(8,128)} %get-tuple-element.24.sin_ref, f32[8,128]{1,0:T(8,128)} %stack.2.step_ref), custom_call_target="tpu_custom_call" | custom-call | tf_op jit(solution)/shard_map/prepare_tables/pallas_call | solution.py:171
  23.4 0.0 copy-done.1
  23.5 0.0 copy-done.2
  23.5 1.9 %fusion.2.refs_5_ = bf16[2560,256]{1,0:T(8,128)(2,1)} fusion(bf16[160,2560]{1,0:T(8,128)(2,1)S(1)} %copy-done.1, f32[2560]{0:T(1024)S(1)} %copy-done.2, s32[160]{0:T(256)S(1)} %fusion.16), kind=kOutput, calls=%fused_computation.4 | convolution fusion | flops 211066880 | bytes 2140800 | tf_op jit(solution)/shard_map/dot_general | solution.py:506
  25.4 0.0 copy-done
  25.4 3.2 %fusion.refs_4_ = bf16[2560,512]{1,0:T(8,128)(2,1)} fusion(bf16[2560,320]{0,1:T(8,128)(2,1)S(1)} %copy-done, f32[2560]{0:T(1024)S(1)} %copy-done.2, s32[320]{0:T(512)S(1)} %fusion.10), kind=kOutput, calls=%fused_computation.2 | convolution fusion | flops 841646080 | bytes 4271360 | tf_op jit(solution)/shard_map/dot_general | solution.py:505
  28.6 22.4 %all-gather.7.cloned.1.call-done = bf16[16,480,128]{2,1,0:T(8,128)(2,1)} async-done(((bf16[2,480,128]{2,1,0:T(8,128)(2,1)}), bf16[16,480,128]{2,1,0:T(8,128)(2,1)}) %all-gather.7.cloned.1.call-update) | async-done | bytes 1966096 | tf_op jit(solution)/shard_map/all_gather | solution.py:494
  51.0 14.9 %verify_layer.2 = (bf16[8,2,480,128]{3,2,1,0:T(8,128)(2,1)}, bf16[32,64,512]{2,1,0:T(8,128)(2,1)}) custom-call(s32[32]{0:T(128)} %refs_0_.3, s32[128]{0:T(128)} %reshape.153.refs_1_, s32[32]{0:T(128)} %copy-done.5, bf16[8,2,480,128]{3,2,1,0:T(8,128)(2,1)} %bitcast.19, bf16[2560,512]{1,0:T(8,128)(2,1)} %fusion.refs_4_, ...), custom_call_target="tpu_custom_call", output_to_operand_aliasing={{1}: (11, {})} | custom-call | tf_op jit(solution)/shard_map/verify_layer/pallas_call | solution.py:389
  65.9 0.0 reduce-scatter.5.cloned.1.call-update
  65.9 0.0 reduce-scatter.3.cloned.1.call-start
  65.9 56.6 %all_to_all.10.early_ref = bf16[32,112,512]{2,1,0:T(8,128)(2,1)} all-to-all(bf16[32,112,512]{2,1,0:T(8,128)(2,1)} %get-tuple-element.16), channel_id=1, replica_groups=mesh['req'=32,'tp'=8] {'req'}, dimensions={0} | all-to-all | bytes 7340032 | tf_op jit(solution)/shard_map/all_to_all | solution.py:481
  122.5 0.0 all-gather.5.cloned.1.call-done
  122.5 14.9 %verify_layer.3 = (bf16[8,2,480,128]{3,2,1,0:T(8,128)(2,1)}, bf16[32,64,512]{2,1,0:T(8,128)(2,1)}) custom-call(s32[32]{0:T(128)} %refs_0_.3, s32[128]{0:T(128)} %reshape.153.refs_1_, s32[32]{0:T(128)} %copy-done.5, bf16[8,2,480,128]{3,2,1,0:T(8,128)(2,1)} %bitcast.18, bf16[2560,512]{1,0:T(8,128)(2,1)} %fusion.refs_4_, ...), custom_call_target="tpu_custom_call", output_to_operand_aliasing={{1}: (11, {})} | custom-call | tf_op jit(solution)/shard_map/verify_layer/pallas_call | solution.py:389
  137.5 0.0 reduce-scatter.3.cloned.1.call-update
  137.5 32.4 %all_to_all.11.late_ref = bf16[32,64,512]{2,1,0:T(8,128)(2,1)} all-to-all(bf16[32,64,512]{2,1,0:T(8,128)(2,1)} %get-tuple-element.23), channel_id=1, replica_groups=mesh['req'=32,'tp'=8] {'req'}, dimensions={0} | all-to-all | bytes 4194304 | tf_op jit(solution)/shard_map/all_to_all | solution.py:481
  169.9 8.4 %assemble_cache.1 = bf16[32,160,512]{2,1,0:T(8,128)(2,1)} custom-call(bf16[32,112,512]{2,1,0:T(8,128)(2,1)} %all_to_all.10.early_ref, bf16[32,64,512]{2,1,0:T(8,128)(2,1)} %all_to_all.11.late_ref), custom_call_target="tpu_custom_call" | custom-call | tf_op jit(solution)/shard_map/assemble_cache/pallas_call | solution.py:461
  178.3 0.0 reduce-scatter.5.cloned.1.call-done
  178.3 1.9 finish_rows.2.done_ref
  180.2 0.0 reduce-scatter.3.cloned.1.call-done
  180.2 1.9 %finish_rows.3 = bf16[768,320]{1,0:T(8,128)(2,1)} custom-call(s32[1]{0:T(128)} %bitcast.parity, bf16[2,480,128]{2,1,0:T(8,128)(2,1)} %bitcast.21, bf16[768,320]{1,0:T(8,128)(2,1)} %bitcast.16, bf16[768,320]{1,0:T(8,128)(2,1)} %finish_rows.2.done_ref), custom_call_target="tpu_custom_call", output_to_operand_aliasing={{}: (3, {})} | custom-call | tf_op jit(solution)/shard_map/finish_rows/pallas_call | solution.py:121
  (6 shorter events, 0.1 us)
Async XLA Ops:
  7.2 18.2 %copy-start = (bf16[2560,320]{0,1:T(8,128)(2,1)S(1)}, bf16[2560,320]{0,1:T(8,128)(2,1)}, u32[]{:S(2)}) copy-start(bf16[2560,320]{0,1:T(8,128)(2,1)} %param.12) | copy-start | bytes 4915204
  7.2 3.8 %copy-start.4 = (s32[32]{0:T(128)S(1)}, s32[32]{0:T(128)}, u32[]{:S(2)}) copy-start(s32[32]{0:T(128)} %refs_0_.3) | copy-start | bytes 388
  7.2 3.8 %copy-start.3 = (s32[32,24]{0,1:T(8,128)S(1)}, s32[32,24]{0,1:T(8,128)}, u32[]{:S(2)}) copy-start(s32[32,24]{0,1:T(8,128)} %param.17) | copy-start | bytes 9220
  7.2 4.5 %copy-start.6 = (s32[32,4]{0,1:T(4,128)S(1)}, s32[32,4]{0,1:T(4,128)}, u32[]{:S(2)}) copy-start(s32[32,4]{0,1:T(4,128)} %param.18) | copy-start | bytes 1540
  7.2 5.2 %copy-start.7 = (s32[32]{0:T(128)S(1)}, s32[32]{0:T(128)}, u32[]{:S(2)}) copy-start(s32[32]{0:T(128)} %param.19) | copy-start | bytes 388
  7.2 43.8 %all-gather.7.cloned.1.call-start = ((), (), s32[]{:S(2)}) async-start(), calls=%async_computation.7 | async-start | bytes 2211840 | tf_op jit(solution)/shard_map/all_gather | solution.py:494
  9.1 113.4 %all-gather.5.cloned.1.call-start = ((), (), s32[]{:S(2)}) async-start(), calls=%async_computation.6 | async-start | bytes 2211840 | tf_op jit(solution)/shard_map/all_gather | solution.py:494
  11.0 167.3 %reduce-scatter.5.cloned.1.call-start = ((), (), s32[]{:S(2)}) async-start(), calls=%async_computation.5 | async-start | bytes 2211840 | tf_op jit(solution)/shard_map/reduce_scatter | solution.py:528
  12.5 6.9 %copy-start.5 = (s32[32]{0:T(128)}, s32[32]{0:T(128)S(1)}, u32[]{:S(2)}) copy-start(s32[32]{0:T(128)S(1)} %and_select_fusion.2.refs_2_) | copy-start | bytes 388
  13.1 10.4 %copy-start.1 = (bf16[160,2560]{1,0:T(8,128)(2,1)S(1)}, bf16[160,2560]{1,0:T(8,128)(2,1)}, u32[]{:S(2)}) copy-start(bf16[160,2560]{1,0:T(8,128)(2,1)} %param.13) | copy-start | bytes 2457604
  13.1 10.4 %copy-start.2 = (f32[2560]{0:T(1024)S(1)}, f32[2560]{0:T(1024)}, u32[]{:S(2)}) copy-start(f32[2560]{0:T(1024)} %param.11) | copy-start | bytes 30724
  65.9 114.3 %reduce-scatter.3.cloned.1.call-start = ((), (), s32[]{:S(2)}) async-start(), calls=%async_computation.4 | async-start | bytes 2211840 | tf_op jit(solution)/shard_map/reduce_scatter | solution.py:528
Sparse Core Ops, SparseCore 0:
  9.8 41.1 all-gather.6
  52.8 39.2 all-gather.4
  94.6 40.0 reduce-scatter.4
  137.6 39.9 reduce-scatter.2

commit v4 on v2

v4 whole, which is shorter than its diff:
```python
import math

import jax
import jax.numpy as jnp
from jax import lax
from jax.experimental import pallas as pl
from jax.experimental.pallas import tpu as pltpu
from jax.sharding import PartitionSpec as P

H = 32
KVH = 8
HD = 80
D = 2560
TREE = 24
CACHE = 512
DEPTH = 4
N_TP = 8
GROUP = H // KVH
LANES = 128
REQ_BLOCK = 8
ROWS = REQ_BLOCK * TREE
HALF = ROWS // 2
PACKED = 2 * ROWS + HALF
WIDTH = D // N_TP
NEG = -1e30
EXTRA = 16
HALF_BLOCKS = 2
BF = jnp.bfloat16
F32 = jnp.float32
VMEM_LIMIT = 56 * 1024 * 1024


def lane_index(shape):
    return lax.broadcasted_iota(jnp.int32, shape, len(shape) - 1)


def swap_halves(tile):
    return pltpu.roll(tile, 64, 1)


def pack_kernel(parity, x_ref, o_ref):
    x = x_ref[...].astype(F32)
    t0 = x[:, 0:128]
    t1 = x[:, 128:256]
    t2 = jnp.concatenate([x[:, 256:320], jnp.zeros((ROWS, 64), F32)], axis=1)
    low = lane_index((ROWS, LANES)) < 64
    low_half = lane_index((HALF, LANES)) < 64
    even = jnp.bitwise_and(parity[0], 1) == 0

    @pl.when(even)
    def _():
        o_ref[0, 0:ROWS] = t0.astype(BF)
        o_ref[0, ROWS : 2 * ROWS] = t1.astype(BF)
        o_ref[0, 2 * ROWS : PACKED] = jnp.where(
            low_half, t2[:HALF], swap_halves(t2[HALF:])
        ).astype(BF)

    @pl.when(jnp.logical_not(even))
    def _():
        s0, s1, s2 = swap_halves(t0), swap_halves(t1), swap_halves(t2)
        o_ref[0, 0:ROWS] = jnp.where(low, s0, s1).astype(BF)
        o_ref[0, ROWS : 2 * ROWS] = jnp.where(low, s1, s2).astype(BF)
        o_ref[0, 2 * ROWS : PACKED] = jnp.where(low_half, t0[:HALF], s0[HALF:]).astype(BF)


def pack_rows(rows, parity):
    blocks = rows.shape[0] // ROWS
    return pl.pallas_call(
        pack_kernel,
        out_shape=jax.ShapeDtypeStruct((blocks, PACKED, LANES), BF),
        grid_spec=pltpu.PrefetchScalarGridSpec(
            num_scalar_prefetch=1,
            grid=(blocks,),
            in_specs=[pl.BlockSpec((ROWS, WIDTH), lambda b, p: (b, 0))],
            out_specs=pl.BlockSpec((1, PACKED, LANES), lambda b, p: (b, 0, 0)),
        ),
        name="pack_rows",
    )(parity, rows)


def finish_kernel(parity, own_ref, up_ref, down_ref, x_ref, o_ref):
    packed = (
        own_ref[0].astype(F32) + up_ref[0].astype(F32) + down_ref[0].astype(F32)
    )
    m0 = packed[0:ROWS]
    m1 = packed[ROWS : 2 * ROWS]
    packed_tail = packed[2 * ROWS : PACKED]
    tail = jnp.concatenate([packed_tail, swap_halves(packed_tail)], axis=0)
    low = lane_index((ROWS, LANES)) < 64
    even = jnp.bitwise_and(parity[0], 1) == 0

    @pl.when(even)
    def _():
        total = jnp.concatenate([m0, m1, tail], axis=1)[:, :WIDTH]
        o_ref[...] = (x_ref[...].astype(F32) + total).astype(BF)

    @pl.when(jnp.logical_not(even))
    def _():
        s0, s1 = swap_halves(m0), swap_halves(m1)
        total = jnp.concatenate(
            [jnp.where(low, tail, s0), jnp.where(low, s0, s1), s1], axis=1
        )[:, :WIDTH]
        o_ref[...] = (x_ref[...].astype(F32) + total).astype(BF)


def finish_rows(own, up, down, rows, parity):
    blocks = rows.shape[0] // ROWS
    packed = pl.BlockSpec((1, PACKED, LANES), lambda b, p: (b, 0, 0))
    flat = pl.BlockSpec((ROWS, WIDTH), lambda b, p: (b, 0))
    return pl.pallas_call(
        finish_kernel,
        out_shape=jax.ShapeDtypeStruct(rows.shape, BF),
        grid_spec=pltpu.PrefetchScalarGridSpec(
            num_scalar_prefetch=1,
            grid=(blocks,),
            in_specs=[packed, packed, packed, flat],
            out_specs=flat,
        ),
        name="finish_rows",
    )(parity, own, up, down, rows)


def arrange_kernel(me, wq_ref, wkv_ref, wo_ref, w_ref, o_ref):
    o_ref[...] = jnp.zeros_like(o_ref)
    query = GROUP * LANES
    low = lane_index((GROUP * HD, LANES)) < 64
    for j in range(N_TP // 2):
        base = j * 5 * LANES
        tails = []
        for k, at, tail_at in (
            (2 * j, base, base + 256),
            (2 * j + 1, base + 384, base + 320),
        ):
            device = jnp.bitwise_and(me[0] + k, N_TP - 1)
            odd = jnp.bitwise_and(device, 1)
            main_from = pl.multiple_of(device * WIDTH + 64 * odd, 64)
            tail_from = pl.multiple_of(device * WIDTH + 256 * (1 - odd), 64)
            w_ref[at : at + 256, :query] = wq_ref[pl.ds(main_from, 256), :]
            w_ref[at : at + 256, query:] = wkv_ref[pl.ds(main_from, 256), :]
            w_ref[tail_at : tail_at + 64, :query] = wq_ref[pl.ds(tail_from, 64), :]
            w_ref[tail_at : tail_at + 64, query:] = wkv_ref[pl.ds(tail_from, 64), :]
            tile = device // 2 * 5
            for part in range(2):
                column = pl.multiple_of((tile + 3 * odd + part) * LANES, LANES)
                piece = wo_ref[:, pl.ds(column, LANES)]
                for h in range(GROUP):
                    o_ref[
                        h * LANES : h * LANES + HD,
                        at + part * LANES : at + (part + 1) * LANES,
                    ] = piece[h * HD : (h + 1) * HD]
            column = pl.multiple_of((tile + 2) * LANES, LANES)
            tail = wo_ref[:, pl.ds(column, LANES)].astype(F32)
            wrong = odd == (1 - k % 2)
            tails.append(jnp.where(wrong, swap_halves(tail), tail))
        joined = jnp.where(low, tails[0], tails[1]).astype(BF)
        for h in range(GROUP):
            o_ref[h * LANES : h * LANES + HD, base + 256 : base + 384] = joined[
                h * HD : (h + 1) * HD
            ]


def arrange_weights(wq, wkv, w_out, me):
    return pl.pallas_call(
        arrange_kernel,
        out_shape=(
            jax.ShapeDtypeStruct((D, (GROUP + 2) * LANES), BF),
            jax.ShapeDtypeStruct((GROUP * LANES, D), BF),
        ),
        in_specs=[pl.BlockSpec(memory_space=pltpu.SMEM)]
        + [pl.BlockSpec(memory_space=pltpu.VMEM)] * 3,
        out_specs=(
            pl.BlockSpec(memory_space=pltpu.VMEM),
            pl.BlockSpec(memory_space=pltpu.VMEM),
        ),
        compiler_params=pltpu.CompilerParams(vmem_limit_bytes=VMEM_LIMIT),
        name="arrange_weights",
    )(me, wq, wkv, w_out)


def prep_kernel(parents_ref, cos_ref, sin_ref, step_ref, bias_out, cos_out, sin_out):
    requests = parents_ref.shape[0]
    lane = lane_index((requests, LANES))
    step_cos = step_ref[0:1, :]
    step_sin = step_ref[1:2, :]
    sign = step_ref[2:3, :]
    parents = parents_ref[...]
    marks = jnp.where(lane == 0, 1.0, 0.0)
    cosines, sines = cos_ref[...], sin_ref[...]
    older = (marks, cosines, sines)
    newer = older
    for t in range(TREE):
        if t > 0:
            near = jnp.broadcast_to(parents[:, t : t + 1], (requests, LANES)) == t - 1
            marks, cosines, sines = (jnp.where(near, a, b) for a, b in zip(newer, older))
            marks = jnp.where(lane == t, 1.0, marks)
            if t > 0:
                cosines, sines = (
                    cosines * step_cos - sines * step_sin,
                    sines * step_cos + cosines * step_sin,
                )
            older, newer = newer, (marks, cosines, sines)
        bias_out[:, t, :] = jnp.where(marks > 0.5, 0.0, NEG)
        cos_out[:, t, :] = cosines
        sin_out[:, t, :] = sines * sign


def prepare_tables(parents, lengths):
    requests = parents.shape[0]
    lane = jnp.arange(LANES)
    pair = jnp.where(lane < HD // 2, lane, lane - HD // 2)
    frequency = 10000.0 ** (-2.0 * pair.astype(F32) / HD)
    angles = lengths.astype(F32)[:, None] * frequency[None, :]
    sign = jnp.where(lane < HD // 2, -1.0, jnp.where(lane < HD, 1.0, 0.0))
    steps = jnp.stack([jnp.cos(frequency), jnp.sin(frequency), sign] + [sign] * 5)
    table = jax.ShapeDtypeStruct((requests, TREE, LANES), F32)
    return pl.pallas_call(
        prep_kernel, out_shape=(table, table, table), name="prepare_tables"
    )(parents, jnp.cos(angles), jnp.sin(angles), steps)


def order_kernel(order, cache_ref, out_ref, buffer, load_sems, store_sems):
    loads, stores = [], []
    for d in range(cache_ref.shape[0]):
        loads.append(
            pltpu.make_async_copy(cache_ref.at[order[d]], buffer.at[d], load_sems.at[d])
        )
        loads[-1].start()
    for d, load in enumerate(loads):
        load.wait()
        stores.append(pltpu.make_async_copy(buffer.at[d], out_ref.at[d], store_sems.at[d]))
        stores[-1].start()
    for store in stores:
        store.wait()


def order_cache(kv_cache, send_order):
    held = kv_cache.shape[0]
    return pl.pallas_call(
        order_kernel,
        out_shape=jax.ShapeDtypeStruct(kv_cache.shape, BF),
        grid_spec=pltpu.PrefetchScalarGridSpec(
            num_scalar_prefetch=1,
            grid=(1,),
            in_specs=[pl.BlockSpec(memory_space=pl.ANY)],
            out_specs=pl.BlockSpec(memory_space=pl.ANY),
            scratch_shapes=[
                pltpu.VMEM(kv_cache.shape, BF),
                pltpu.SemaphoreType.DMA((held,)),
                pltpu.SemaphoreType.DMA((held,)),
            ],
        ),
        compiler_params=pltpu.CompilerParams(vmem_limit_bytes=VMEM_LIMIT),
        name="order_cache",
    )(send_order, kv_cache)


def layer_kernel(lengths, accepted, destination, *refs):
    x_refs = refs[: N_TP + 1]
    w_ref, wo_ref, cache_ref, bias_ref, cos_ref, sin_ref = refs[N_TP + 1 : N_TP + 7]
    out_refs = refs[N_TP + 7 : 2 * N_TP + 7]
    extra_out, xs, qkv, ctx, extra, sems = refs[2 * N_TP + 7 :]
    b = pl.program_id(0)

    @pl.when(b == 0)
    def _():
        ctx[...] = jnp.zeros_like(ctx)
        extra[...] = jnp.zeros_like(extra)

    def received(k, first, last):
        piece = x_refs[k][0, first:last]
        if k == N_TP // 2:
            piece = jnp.where(b < HALF_BLOCKS, piece, x_refs[N_TP][0, first:last])
        return piece

    low_half = lane_index((HALF, LANES)) < 64
    squares = jnp.zeros((ROWS, LANES), F32)
    for j in range(N_TP // 2):
        base = j * 5 * LANES
        for device, at in ((2 * j, base), (2 * j + 1, base + 3 * LANES)):
            for part in range(2):
                piece = received(device, part * ROWS, (part + 1) * ROWS)
                xs[:, at + part * LANES : at + (part + 1) * LANES] = piece
                wide = piece.astype(F32)
                squares = squares + wide * wide
        even_tail = received(2 * j, 2 * ROWS, PACKED).astype(F32)
        odd_tail = received(2 * j + 1, 2 * ROWS, PACKED).astype(F32)
        tail = jnp.concatenate(
            [
                jnp.where(low_half, even_tail, swap_halves(odd_tail)),
                jnp.where(low_half, swap_halves(even_tail), odd_tail),
            ],
            axis=0,
        )
        xs[:, base + 2 * LANES : base + 3 * LANES] = tail.astype(BF)
        squares = squares + tail * tail
    scale = lax.rsqrt(jnp.sum(squares, axis=1, keepdims=True) * (1.0 / D) + 1e-05)
    flat = xs[...]
    projected = jnp.dot(flat, w_ref[...], preferred_element_type=F32) * scale
    cosines = cos_ref[...].reshape(ROWS, LANES)
    sines = sin_ref[...].reshape(ROWS, LANES)
    first = lane_index((ROWS, LANES)) < HD // 2

    def rotate(tile):
        other = jnp.where(
            first, pltpu.roll(tile, LANES - HD // 2, 1), pltpu.roll(tile, HD // 2, 1)
        )
        return tile * cosines + other * sines

    for h in range(GROUP + 1):
        head = slice(h * LANES, (h + 1) * LANES)
        qkv[:, head] = rotate(projected[:, head])
    qkv[:, (GROUP + 1) * LANES :] = projected[:, (GROUP + 1) * LANES :]

    factor = math.log2(math.e) / math.sqrt(HD)
    column = lane_index((GROUP * TREE, CACHE))
    extra_row = lax.broadcasted_iota(jnp.int32, (EXTRA, LANES), 0)
    extra_lane = lane_index((EXTRA, LANES))
    pick_row = lax.broadcasted_iota(jnp.int32, (EXTRA, TREE), 0)
    pick_column = lane_index((EXTRA, TREE))
    copies = []
    for i in range(REQ_BLOCK):
        r = b * REQ_BLOCK + i
        length = lengths[r]
        rows = slice(i * TREE, (i + 1) * TREE)
        q = jnp.concatenate(
            [qkv[rows, h * LANES : (h + 1) * LANES] for h in range(GROUP)], axis=0
        ).astype(BF)
        k = qkv[rows, GROUP * LANES : (GROUP + 1) * LANES].astype(BF)
        v = qkv[rows, (GROUP + 1) * LANES :].astype(BF)
        cached = jnp.dot(q[:, :HD], cache_ref[i, 0:HD], preferred_element_type=F32)
        cached = jnp.where(column < length, cached * factor, NEG)
        fresh = lax.dot_general(q, k, (((1,), (1,)), ((), ())), preferred_element_type=F32)
        bias = bias_ref[i][:, :TREE]
        fresh = fresh * factor + jnp.concatenate([bias] * GROUP, axis=0)
        top = jnp.maximum(
            jnp.max(cached, axis=1, keepdims=True), jnp.max(fresh, axis=1, keepdims=True)
        )
        cached = jnp.exp2(cached - top)
        fresh = jnp.exp2(fresh - top)
        total = jnp.sum(cached, axis=1, keepdims=True) + jnp.sum(fresh, axis=1, keepdims=True)
        mixed = lax.dot_general(
            cached.astype(BF),
            cache_ref[i, HD : 2 * HD],
            (((1,), (1,)), ((), ())),
            preferred_element_type=F32,
        ) + jnp.dot(fresh.astype(BF), v[:, :HD], preferred_element_type=F32)
        mixed = mixed / total
        for h in range(GROUP):
            ctx[rows, h * LANES : h * LANES + HD] = mixed[h * TREE : (h + 1) * TREE]

        wanted = jnp.full((EXTRA, TREE), -1, jnp.int32)
        for m in range(DEPTH):
            wanted = jnp.where(pick_row == m, accepted[r * DEPTH + m], wanted)
        pick = jnp.where(pick_column == wanted, 1.0, 0.0).astype(BF)
        new_keys = jnp.dot(pick, k, preferred_element_type=F32)
        new_values = jnp.dot(pick, v, preferred_element_type=F32)
        coarse = (length // 16).astype(F32)
        fine = (length % 16).astype(F32)
        shifted = pltpu.roll(new_values, HD, 1)
        new_keys = jnp.where(extra_lane < HD, new_keys, shifted)
        extra[i, :, 0:LANES] = jnp.where(
            extra_row == 8, coarse, jnp.where(extra_row == 9, fine, new_keys)
        ).astype(BF)
        extra[i, :, LANES : 2 * LANES] = jnp.where(
            extra_lane < 2 * HD - LANES, shifted, 0.0
        ).astype(BF)
        copies.append(
            pltpu.make_async_copy(
                extra.at[i], extra_out.at[destination[r]], sems.at[i]
            )
        )
        copies[-1].start()

    partial = jnp.dot(ctx[...].astype(BF), wo_ref[...], preferred_element_type=F32)
    for j in range(N_TP // 2):
        base = j * 5 * LANES
        for device, at in ((2 * j, base), (2 * j + 1, base + 3 * LANES)):
            for part in range(2):
                out_refs[device][0, part * ROWS : (part + 1) * ROWS] = partial[
                    :, at + part * LANES : at + (part + 1) * LANES
                ].astype(BF)
        tail = partial[:, base + 2 * LANES : base + 3 * LANES]
        out_refs[2 * j][0, 2 * ROWS : PACKED] = jnp.where(
            low_half, tail[:HALF], swap_halves(tail[HALF:])
        ).astype(BF)
        out_refs[2 * j + 1][0, 2 * ROWS : PACKED] = jnp.where(
            low_half, swap_halves(tail[:HALF]), tail[HALF:]
        ).astype(BF)
    for copy in copies:
        copy.wait()


def verify_layer(parts, w, wo, kv_cache, tables, lengths, accepted, destination):
    held = kv_cache.shape[0]
    blocks = held // REQ_BLOCK
    full = lambda b, *_: (0, 0)
    packed = pl.BlockSpec((1, PACKED, LANES), lambda b, *_: (b, 0, 0))
    table = pl.BlockSpec((REQ_BLOCK, TREE, LANES), lambda b, *_: (b, 0, 0))
    in_specs = [packed] * (N_TP + 1)
    in_specs[N_TP // 2] = pl.BlockSpec(
        (1, PACKED, LANES), lambda b, *_: (jnp.minimum(b, HALF_BLOCKS - 1), 0, 0)
    )
    in_specs[N_TP] = pl.BlockSpec(
        (1, PACKED, LANES), lambda b, *_: (jnp.maximum(b - HALF_BLOCKS, 0), 0, 0)
    )
    return pl.pallas_call(
        layer_kernel,
        out_shape=[jax.ShapeDtypeStruct((blocks, PACKED, LANES), BF)] * N_TP
        + [jax.ShapeDtypeStruct((held, EXTRA, 2 * LANES), BF)],
        grid_spec=pltpu.PrefetchScalarGridSpec(
            num_scalar_prefetch=3,
            grid=(blocks,),
            in_specs=in_specs
            + [
                pl.BlockSpec(w.shape, full),
                pl.BlockSpec(wo.shape, full),
                pl.BlockSpec((REQ_BLOCK, 2 * HD, CACHE), lambda b, *_: (b, 0, 0)),
                table,
                table,
                table,
            ],
            out_specs=[packed] * N_TP + [pl.BlockSpec(memory_space=pl.ANY)],
            scratch_shapes=[
                pltpu.VMEM((ROWS, D), BF),
                pltpu.VMEM((ROWS, (GROUP + 2) * LANES), F32),
                pltpu.VMEM((ROWS, GROUP * LANES), F32),
                pltpu.VMEM((REQ_BLOCK, EXTRA, 2 * LANES), BF),
                pltpu.SemaphoreType.DMA((REQ_BLOCK,)),
            ],
        ),
        compiler_params=pltpu.CompilerParams(vmem_limit_bytes=VMEM_LIMIT),
        cost_estimate=pl.CostEstimate(
            flops=30_000_000_000, transcendentals=0, bytes_accessed=10_000_000
        ),
        name="verify_layer",
    )(lengths, accepted, destination, *parts, w, wo, kv_cache, *tables)


def assemble_kernel(cache_ref, extra_ref, o_ref):
    place_row = lax.broadcasted_iota(jnp.int32, (EXTRA, CACHE), 0)
    place_column = lane_index((EXTRA, CACHE))
    for i in range(cache_ref.shape[0]):
        extra = extra_ref[i]
        wide = extra[:, :LANES].astype(F32)
        length = (wide[8:9] * 16.0 + wide[9:10]).astype(jnp.int32)
        length = jnp.concatenate([length] * (CACHE // LANES), axis=1)
        offset = place_column - length
        place = jnp.where(
            jnp.logical_and(offset == place_row, place_row < DEPTH), 1.0, 0.0
        ).astype(BF)
        live = jnp.where(offset[0:1] < 0, 1.0, 0.0).astype(BF)
        new = lax.dot_general(
            extra, place, (((0,), (0,)), ((), ())), preferred_element_type=F32
        ).astype(BF)
        o_ref[i] = cache_ref[i] * live + new[: 2 * HD]


def assemble_cache(cached, extra):
    step = 4
    cache_spec = pl.BlockSpec((step,) + cached.shape[1:], lambda s: (s, 0, 0))
    extra_spec = pl.BlockSpec((step,) + extra.shape[1:], lambda s: (s, 0, 0))
    return pl.pallas_call(
        assemble_kernel,
        out_shape=jax.ShapeDtypeStruct(cached.shape, BF),
        grid=(cached.shape[0] // step,),
        in_specs=[cache_spec, extra_spec],
        out_specs=cache_spec,
        name="assemble_cache",
    )(cached, extra)


def spread_heads(heads):
    source = jnp.arange(heads * HD)[:, None]
    target = jnp.arange(heads * LANES)[None, :]
    return (source // HD * LANES + source % HD == target).astype(BF)


def exchange(values):
    return lax.all_to_all(values, "req", split_axis=0, concat_axis=0, tiled=True)


def go_up(values):
    return lax.ppermute(values, "tp", [(i, (i + 1) % N_TP) for i in range(N_TP)])


def go_down(values):
    return lax.ppermute(values, "tp", [(i, (i - 1) % N_TP) for i in range(N_TP)])


def add_up(a, b):
    return (a.astype(F32) + b.astype(F32)).astype(BF)


def gather_ring(packed):
    parts = [packed] * (N_TP + 1)
    from_below = from_above = packed
    for step in range(1, N_TP // 2):
        from_below = go_up(from_below)
        from_above = go_down(from_above)
        parts[N_TP - step] = from_below
        parts[step] = from_above
    parts[N_TP // 2] = go_up(from_below[:HALF_BLOCKS])
    parts[N_TP] = go_down(from_above[HALF_BLOCKS:])
    return parts


def scatter_ring(targets):
    half = N_TP // 2
    up = go_up(targets[half][:HALF_BLOCKS])
    down = go_down(targets[half][HALF_BLOCKS:])
    for step in range(1, half):
        above, below = targets[half - step], targets[half + step]
        if step == 1:
            above = jnp.concatenate([add_up(above[:HALF_BLOCKS], up), above[HALF_BLOCKS:]])
            below = jnp.concatenate([below[:HALF_BLOCKS], add_up(below[HALF_BLOCKS:], down)])
        else:
            above, below = add_up(above, up), add_up(below, down)
        up = go_up(above)
        down = go_down(below)
    return up, down


def per_device(
    hidden, norm_gain, w_query, w_keyval, w_out, kv_cache, lengths, parents, accepted, slot_of
):
    held = hidden.shape[0]
    rows = hidden.reshape(held * TREE, WIDTH)
    me = lax.axis_index("tp").astype(jnp.int32).reshape(1)
    parts = gather_ring(pack_rows(rows, me))

    destination = slot_of // held
    peer_index = jnp.arange(held, dtype=jnp.int32)
    matches = (destination[None, :] == peer_index[:, None]).astype(jnp.int32)
    send_order = jnp.sum(matches * peer_index[None, :], axis=1)
    cached = exchange(order_cache(kv_cache, send_order))

    tables = prepare_tables(parents, lengths)
    gain = norm_gain[:, None]
    wq = (jnp.dot(w_query, spread_heads(GROUP), preferred_element_type=F32) * gain).astype(BF)
    wkv = lax.dot_general(
        w_keyval, spread_heads(2), (((0,), (0,)), ((), ())), preferred_element_type=F32
    )
    wkv = (wkv * gain).astype(BF)
    w, wo = arrange_weights(wq, wkv, w_out, me)

    *targets, extra = verify_layer(
        parts, w, wo, kv_cache, tables, lengths, accepted.reshape(-1), destination
    )
    cached, extra = lax.optimization_barrier((cached, extra))
    new_cache = assemble_cache(cached, exchange(extra))
    up, down = scatter_ring(targets)
    out_rows = finish_rows(targets[0], up, down, rows, me)
    return (out_rows.reshape(hidden.shape), new_cache)


def solution(mesh):
    in_specs = (
        P("req", None, "tp"),
        P(),
        P(None, "tp"),
        P("tp", None),
        P("tp", None),
        P("req", "tp", None),
        P("req"),
        P("req", None),
        P("req", None),
        P("req"),
    )
    out_specs = (P("req", None, "tp"), P("req", "tp", None))
    return jax.shard_map(
        per_device, mesh=mesh, in_specs=in_specs, out_specs=out_specs, check_vma=False
    )
```

time: 158 us -> 155 us (0.981)
  blocking collectives: 47 us -> 0 us
  starting transfers between devices: 8.86 us -> 45.5 us
  between operations: 14.2 us -> 1.01 us
  waiting for transfers between devices: 29.3 us -> 36 us
  Pallas kernels: 48.6 us -> 54.9 us
  local copies, waits for them, and re-layouts: 2.06 us -> 7.55 us
  other arithmetic: 2.19 us -> 4.7 us
    all_to_all x1 -> x0, blocking collectives: 47 us -> none  [exchange(): lax.all_to_all(values, 'req', split_axis=0, concat_axis=0, tiled=True)]
    ppermute x0 -> x16, waiting for transfers between devices: none -> 31.7 us  [the longest x8 16.2 us: go_up(): lax.ppermute(values, 'tp', [(i, (i + 1) % N_TP) for i in range(N_TP)])]
    ppermute x0 -> x16, starting transfers between devices: none -> 23.9 us  [the longest x8 19.3 us: go_down(): lax.ppermute(values, 'tp', [(i, (i - 1) % N_TP) for i in range(N_TP)])]
    all_to_all x1 -> x2, waiting for transfers between devices: 23.2 us -> 4.23 us  [exchange(): lax.all_to_all(values, 'req', split_axis=0, concat_axis=0, tiled=True)]
    all_to_all x1 -> x2, starting transfers between devices: 8.78 us -> 21.6 us  [exchange(): lax.all_to_all(values, 'req', split_axis=0, concat_axis=0, tiled=True)]
    all_gather x1 -> x0, waiting for transfers between devices: 6.09 us -> none  [per_device(): gathered = lax.all_gather(packed, 'tp', axis=0, tiled=False)]
    pallas_call x3 -> x4, Pallas kernels: 39 us -> 45 us  [the longest x1 24.8 us: verify_layer(): pl.pallas_call(layer_kernel, out_shape=[jax.ShapeDtypeStruct((blocks, PAC...]
    slice x0 -> x5, local copies, waits for them, and re-layouts: none -> 3.19 us  [the longest x1 1.18 us: scatter_ring(): down = go_down(targets[half][HALF_BLOCKS:])]
  transfers between devices with their start and end apart: 3 -> 18, of which waited for: 2 -> 6; matrix products, arithmetic and copies ran while one was open for 6% -> 10% of each run, Pallas kernels for 11% -> 28%
where the time goes in v4:
time: 155 us
  Pallas kernels  54.9 us (35%)
  starting transfers between devices  45.5 us (29%)
  waiting for transfers between devices  36 us (23%)
  local copies, waits for them, and re-layouts  7.55 us (5%)
  matrix products  5.14 us (3%)
  other arithmetic  4.7 us (3%)
    pallas_call x1, Pallas kernels, verify_layer(): pl.pallas_call(layer_kernel, out_shape=[jax.ShapeDtypeStruct((blocks, PAC...  24.8 us
    all_to_all x2, starting transfers between devices, exchange(): lax.all_to_all(values, 'req', split_axis=0, concat_axis=0, tiled=True)  21.6 us
    ppermute x8, starting transfers between devices, go_down(): lax.ppermute(values, 'tp', [(i, (i - 1) % N_TP) for i in range(N_TP)])  19.3 us
    ppermute x8, waiting for transfers between devices, go_up(): lax.ppermute(values, 'tp', [(i, (i + 1) % N_TP) for i in range(N_TP)])  16.2 us
    ppermute x8, waiting for transfers between devices, go_down(): lax.ppermute(values, 'tp', [(i, (i - 1) % N_TP) for i in range(N_TP)])  15.6 us
    pallas_call x1, Pallas kernels, assemble_cache(): pl.pallas_call(assemble_kernel, out_shape=jax.ShapeDtypeStruct(cached.sha...  8.38 us
    pallas_call x1, Pallas kernels, arrange_weights(): pl.pallas_call(arrange_kernel, out_shape=(jax.ShapeDtypeStruct((D, (GROUP...  5.99 us
    pallas_call x1, Pallas kernels, order_cache(): pl.pallas_call(order_kernel, out_shape=jax.ShapeDtypeStruct(kv_cache.shap...  5.83 us
  transfers between devices with their start and end apart: 18, of which 6 were waited for; matrix products, arithmetic and copies ran while one was open for 10% of the time, Pallas kernels for 28%

profile of v4, /device:TPU:1, one launch (start us, length us, event | category | flops | bytes accessed | tf_op | source)
XLA Modules:
  0.0 154.7 jit_solution(14217460841935776500)
XLA Ops:
  0.6 3.4 %pack_rows.1.refs_0_ = bf16[4,480,128]{2,1,0:T(8,128)(2,1)} custom-call(s32[1]{0:T(128)} %bitcast.parity.me, bf16[768,320]{1,0:T(8,128)(2,1)} %bitcast.9), custom_call_target="tpu_custom_call" | custom-call | tf_op jit(solution)/shard_map/pack_rows/pallas_call | solution.py:68
  4.1 2.5 %collective-permute-start.3 = (bf16[4,480,128]{2,1,0:T(8,128)(2,1)}, bf16[4,480,128]{2,1,0:T(8,128)(2,1)S(1)}, u32[]{:S(2)}, u32[]{:S(2)}) collective-permute-start(bf16[4,480,128]{2,1,0:T(8,128)(2,1)} %pack_rows.1.refs_0_), channel_id=1, source_target_pairs={{0,1},{1,2},{2,3},{3,4},{4,5},{5,6},{6,7},{7,0},{8,9},{9,10},{10,1... | collective-permute-start | bytes 1474568 | tf_op jit(solution)/shard_map/ppermute | solution.py:483
  6.6 3.9 %collective-permute-start = (bf16[4,480,128]{2,1,0:T(8,128)(2,1)}, bf16[4,480,128]{2,1,0:T(8,128)(2,1)}, u32[]{:S(2)}, u32[]{:S(2)}) collective-permute-start(bf16[4,480,128]{2,1,0:T(8,128)(2,1)} %pack_rows.1.refs_0_), channel_id=1, source_target_pairs={{0,7},{1,0},{2,1},{3,2},{4,3},{5,4},{6,5},{7,6},{8,15},{9,8},{10,9... | collective-permute-start | bytes 1474568 | tf_op jit(solution)/shard_map/ppermute | solution.py:487
  10.6 0.7 and_select_fusion.2.destination
  11.2 0.7 select_reduce_fusion.order
  11.9 5.8 %order_cache.1 = bf16[32,160,512]{2,1,0:T(8,128)(2,1)} custom-call(s32[32]{0:T(128)} %select_reduce_fusion.order, bf16[32,160,512]{2,1,0:T(8,128)(2,1)} %cache_ref.1), custom_call_target="tpu_custom_call" | custom-call | tf_op jit(solution)/shard_map/order_cache/pallas_call | solution.py:238
  17.8 8.2 %all-to-all-start = ((bf16[32,160,512]{2,1,0:T(8,128)(2,1)}), bf16[32,160,512]{2,1,0:T(8,128)(2,1)}, u32[]{:S(2)}, u32[]{:S(2)}) async-start(bf16[32,160,512]{2,1,0:T(8,128)(2,1)} %order_cache.1), calls=%async_computation | async-start | bytes 10485760 | tf_op jit(solution)/shard_map/all_to_all | solution.py:479
  26.0 0.1 collective-permute-start.4
  26.1 2.7 %collective-permute-start.1 = (bf16[4,480,128]{2,1,0:T(8,128)(2,1)}, bf16[4,480,128]{2,1,0:T(8,128)(2,1)S(1)}, u32[]{:S(2)}, u32[]{:S(2)}) collective-permute-start(bf16[4,480,128]{2,1,0:T(8,128)(2,1)} %collective-permute-done.refs_1_), channel_id=1, source_target_pairs={{0,7},{1,0},{2,1},{3,2},{4,3},{5,4},{6,5},{7,6},{8,15},{9,8},{10,9... | collective-permute-start | bytes 1474568 | tf_op jit(solution)/shard_map/ppermute | solution.py:487
  28.9 2.0 %fusion.2.wkv_ref = bf16[2560,256]{1,0:T(8,128)(2,1)} fusion(bf16[160,2560]{1,0:T(8,128)(2,1)S(1)} %copy-done.2, f32[2560]{0:T(1024)S(1)} %copy-done.12, s32[160]{0:T(256)S(1)} %fusion.16), kind=kOutput, calls=%fused_computation.4 | convolution fusion | flops 211066880 | bytes 2140800 | tf_op jit(solution)/shard_map/dot_general | solution.py:540
  30.9 9.1 %collective-permute-done.4.refs_6_ = bf16[4,480,128]{2,1,0:T(8,128)(2,1)S(1)} collective-permute-done((bf16[4,480,128]{2,1,0:T(8,128)(2,1)S(1)}, bf16[4,480,128]{2,1,0:T(8,128)(2,1)S(1)}, u32[]{:S(2)}, u32[]{:S(2)}) %collective-permute-start.4) | collective-permute-done | bytes 491552 | tf_op jit(solution)/shard_map/ppermute | solution.py:483
  40.0 2.7 %collective-permute-start.2 = (bf16[4,480,128]{2,1,0:T(8,128)(2,1)S(1)}, bf16[4,480,128]{2,1,0:T(8,128)(2,1)S(1)}, u32[]{:S(2)}, u32[]{:S(2)}) collective-permute-start(bf16[4,480,128]{2,1,0:T(8,128)(2,1)S(1)} %collective-permute-done.1.refs_2_), channel_id=1, source_target_pairs={{0,7},{1,0},{2,1},{3,2},{4,3},{5,4},{6,5},{7,6},{8,15},{9,8},{10,9... | collective-permute-start | bytes 1474568 | tf_op jit(solution)/shard_map/ppermute | solution.py:487
  42.7 3.2 %fusion.wq_ref = bf16[2560,512]{1,0:T(8,128)(2,1)} fusion(bf16[2560,320]{0,1:T(8,128)(2,1)S(1)} %copy-done, f32[2560]{0:T(1024)S(1)} %copy-done.12, s32[320]{0:T(512)S(1)} %fusion.10), kind=kOutput, calls=%fused_computation.2 | convolution fusion | flops 841646080 | bytes 4271360 | tf_op jit(solution)/shard_map/dot_general | solution.py:539
  45.9 7.0 %collective-permute-done.5.refs_5_ = bf16[4,480,128]{2,1,0:T(8,128)(2,1)S(1)} collective-permute-done((bf16[4,480,128]{2,1,0:T(8,128)(2,1)S(1)}, bf16[4,480,128]{2,1,0:T(8,128)(2,1)S(1)}, u32[]{:S(2)}, u32[]{:S(2)}) %collective-permute-start.5) | collective-permute-done | bytes 491552 | tf_op jit(solution)/shard_map/ppermute | solution.py:483
  53.1 2.9 %collective-permute-start.7 = (bf16[2,480,128]{2,1,0:T(8,128)(2,1)S(1)}, bf16[2,480,128]{2,1,0:T(8,128)(2,1)}, u32[]{:S(2)}, u32[]{:S(2)}) collective-permute-start(bf16[2,480,128]{2,1,0:T(8,128)(2,1)S(1)} %slice.33), channel_id=1, source_target_pairs={{0,7},{1,0},{2,1},{3,2},{4,3},{5,4},{6,5},{7,6},{8,15},{9,8},{10,9... | collective-permute-start | bytes 737288 | tf_op jit(solution)/shard_map/ppermute | solution.py:487
  56.1 0.7 copy.23.parents_ref
  56.7 0.1 copy.20
  56.8 0.6 reshape.146.accepted
  57.4 0.6 stack.2.step_ref
  58.0 6.0 %arrange_weights.1 = (bf16[2560,768]{1,0:T(8,128)(2,1)}, bf16[512,2560]{1,0:T(8,128)(2,1)}) custom-call(s32[1]{0:T(128)} %bitcast.parity.me, bf16[2560,512]{1,0:T(8,128)(2,1)} %fusion.wq_ref, bf16[2560,256]{1,0:T(8,128)(2,1)} %fusion.2.wkv_ref, bf16[320,2560]{1,0:T(8,128)(2,1)} %wo_ref.1), custom_call_target="tpu_custom_call" | custom-call | tf_op jit(solution)/shard_map/arrange_weights/pallas_call | solution.py:163
  64.0 0.8 multiply_sine_fusion
  64.8 2.6 %prepare_tables.1 = (f32[32,24,128]{2,1,0:T(8,128)}, f32[32,24,128]{2,1,0:T(8,128)}, f32[32,24,128]{2,1,0:T(8,128)}) custom-call(s32[32,24]{1,0:T(8,128)} %copy.23.parents_ref, f32[32,128]{1,0:T(8,128)} %get-tuple-element.37.cos_ref, f32[32,128]{1,0:T(8,128)} %get-tuple-element.36.sin_ref, f32[8,128]{1,0:T(8,128)} %stack.2.step_ref), custom_call_target="tpu_custom_call" | custom-call | tf_op jit(solution)/shard_map/prepare_tables/pallas_call | solution.py:216
  67.4 0.7 copy-done.18
  68.1 24.8 %verify_layer.1 = (bf16[4,480,128]{2,1,0:T(8,128)(2,1)}, bf16[4,480,128]{2,1,0:T(8,128)(2,1)}, bf16[4,480,128]{2,1,0:T(8,128)(2,1)}, bf16[4,480,128]{2,1,0:T(8,1...) custom-call(s32[32]{0:T(128)} %lengths.1, ...), custom_call_target="tpu_custom_call" | custom-call | flops 30000001024 | bytes 10000000 | tf_op jit(solution)/shard_map/verify_layer/pallas_call | solution.py:406
  92.9 1.2 fusion.26
  94.1 0.1 collective-permute-start.12
  94.2 1.0 slice.29
  95.2 1.5 collective-permute-start.8
  96.7 1.0 slice.28
  97.7 1.5 collective-permute-done.12
  99.2 1.0 add_convert_fusion.4
  100.3 1.3 collective-permute-start.13
  101.8 0.3 collective-permute-start.9
  102.1 7.5 %collective-permute-done.13 = bf16[4,480,128]{2,1,0:T(8,128)(2,1)S(1)} collective-permute-done((bf16[4,480,128]{2,1,0:T(8,128)(2,1)S(1)}, bf16[4,480,128]{2,1,0:T(8,128)(2,1)S(1)}, u32[]{:S(2)}, u32[]{:S(2)}) %collective-permute-start.13) | collective-permute-done | bytes 491552 | tf_op jit(solution)/shard_map/ppermute | solution.py:487
  109.6 0.1 add_convert_fusion.1
  109.7 2.7 %collective-permute-start.14 = (bf16[4,480,128]{2,1,0:T(8,128)(2,1)S(1)}, bf16[4,480,128]{2,1,0:T(8,128)(2,1)S(1)}, u32[]{:S(2)}, u32[]{:S(2)}) collective-permute-start(bf16[4,480,128]{2,1,0:T(8,128)(2,1)S(1)} %add_convert_fusion.1), channel_id=1, source_target_pairs={{0,7},{1,0},{2,1},{3,2},{4,3},{5,4},{6,5},{7,6},{8,15},{9,8},{10,9... | collective-permute-start | bytes 1474568 | tf_op jit(solution)/shard_map/ppermute | solution.py:487
  112.4 0.1 add_convert_fusion.3
  112.7 6.6 %collective-permute-done.14 = bf16[4,480,128]{2,1,0:T(8,128)(2,1)S(1)} collective-permute-done((bf16[4,480,128]{2,1,0:T(8,128)(2,1)S(1)}, bf16[4,480,128]{2,1,0:T(8,128)(2,1)S(1)}, u32[]{:S(2)}, u32[]{:S(2)}) %collective-permute-start.14) | collective-permute-done | bytes 491552 | tf_op jit(solution)/shard_map/ppermute | solution.py:487
  119.2 0.1 add_convert_fusion
  119.4 3.0 %collective-permute-start.15 = (bf16[4,480,128]{2,1,0:T(8,128)(2,1)S(1)}, bf16[4,480,128]{2,1,0:T(8,128)(2,1)S(1)}, u32[]{:S(2)}, u32[]{:S(2)}) collective-permute-start(bf16[4,480,128]{2,1,0:T(8,128)(2,1)S(1)} %add_convert_fusion), channel_id=1, source_target_pairs={{0,7},{1,0},{2,1},{3,2},{4,3},{5,4},{6,5},{7,6},{8,15},{9,8},{10,9... | collective-permute-start | bytes 1474568 | tf_op jit(solution)/shard_map/ppermute | solution.py:487
  122.3 0.9 add_convert_fusion.2
  123.3 13.3 %all-to-all-start.1 = ((bf16[32,16,256]{2,1,0:T(8,128)(2,1)}), bf16[32,16,256]{2,1,0:T(8,128)(2,1)S(1)}, u32[]{:S(2)}, u32[]{:S(2)}) async-start(bf16[32,16,256]{2,1,0:T(8,128)(2,1)} %get-tuple-element.33), calls=%async_computation.1 | async-start | bytes 524288 | tf_op jit(solution)/shard_map/all_to_all | solution.py:479
  136.6 0.7 copy-done.8
  137.4 0.2 copy-done.9
  137.5 3.8 %finish_rows.1 = bf16[768,320]{1,0:T(8,128)(2,1)} custom-call(s32[1]{0:T(128)} %bitcast.parity.me, bf16[4,480,128]{2,1,0:T(8,128)(2,1)} %get-tuple-element.23.own_ref, bf16[4,480,128]{2,1,0:T(8,128)(2,1)} %copy-done.9, bf16[4,480,128]{2,1,0:T(8,128)(2,1)} %copy-done.8, bf16[768,320]{1,0:T(8,128)(2,1)} %bitcast.10), custom_call_target="tpu_custom_call" | custom-call | tf_op jit(solution)/shard_map/finish_rows/pallas_call | solution.py:110
  141.4 4.2 %all-to-all-done.1.extra_ref = bf16[32,16,256]{2,1,0:T(8,128)(2,1)S(1)} async-done(((bf16[32,16,256]{2,1,0:T(8,128)(2,1)}), bf16[32,16,256]{2,1,0:T(8,128)(2,1)S(1)}, u32[]{:S(2)}, u32[]{:S(2)}) %all-to-all-start.1) | async-done | bytes 262176 | tf_op jit(solution)/shard_map/all_to_all | solution.py:479
  145.6 0.7 copy-done.1
  146.3 8.4 %assemble_cache.1 = bf16[32,160,512]{2,1,0:T(8,128)(2,1)} custom-call(bf16[32,160,512]{2,1,0:T(8,128)(2,1)} %all-to-all-done.cache_ref, bf16[32,16,256]{2,1,0:T(8,128)(2,1)} %copy-done.1), custom_call_target="tpu_custom_call" | custom-call | tf_op jit(solution)/shard_map/assemble_cache/pallas_call | solution.py:462
  (65 shorter events, 0.6 us)
Async XLA Ops:
  0.6 42.1 %copy-start = (bf16[2560,320]{0,1:T(8,128)(2,1)S(1)}, bf16[2560,320]{0,1:T(8,128)(2,1)}, u32[]{:S(2)}) copy-start(bf16[2560,320]{0,1:T(8,128)(2,1)} %param.12) | copy-start | bytes 4915204
  4.1 21.9 %collective-permute-start.3 = (bf16[4,480,128]{2,1,0:T(8,128)(2,1)}, bf16[4,480,128]{2,1,0:T(8,128)(2,1)S(1)}, u32[]{:S(2)}, u32[]{:S(2)}) collective-permute-start(bf16[4,480,128]{2,1,0:T(8,128)(2,1)} %pack_rows.1.refs_0_), channel_id=1, source_target_pairs={{0,1},{1,2},{2,3},{3,4},{4,5},{5,6},{6,7},{7,0},{8,9},{9,10},{10,1... | collective-permute-start | bytes 1474568 | tf_op jit(solution)/shard_map/ppermute | solution.py:483
  6.6 19.5 %collective-permute-start = (bf16[4,480,128]{2,1,0:T(8,128)(2,1)}, bf16[4,480,128]{2,1,0:T(8,128)(2,1)}, u32[]{:S(2)}, u32[]{:S(2)}) collective-permute-start(bf16[4,480,128]{2,1,0:T(8,128)(2,1)} %pack_rows.1.refs_0_), channel_id=1, source_target_pairs={{0,7},{1,0},{2,1},{3,2},{4,3},{5,4},{6,5},{7,6},{8,15},{9,8},{10,9... | collective-permute-start | bytes 1474568 | tf_op jit(solution)/shard_map/ppermute | solution.py:487
  11.2 6.5 %copy-start.20 = (s32[32]{0:T(128)}, s32[32]{0:T(128)S(1)}, u32[]{:S(2)}) copy-start(s32[32]{0:T(128)S(1)} %and_select_fusion.2.destination) | copy-start | bytes 388
  17.8 11.1 %copy-start.2 = (bf16[160,2560]{1,0:T(8,128)(2,1)S(1)}, bf16[160,2560]{1,0:T(8,128)(2,1)}, u32[]{:S(2)}) copy-start(bf16[160,2560]{1,0:T(8,128)(2,1)} %param.13) | copy-start | bytes 2457604
  17.8 11.1 %copy-start.12 = (f32[2560]{0:T(1024)S(1)}, f32[2560]{0:T(1024)}, u32[]{:S(2)}) copy-start(f32[2560]{0:T(1024)} %param.11) | copy-start | bytes 30724
  17.8 105.5 %all-to-all-start = ((bf16[32,160,512]{2,1,0:T(8,128)(2,1)}), bf16[32,160,512]{2,1,0:T(8,128)(2,1)}, u32[]{:S(2)}, u32[]{:S(2)}) async-start(bf16[32,160,512]{2,1,0:T(8,128)(2,1)} %order_cache.1), calls=%async_computation | async-start | bytes 10485760 | tf_op jit(solution)/shard_map/all_to_all | solution.py:479
  26.0 4.8 %copy-start.15 = (bf16[4,480,128]{2,1,0:T(8,128)(2,1)}, bf16[4,480,128]{2,1,0:T(8,128)(2,1)S(1)}, u32[]{:S(2)}) copy-start(bf16[4,480,128]{2,1,0:T(8,128)(2,1)S(1)} %collective-permute-done.3.refs_7_) | copy-start | bytes 1474564
  26.0 13.9 %collective-permute-start.4 = (bf16[4,480,128]{2,1,0:T(8,128)(2,1)S(1)}, bf16[4,480,128]{2,1,0:T(8,128)(2,1)S(1)}, u32[]{:S(2)}, u32[]{:S(2)}) collective-permute-start(bf16[4,480,128]{2,1,0:T(8,128)(2,1)S(1)} %collective-permute-done.3.refs_7_), channel_id=1, source_target_pairs={{0,1},{1,2},{2,3},{3,4},{4,5},{5,6},{6,7},{7,0},{8,9},{9,10},{10,1... | collective-permute-start | bytes 1474568 | tf_op jit(solution)/shard_map/ppermute | solution.py:483
  26.1 13.8 %collective-permute-start.1 = (bf16[4,480,128]{2,1,0:T(8,128)(2,1)}, bf16[4,480,128]{2,1,0:T(8,128)(2,1)S(1)}, u32[]{:S(2)}, u32[]{:S(2)}) collective-permute-start(bf16[4,480,128]{2,1,0:T(8,128)(2,1)} %collective-permute-done.refs_1_), channel_id=1, source_target_pairs={{0,7},{1,0},{2,1},{3,2},{4,3},{5,4},{6,5},{7,6},{8,15},{9,8},{10,9... | collective-permute-start | bytes 1474568 | tf_op jit(solution)/shard_map/ppermute | solution.py:487
  40.0 6.0 %copy-start.16 = (bf16[4,480,128]{2,1,0:T(8,128)(2,1)}, bf16[4,480,128]{2,1,0:T(8,128)(2,1)S(1)}, u32[]{:S(2)}) copy-start(bf16[4,480,128]{2,1,0:T(8,128)(2,1)S(1)} %collective-permute-done.4.refs_6_) | copy-start | bytes 1474564
  40.0 13.0 %collective-permute-start.5 = (bf16[4,480,128]{2,1,0:T(8,128)(2,1)S(1)}, bf16[4,480,128]{2,1,0:T(8,128)(2,1)S(1)}, u32[]{:S(2)}, u32[]{:S(2)}) collective-permute-start(bf16[4,480,128]{2,1,0:T(8,128)(2,1)S(1)} %collective-permute-done.4.refs_6_), channel_id=1, source_target_pairs={{0,1},{1,2},{2,3},{3,4},{4,5},{5,6},{6,7},{7,0},{8,9},{9,10},{10,1... | collective-permute-start | bytes 1474568 | tf_op jit(solution)/shard_map/ppermute | solution.py:483
  40.0 6.0 %copy-start.17 = (bf16[4,480,128]{2,1,0:T(8,128)(2,1)}, bf16[4,480,128]{2,1,0:T(8,128)(2,1)S(1)}, u32[]{:S(2)}) copy-start(bf16[4,480,128]{2,1,0:T(8,128)(2,1)S(1)} %collective-permute-done.1.refs_2_) | copy-start | bytes 1474564
  40.0 13.1 %collective-permute-start.2 = (bf16[4,480,128]{2,1,0:T(8,128)(2,1)S(1)}, bf16[4,480,128]{2,1,0:T(8,128)(2,1)S(1)}, u32[]{:S(2)}, u32[]{:S(2)}) collective-permute-start(bf16[4,480,128]{2,1,0:T(8,128)(2,1)S(1)} %collective-permute-done.1.refs_2_), channel_id=1, source_target_pairs={{0,7},{1,0},{2,1},{3,2},{4,3},{5,4},{6,5},{7,6},{8,15},{9,8},{10,9... | collective-permute-start | bytes 1474568 | tf_op jit(solution)/shard_map/ppermute | solution.py:487
  42.7 13.3 %copy-start.19 = (s32[32]{0:T(128)S(1)}, s32[32]{0:T(128)}, u32[]{:S(2)}) copy-start(s32[32]{0:T(128)} %lengths.1) | copy-start | bytes 388
  42.7 13.3 %copy-start.13 = (s32[32,24]{0,1:T(8,128)S(1)}, s32[32,24]{0,1:T(8,128)}, u32[]{:S(2)}) copy-start(s32[32,24]{0,1:T(8,128)} %param.17) | copy-start | bytes 9220
  42.7 14.0 %copy-start.14 = (s32[32,4]{0,1:T(4,128)S(1)}, s32[32,4]{0,1:T(4,128)}, u32[]{:S(2)}) copy-start(s32[32,4]{0,1:T(4,128)} %param.18) | copy-start | bytes 1540
  53.0 11.0 %copy-start.10 = (bf16[4,480,128]{2,1,0:T(8,128)(2,1)}, bf16[4,480,128]{2,1,0:T(8,128)(2,1)S(1)}, u32[]{:S(2)}) copy-start(bf16[4,480,128]{2,1,0:T(8,128)(2,1)S(1)} %collective-permute-done.5.refs_5_) | copy-start | bytes 1474564
  53.0 14.4 %collective-permute-start.6 = (bf16[2,480,128]{2,1,0:T(8,128)(2,1)S(1)}, bf16[2,480,128]{2,1,0:T(8,128)(2,1)S(1)}, u32[]{:S(2)}, u32[]{:S(2)}) collective-permute-start(bf16[2,480,128]{2,1,0:T(8,128)(2,1)S(1)} %slice.32), channel_id=1, source_target_pairs={{0,1},{1,2},{2,3},{3,4},{4,5},{5,6},{6,7},{7,0},{8,9},{9,10},{10,1... | collective-permute-start | bytes 737288 | tf_op jit(solution)/shard_map/ppermute | solution.py:483
  53.1 10.9 %copy-start.11 = (bf16[4,480,128]{2,1,0:T(8,128)(2,1)}, bf16[4,480,128]{2,1,0:T(8,128)(2,1)S(1)}, u32[]{:S(2)}) copy-start(bf16[4,480,128]{2,1,0:T(8,128)(2,1)S(1)} %collective-permute-done.2.refs_3_) | copy-start | bytes 1474564
  53.1 14.2 %collective-permute-start.7 = (bf16[2,480,128]{2,1,0:T(8,128)(2,1)S(1)}, bf16[2,480,128]{2,1,0:T(8,128)(2,1)}, u32[]{:S(2)}, u32[]{:S(2)}) collective-permute-start(bf16[2,480,128]{2,1,0:T(8,128)(2,1)S(1)} %slice.33), channel_id=1, source_target_pairs={{0,7},{1,0},{2,1},{3,2},{4,3},{5,4},{6,5},{7,6},{8,15},{9,8},{10,9... | collective-permute-start | bytes 737288 | tf_op jit(solution)/shard_map/ppermute | solution.py:487
  67.4 0.7 copy-start.18
  92.9 8.7 %copy-start.7 = (bf16[4,480,128]{2,1,0:T(8,128)(2,1)S(1)}, bf16[4,480,128]{2,1,0:T(8,128)(2,1)}, u32[]{:S(2)}) copy-start(bf16[4,480,128]{2,1,0:T(8,128)(2,1)} %get-tuple-element.26) | copy-start | bytes 1474564
  92.9 16.6 %copy-start.6 = (bf16[4,480,128]{2,1,0:T(8,128)(2,1)S(1)}, bf16[4,480,128]{2,1,0:T(8,128)(2,1)}, u32[]{:S(2)}) copy-start(bf16[4,480,128]{2,1,0:T(8,128)(2,1)} %get-tuple-element.29) | copy-start | bytes 1474564
  94.1 5.1 %collective-permute-start.12 = (bf16[2,480,128]{2,1,0:T(8,128)(2,1)S(1)}, bf16[2,480,128]{2,1,0:T(8,128)(2,1)S(1)}, u32[]{:S(2)}, u32[]{:S(2)}) collective-permute-start(bf16[2,480,128]{2,1,0:T(8,128)(2,1)S(1)} %get-tuple-element.34), channel_id=1, source_target_pairs={{0,7},{1,0},{2,1},{3,2},{4,3},{5,4},{6,5},{7,6},{8,15},{9,8},{10,9... | collective-permute-start | bytes 737288 | tf_op jit(solution)/shard_map/ppermute | solution.py:487
  95.2 6.5 %collective-permute-start.8 = (bf16[2,480,128]{2,1,0:T(8,128)(2,1)S(1)}, bf16[2,480,128]{2,1,0:T(8,128)(2,1)S(1)}, u32[]{:S(2)}, u32[]{:S(2)}) collective-permute-start(bf16[2,480,128]{2,1,0:T(8,128)(2,1)S(1)} %get-tuple-element.35), channel_id=1, source_target_pairs={{0,1},{1,2},{2,3},{3,4},{4,5},{5,6},{6,7},{7,0},{8,9},{9,10},{10,1... | collective-permute-start | bytes 737288 | tf_op jit(solution)/shard_map/ppermute | solution.py:483
  96.7 15.8 %copy-start.5 = (bf16[4,480,128]{2,1,0:T(8,128)(2,1)S(1)}, bf16[4,480,128]{2,1,0:T(8,128)(2,1)}, u32[]{:S(2)}) copy-start(bf16[4,480,128]{2,1,0:T(8,128)(2,1)} %get-tuple-element.25) | copy-start | bytes 1474564
  100.2 19.0 %copy-start.4 = (bf16[4,480,128]{2,1,0:T(8,128)(2,1)S(1)}, bf16[4,480,128]{2,1,0:T(8,128)(2,1)}, u32[]{:S(2)}) copy-start(bf16[4,480,128]{2,1,0:T(8,128)(2,1)} %get-tuple-element.28) | copy-start | bytes 1474564
  100.3 9.2 %collective-permute-start.13 = (bf16[4,480,128]{2,1,0:T(8,128)(2,1)S(1)}, bf16[4,480,128]{2,1,0:T(8,128)(2,1)S(1)}, u32[]{:S(2)}, u32[]{:S(2)}) collective-permute-start(bf16[4,480,128]{2,1,0:T(8,128)(2,1)S(1)} %pad_maximum_fusion.1), channel_id=1, source_target_pairs={{0,7},{1,0},{2,1},{3,2},{4,3},{5,4},{6,5},{7,6},{8,15},{9,8},{10,9... | collective-permute-start | bytes 1474568 | tf_op jit(solution)/shard_map/ppermute | solution.py:487
  101.7 20.6 %copy-start.3 = (bf16[4,480,128]{2,1,0:T(8,128)(2,1)S(1)}, bf16[4,480,128]{2,1,0:T(8,128)(2,1)}, u32[]{:S(2)}) copy-start(bf16[4,480,128]{2,1,0:T(8,128)(2,1)} %get-tuple-element.24) | copy-start | bytes 1474564
  101.8 10.7 %collective-permute-start.9 = (bf16[4,480,128]{2,1,0:T(8,128)(2,1)S(1)}, bf16[4,480,128]{2,1,0:T(8,128)(2,1)S(1)}, u32[]{:S(2)}, u32[]{:S(2)}) collective-permute-start(bf16[4,480,128]{2,1,0:T(8,128)(2,1)S(1)} %pad_maximum_fusion), channel_id=1, source_target_pairs={{0,1},{1,2},{2,3},{3,4},{4,5},{5,6},{6,7},{7,0},{8,9},{9,10},{10,1... | collective-permute-start | bytes 1474568 | tf_op jit(solution)/shard_map/ppermute | solution.py:483
  109.7 9.5 %collective-permute-start.14 = (bf16[4,480,128]{2,1,0:T(8,128)(2,1)S(1)}, bf16[4,480,128]{2,1,0:T(8,128)(2,1)S(1)}, u32[]{:S(2)}, u32[]{:S(2)}) collective-permute-start(bf16[4,480,128]{2,1,0:T(8,128)(2,1)S(1)} %add_convert_fusion.1), channel_id=1, source_target_pairs={{0,7},{1,0},{2,1},{3,2},{4,3},{5,4},{6,5},{7,6},{8,15},{9,8},{10,9... | collective-permute-start | bytes 1474568 | tf_op jit(solution)/shard_map/ppermute | solution.py:487
  112.6 9.8 %collective-permute-start.10 = (bf16[4,480,128]{2,1,0:T(8,128)(2,1)S(1)}, bf16[4,480,128]{2,1,0:T(8,128)(2,1)S(1)}, u32[]{:S(2)}, u32[]{:S(2)}) collective-permute-start(bf16[4,480,128]{2,1,0:T(8,128)(2,1)S(1)} %add_convert_fusion.3), channel_id=1, source_target_pairs={{0,1},{1,2},{2,3},{3,4},{4,5},{5,6},{6,7},{7,0},{8,9},{9,10},{10,1... | collective-permute-start | bytes 1474568 | tf_op jit(solution)/shard_map/ppermute | solution.py:483
  119.4 17.2 %collective-permute-start.15 = (bf16[4,480,128]{2,1,0:T(8,128)(2,1)S(1)}, bf16[4,480,128]{2,1,0:T(8,128)(2,1)S(1)}, u32[]{:S(2)}, u32[]{:S(2)}) collective-permute-start(bf16[4,480,128]{2,1,0:T(8,128)(2,1)S(1)} %add_convert_fusion), channel_id=1, source_target_pairs={{0,7},{1,0},{2,1},{3,2},{4,3},{5,4},{6,5},{7,6},{8,15},{9,8},{10,9... | collective-permute-start | bytes 1474568 | tf_op jit(solution)/shard_map/ppermute | solution.py:487
  123.2 13.4 %collective-permute-start.11 = (bf16[4,480,128]{2,1,0:T(8,128)(2,1)}, bf16[4,480,128]{2,1,0:T(8,128)(2,1)S(1)}, u32[]{:S(2)}, u32[]{:S(2)}) collective-permute-start(bf16[4,480,128]{2,1,0:T(8,128)(2,1)} %add_convert_fusion.2), channel_id=1, source_target_pairs={{0,1},{1,2},{2,3},{3,4},{4,5},{5,6},{6,7},{7,0},{8,9},{9,10},{10,1... | collective-permute-start | bytes 1474568 | tf_op jit(solution)/shard_map/ppermute | solution.py:483
  123.3 22.3 %all-to-all-start.1 = ((bf16[32,16,256]{2,1,0:T(8,128)(2,1)}), bf16[32,16,256]{2,1,0:T(8,128)(2,1)S(1)}, u32[]{:S(2)}, u32[]{:S(2)}) async-start(bf16[32,16,256]{2,1,0:T(8,128)(2,1)} %get-tuple-element.33), calls=%async_computation.1 | async-start | bytes 524288 | tf_op jit(solution)/shard_map/all_to_all | solution.py:479
  136.6 0.8 copy-start.8
  136.6 0.9 copy-start.9
  145.6 0.7 copy-start.1

commit v5 on v4

--- a/solution.py
+++ b/solution.py
@@ -39,6 +39,11 @@
 
 
 def pack_kernel(parity, x_ref, o_ref):
+    for i in range(HALF_BLOCKS):
+        pack_block(parity, x_ref.at[pl.ds(i * ROWS, ROWS)], o_ref.at[pl.ds(i, 1)])
+
+
+def pack_block(parity, x_ref, o_ref):
     x = x_ref[...].astype(F32)
     t0 = x[:, 0:128]
     t1 = x[:, 128:256]
@@ -70,15 +75,29 @@
         out_shape=jax.ShapeDtypeStruct((blocks, PACKED, LANES), BF),
         grid_spec=pltpu.PrefetchScalarGridSpec(
             num_scalar_prefetch=1,
-            grid=(blocks,),
-            in_specs=[pl.BlockSpec((ROWS, WIDTH), lambda b, p: (b, 0))],
-            out_specs=pl.BlockSpec((1, PACKED, LANES), lambda b, p: (b, 0, 0)),
+            grid=(blocks // HALF_BLOCKS,),
+            in_specs=[pl.BlockSpec((HALF_BLOCKS * ROWS, WIDTH), lambda b, p: (b, 0))],
+            out_specs=pl.BlockSpec((HALF_BLOCKS, PACKED, LANES), lambda b, p: (b, 0, 0)),
         ),
         name="pack_rows",
     )(parity, rows)
 
 
 def finish_kernel(parity, own_ref, up_ref, down_ref, x_ref, o_ref):
+    for i in range(HALF_BLOCKS):
+        block = pl.ds(i, 1)
+        flat = pl.ds(i * ROWS, ROWS)
+        finish_block(
+            parity,
+            own_ref.at[block],
+            up_ref.at[block],
+            down_ref.at[block],
+            x_ref.at[flat],
+            o_ref.at[flat],
+        )
+
+
+def finish_block(parity, own_ref, up_ref, down_ref, x_ref, o_ref):
     packed = (
         own_ref[0].astype(F32) + up_ref[0].astype(F32) + down_ref[0].astype(F32)
     )
@@ -105,14 +124,14 @@
 
 def finish_rows(own, up, down, rows, parity):
     blocks = rows.shape[0] // ROWS
-    packed = pl.BlockSpec((1, PACKED, LANES), lambda b, p: (b, 0, 0))
-    flat = pl.BlockSpec((ROWS, WIDTH), lambda b, p: (b, 0))
+    packed = pl.BlockSpec((HALF_BLOCKS, PACKED, LANES), lambda b, p: (b, 0, 0))
+    flat = pl.BlockSpec((HALF_BLOCKS * ROWS, WIDTH), lambda b, p: (b, 0))
     return pl.pallas_call(
         finish_kernel,
         out_shape=jax.ShapeDtypeStruct(rows.shape, BF),
         grid_spec=pltpu.PrefetchScalarGridSpec(
             num_scalar_prefetch=1,
-            grid=(blocks,),
+            grid=(blocks // HALF_BLOCKS,),
             in_specs=[packed, packed, packed, flat],
             out_specs=flat,
         ),
@@ -257,8 +276,8 @@
 def layer_kernel(lengths, accepted, destination, *refs):
     x_refs = refs[: N_TP + 1]
     w_ref, wo_ref, cache_ref, bias_ref, cos_ref, sin_ref = refs[N_TP + 1 : N_TP + 7]
-    out_refs = refs[N_TP + 7 : 2 * N_TP + 7]
-    extra_out, xs, qkv, ctx, extra, sems = refs[2 * N_TP + 7 :]
+    out_refs = refs[N_TP + 7 : 2 * N_TP + 8]
+    extra_out, xs, qkv, ctx, extra, sems = refs[2 * N_TP + 8 :]
     b = pl.program_id(0)
 
     @pl.when(b == 0)
@@ -271,6 +290,20 @@
         if k == N_TP // 2:
             piece = jnp.where(b < HALF_BLOCKS, piece, x_refs[N_TP][0, first:last])
         return piece
+
+    def deliver(k, first, last, values):
+        values = values.astype(BF)
+        if k != N_TP // 2:
+            out_refs[k][0, first:last] = values
+            return
+
+        @pl.when(b < HALF_BLOCKS)
+        def _():
+            out_refs[k][0, first:last] = values
+
+        @pl.when(b >= HALF_BLOCKS)
+        def _():
+            out_refs[N_TP][0, first:last] = values
 
     low_half = lane_index((HALF, LANES)) < 64
     squares = jnp.zeros((ROWS, LANES), F32)
@@ -374,18 +407,14 @@
     partial = jnp.dot(ctx[...].astype(BF), wo_ref[...], preferred_element_type=F32)
     for j in range(N_TP // 2):
         base = j * 5 * LANES
-        for device, at in ((2 * j, base), (2 * j + 1, base + 3 * LANES)):
+        for k, at in ((2 * j, base), (2 * j + 1, base + 3 * LANES)):
             for part in range(2):
-                out_refs[device][0, part * ROWS : (part + 1) * ROWS] = partial[
-                    :, at + part * LANES : at + (part + 1) * LANES
-                ].astype(BF)
+                tile = partial[:, at + part * LANES : at + (part + 1) * LANES]
+                deliver(k, part * ROWS, (part + 1) * ROWS, tile)
         tail = partial[:, base + 2 * LANES : base + 3 * LANES]
-        out_refs[2 * j][0, 2 * ROWS : PACKED] = jnp.where(
-            low_half, tail[:HALF], swap_halves(tail[HALF:])
-        ).astype(BF)
-        out_refs[2 * j + 1][0, 2 * ROWS : PACKED] = jnp.where(
-            low_half, swap_halves(tail[:HALF]), tail[HALF:]
-        ).astype(BF)
+        top, bottom = tail[:HALF], tail[HALF:]
+        deliver(2 * j, 2 * ROWS, PACKED, jnp.where(low_half, top, swap_halves(bottom)))
+        deliver(2 * j + 1, 2 * ROWS, PACKED, jnp.where(low_half, swap_halves(top), bottom))
     for copy in copies:
         copy.wait()
 
@@ -405,7 +434,12 @@
     )
     return pl.pallas_call(
         layer_kernel,
-        out_shape=[jax.ShapeDtypeStruct((blocks, PACKED, LANES), BF)] * N_TP
+        out_shape=[
+            jax.ShapeDtypeStruct(
+                (HALF_BLOCKS if k % (N_TP // 2) == 0 and k > 0 else blocks, PACKED, LANES), BF
+            )
+            for k in range(N_TP + 1)
+        ]
         + [jax.ShapeDtypeStruct((held, EXTRA, 2 * LANES), BF)],
         grid_spec=pltpu.PrefetchScalarGridSpec(
             num_scalar_prefetch=3,
@@ -419,7 +453,7 @@
                 table,
                 table,
             ],
-            out_specs=[packed] * N_TP + [pl.BlockSpec(memory_space=pl.ANY)],
+            out_specs=in_specs + [pl.BlockSpec(memory_space=pl.ANY)],
             scratch_shapes=[
                 pltpu.VMEM((ROWS, D), BF),
                 pltpu.VMEM((ROWS, (GROUP + 2) * LANES), F32),
@@ -491,33 +525,58 @@
     return (a.astype(F32) + b.astype(F32)).astype(BF)
 
 
-def gather_ring(packed):
+def gather_ring(packed, weights, tables):
     parts = [packed] * (N_TP + 1)
-    from_below = from_above = packed
+    from_below = go_up(packed)
+    from_above = go_down(packed)
     for step in range(1, N_TP // 2):
+        parts[N_TP - step] = from_below
+        parts[step] = from_above
+        if step == 2:
+            from_below, from_above, weights = lax.optimization_barrier(
+                (from_below, from_above, weights)
+            )
+        if step == 3:
+            from_below, from_above, tables = lax.optimization_barrier(
+                (from_below, from_above, tables)
+            )
+            from_below = from_below[:HALF_BLOCKS]
+            from_above = from_above[HALF_BLOCKS:]
         from_below = go_up(from_below)
         from_above = go_down(from_above)
-        parts[N_TP - step] = from_below
-        parts[step] = from_above
-    parts[N_TP // 2] = go_up(from_below[:HALF_BLOCKS])
-    parts[N_TP] = go_down(from_above[HALF_BLOCKS:])
-    return parts
-
-
-def scatter_ring(targets):
+    parts[N_TP // 2] = from_below
+    parts[N_TP] = from_above
+    return parts, weights, tables
+
+
+def add_blocks(values, more, first):
+    picked = values[first : first + HALF_BLOCKS]
+    return lax.dynamic_update_slice(values, add_up(picked, more), (first, 0, 0))
+
+
+def scatter_ring(targets, cached, extra):
     half = N_TP // 2
-    up = go_up(targets[half][:HALF_BLOCKS])
-    down = go_down(targets[half][HALF_BLOCKS:])
+    up = go_up(targets[half])
+    down = go_down(targets[N_TP])
     for step in range(1, half):
         above, below = targets[half - step], targets[half + step]
         if step == 1:
-            above = jnp.concatenate([add_up(above[:HALF_BLOCKS], up), above[HALF_BLOCKS:]])
-            below = jnp.concatenate([below[:HALF_BLOCKS], add_up(below[HALF_BLOCKS:], down)])
+            above = add_blocks(above, up, 0)
+            below = add_blocks(below, down, HALF_BLOCKS)
         else:
             above, below = add_up(above, up), add_up(below, down)
+        if step == 2:
+            above, below, cached, extra = lax.optimization_barrier(
+                (above, below, cached, extra)
+            )
+            extra = exchange(extra)
+        if step == 3:
+            above, below, extra = lax.optimization_barrier((above, below, extra))
+            new_cache = assemble_cache(cached, extra)
         up = go_up(above)
         down = go_down(below)
-    return up, down
+    up, down, new_cache = lax.optimization_barrier((up, down, new_cache))
+    return up, down, new_cache
 
 
 def per_device(
@@ -526,7 +585,7 @@
     held = hidden.shape[0]
     rows = hidden.reshape(held * TREE, WIDTH)
     me = lax.axis_index("tp").astype(jnp.int32).reshape(1)
-    parts = gather_ring(pack_rows(rows, me))
+    packed = pack_rows(rows, me)
 
     destination = slot_of // held
     peer_index = jnp.arange(held, dtype=jnp.int32)
@@ -541,14 +600,15 @@
         w_keyval, spread_heads(2), (((0,), (0,)), ((), ())), preferred_element_type=F32
     )
     wkv = (wkv * gain).astype(BF)
-    w, wo = arrange_weights(wq, wkv, w_out, me)
+    weights = arrange_weights(wq, wkv, w_out, me)
+    parts, weights, (tables, picks) = gather_ring(
+        packed, weights, (tables, accepted.reshape(-1))
+    )
 
     *targets, extra = verify_layer(
-        parts, w, wo, kv_cache, tables, lengths, accepted.reshape(-1), destination
-    )
-    cached, extra = lax.optimization_barrier((cached, extra))
-    new_cache = assemble_cache(cached, exchange(extra))
-    up, down = scatter_ring(targets)
+        parts, *weights, kv_cache, tables, lengths, picks, destination
+    )
+    up, down, new_cache = scatter_ring(targets, cached, extra)
     out_rows = finish_rows(targets[0], up, down, rows, me)
     return (out_rows.reshape(hidden.shape), new_cache)
 

time: 155 us -> 150 us (0.968)
  other arithmetic: 4.7 us -> 10.8 us
  waiting for transfers between devices: 36 us -> 30.4 us
  local copies, waits for them, and re-layouts: 7.55 us -> 4.09 us
  Pallas kernels: 54.9 us -> 52.9 us
    ppermute x8, waiting for transfers between devices: 15.6 us -> 8.88 us  [go_down(): lax.ppermute(values, 'tp', [(i, (i - 1) % N_TP) for i in range(N_TP)])]
    dynamic_update_slice x0 -> x2, other arithmetic: none -> 3.43 us  [add_blocks(): return lax.dynamic_update_slice(values, add_up(picked, more), (first, 0, 0))]
    slice x5 -> x2, local copies, waits for them, and re-layouts: 3.19 us -> 0.03 us  [the longest x1 0.02 us: gather_ring(): from_below = from_below[:HALF_BLOCKS]]
    convert_element_type x6 -> x4, other arithmetic: 2.38 us -> 5.16 us  [add_up(): return (a.astype(F32) + b.astype(F32)).astype(BF)]
    all_to_all x2, waiting for transfers between devices: 4.23 us -> 5.85 us  [exchange(): lax.all_to_all(values, 'req', split_axis=0, concat_axis=0, tiled=True)]
    unnamed x44 -> x38, local copies, waits for them, and re-layouts: 3.17 us -> 2.79 us
  transfers between devices with their start and end apart: 18 -> 18, of which waited for: 6 -> 8; matrix products, arithmetic and copies ran while one was open for 10% -> 12% of each run, Pallas kernels for 28% -> 32%
where the time goes in v5:
time: 150 us; the launch traced here: 149 us
  Pallas kernels  52.9 us (35%)
  starting transfers between devices  45.4 us (30%)
  waiting for transfers between devices  30.4 us (20%)
  other arithmetic  10.8 us (7%)
  matrix products  5.15 us (3%)
  local copies, waits for them, and re-layouts  4.09 us (3%)
    pallas_call x1, Pallas kernels, verify_layer(): pl.pallas_call(layer_kernel, out_shape=[jax.ShapeDtypeStruct((HALF_BLOCKS...  25.3 us
    all_to_all x2, starting transfers between devices, exchange(): lax.all_to_all(values, 'req', split_axis=0, concat_axis=0, tiled=True)  21.1 us
    ppermute x8, starting transfers between devices, go_down(): lax.ppermute(values, 'tp', [(i, (i - 1) % N_TP) for i in range(N_TP)])  18.3 us
    ppermute x8, waiting for transfers between devices, go_up(): lax.ppermute(values, 'tp', [(i, (i + 1) % N_TP) for i in range(N_TP)])  15.7 us
    ppermute x8, waiting for transfers between devices, go_down(): lax.ppermute(values, 'tp', [(i, (i - 1) % N_TP) for i in range(N_TP)])  8.88 us
    pallas_call x1, Pallas kernels, assemble_cache(): pl.pallas_call(assemble_kernel, out_shape=jax.ShapeDtypeStruct(cached.sha...  8.38 us
    pallas_call x1, Pallas kernels, arrange_weights(): pl.pallas_call(arrange_kernel, out_shape=(jax.ShapeDtypeStruct((D, (GROUP...  6.02 us
    ppermute x8, starting transfers between devices, go_up(): lax.ppermute(values, 'tp', [(i, (i + 1) % N_TP) for i in range(N_TP)])  5.94 us
  transfers between devices with their start and end apart: 18, of which 8 were waited for; matrix products, arithmetic and copies ran while one was open for 12% of the time, Pallas kernels for 32%

profile of v5, /device:TPU:1, one launch (start us, length us, event | category | flops | bytes accessed | tf_op | source)
XLA Modules:
  0.0 149.5 jit_solution(16319317772178010172)
XLA Ops:
  0.6 2.1 %pack_rows.1.refs_0_ = bf16[4,480,128]{2,1,0:T(8,128)(2,1)} custom-call(s32[1]{0:T(128)} %bitcast.parity.me, bf16[768,320]{1,0:T(8,128)(2,1)} %bitcast.9), custom_call_target="tpu_custom_call" | custom-call | tf_op jit(solution)/shard_map/pack_rows/pallas_call | solution.py:73
  2.8 2.6 %collective-permute-start = (bf16[4,480,128]{2,1,0:T(8,128)(2,1)}, bf16[4,480,128]{2,1,0:T(8,128)(2,1)S(1)}, u32[]{:S(2)}, u32[]{:S(2)}) collective-permute-start(bf16[4,480,128]{2,1,0:T(8,128)(2,1)} %pack_rows.1.refs_0_), channel_id=1, source_target_pairs={{0,1},{1,2},{2,3},{3,4},{4,5},{5,6},{6,7},{7,0},{8,9},{9,10},{10,1... | collective-permute-start | bytes 1474568 | tf_op jit(solution)/shard_map/ppermute | solution.py:517
  5.4 3.9 %collective-permute-start.2 = (bf16[4,480,128]{2,1,0:T(8,128)(2,1)}, bf16[4,480,128]{2,1,0:T(8,128)(2,1)}, u32[]{:S(2)}, u32[]{:S(2)}) collective-permute-start(bf16[4,480,128]{2,1,0:T(8,128)(2,1)} %pack_rows.1.refs_0_), channel_id=1, source_target_pairs={{0,7},{1,0},{2,1},{3,2},{4,3},{5,4},{6,5},{7,6},{8,15},{9,8},{10,9... | collective-permute-start | bytes 1474568 | tf_op jit(solution)/shard_map/ppermute | solution.py:521
  9.3 0.7 and_select_fusion.destination
  10.0 0.6 select_reduce_fusion.order
  10.6 5.8 %order_cache.1 = bf16[32,160,512]{2,1,0:T(8,128)(2,1)} custom-call(s32[32]{0:T(128)} %select_reduce_fusion.order, bf16[32,160,512]{2,1,0:T(8,128)(2,1)} %cache_ref.1), custom_call_target="tpu_custom_call" | custom-call | tf_op jit(solution)/shard_map/order_cache/pallas_call | solution.py:257
  16.5 8.2 %all-to-all-start = ((bf16[32,160,512]{2,1,0:T(8,128)(2,1)}), bf16[32,160,512]{2,1,0:T(8,128)(2,1)}, u32[]{:S(2)}, u32[]{:S(2)}) async-start(bf16[32,160,512]{2,1,0:T(8,128)(2,1)} %order_cache.1), calls=%async_computation | async-start | bytes 10485760 | tf_op jit(solution)/shard_map/all_to_all | solution.py:513
  24.8 0.1 collective-permute-start.1
  24.9 2.7 %collective-permute-start.3 = (bf16[4,480,128]{2,1,0:T(8,128)(2,1)}, bf16[4,480,128]{2,1,0:T(8,128)(2,1)}, u32[]{:S(2)}, u32[]{:S(2)}) collective-permute-start(bf16[4,480,128]{2,1,0:T(8,128)(2,1)} %collective-permute-done.2.refs_1_), channel_id=1, source_target_pairs={{0,7},{1,0},{2,1},{3,2},{4,3},{5,4},{6,5},{7,6},{8,15},{9,8},{10,9... | collective-permute-start | bytes 1474568 | tf_op jit(solution)/shard_map/ppermute | solution.py:521
  27.5 2.0 %fusion.2.wkv_ref = bf16[2560,256]{1,0:T(8,128)(2,1)} fusion(bf16[160,2560]{1,0:T(8,128)(2,1)S(1)} %copy-done.2, f32[2560]{0:T(1024)S(1)} %copy-done.10, s32[160]{0:T(256)S(1)} %fusion.18), kind=kOutput, calls=%fused_computation.4 | convolution fusion | flops 211066880 | bytes 2140800 | tf_op jit(solution)/shard_map/dot_general | solution.py:599
  29.5 3.2 %fusion.wq_ref = bf16[2560,512]{1,0:T(8,128)(2,1)} fusion(bf16[2560,320]{0,1:T(8,128)(2,1)S(1)} %copy-done, f32[2560]{0:T(1024)S(1)} %copy-done.10, s32[320]{0:T(512)S(1)} %fusion.12), kind=kOutput, calls=%fused_computation.2 | convolution fusion | flops 841646080 | bytes 4271360 | tf_op jit(solution)/shard_map/dot_general | solution.py:598
  32.7 6.0 %arrange_weights.1 = (bf16[2560,768]{1,0:T(8,128)(2,1)}, bf16[512,2560]{1,0:T(8,128)(2,1)}) custom-call(s32[1]{0:T(128)} %bitcast.parity.me, bf16[2560,512]{1,0:T(8,128)(2,1)} %fusion.wq_ref, bf16[2560,256]{1,0:T(8,128)(2,1)} %fusion.2.wkv_ref, bf16[320,2560]{1,0:T(8,128)(2,1)} %wo_ref.1), custom_call_target="tpu_custom_call" | custom-call | tf_op jit(solution)/shard_map/arrange_weights/pallas_call | solution.py:182
  38.7 0.1 collective-permute-start.4
  38.8 2.7 %collective-permute-start.5 = (bf16[4,480,128]{2,1,0:T(8,128)(2,1)}, bf16[4,480,128]{2,1,0:T(8,128)(2,1)S(1)}, u32[]{:S(2)}, u32[]{:S(2)}) collective-permute-start(bf16[4,480,128]{2,1,0:T(8,128)(2,1)} %collective-permute-done.3.refs_2_), channel_id=1, source_target_pairs={{0,7},{1,0},{2,1},{3,2},{4,3},{5,4},{6,5},{7,6},{8,15},{9,8},{10,9... | collective-permute-start | bytes 1474568 | tf_op jit(solution)/shard_map/ppermute | solution.py:521
  41.6 0.7 copy.22.parents_ref
  42.3 0.1 copy.23
  42.3 0.6 reshape.147.accepted
  43.0 0.6 stack.2.step_ref
  43.7 0.7 multiply_sine_fusion
  44.4 2.6 %prepare_tables.1 = (f32[32,24,128]{2,1,0:T(8,128)}, f32[32,24,128]{2,1,0:T(8,128)}, f32[32,24,128]{2,1,0:T(8,128)}) custom-call(s32[32,24]{1,0:T(8,128)} %copy.22.parents_ref, f32[32,128]{1,0:T(8,128)} %get-tuple-element.73.cos_ref, f32[32,128]{1,0:T(8,128)} %get-tuple-element.72.sin_ref, f32[8,128]{1,0:T(8,128)} %stack.2.step_ref), custom_call_target="tpu_custom_call" | custom-call | tf_op jit(solution)/shard_map/prepare_tables/pallas_call | solution.py:235
  47.0 5.0 %collective-permute-done.4.refs_5_ = bf16[4,480,128]{2,1,0:T(8,128)(2,1)S(1)} collective-permute-done((bf16[4,480,128]{2,1,0:T(8,128)(2,1)}, bf16[4,480,128]{2,1,0:T(8,128)(2,1)S(1)}, u32[]{:S(2)}, u32[]{:S(2)}) %collective-permute-start.4) | collective-permute-done | bytes 491552 | tf_op jit(solution)/shard_map/ppermute | solution.py:517
  52.1 1.7 %collective-permute-start.6 = (bf16[2,480,128]{2,1,0:T(8,128)(2,1)S(1)}, bf16[2,480,128]{2,1,0:T(8,128)(2,1)S(1)}, u32[]{:S(2)}, u32[]{:S(2)}) collective-permute-start(bf16[2,480,128]{2,1,0:T(8,128)(2,1)S(1)} %slice.12), channel_id=1, source_target_pairs={{0,1},{1,2},{2,3},{3,4},{4,5},{5,6},{6,7},{7,0},{8,9},{9,10},{10,1... | collective-permute-start | bytes 737288 | tf_op jit(solution)/shard_map/ppermute | solution.py:517
  53.8 1.3 collective-permute-start.7
  55.1 4.0 %collective-permute-done.6.refs_4_ = bf16[2,480,128]{2,1,0:T(8,128)(2,1)S(1)} collective-permute-done((bf16[2,480,128]{2,1,0:T(8,128)(2,1)S(1)}, bf16[2,480,128]{2,1,0:T(8,128)(2,1)S(1)}, u32[]{:S(2)}, u32[]{:S(2)}) %collective-permute-start.6) | collective-permute-done | bytes 245792 | tf_op jit(solution)/shard_map/ppermute | solution.py:517
  59.1 0.4 collective-permute-done.7.refs_8_
  59.5 0.3 copy-done.14
  59.8 0.7 copy-done.15
  60.5 25.3 %verify_layer.1 = (bf16[4,480,128]{2,1,0:T(8,128)(2,1)}, bf16[4,480,128]{2,1,0:T(8,128)(2,1)}, bf16[4,480,128]{2,1,0:T(8,128)(2,1)}, bf16[4,480,128]{2,1,0:T(8,1...) custom-call(s32[32]{0:T(128)} %lengths.1, ...), custom_call_target="tpu_custom_call" | custom-call | flops 30000001024 | bytes 10000000 | tf_op jit(solution)/shard_map/verify_layer/pallas_call | solution.py:435
  85.8 2.1 %collective-permute-start.10 = (bf16[2,480,128]{2,1,0:T(8,128)(2,1)}, bf16[2,480,128]{2,1,0:T(8,128)(2,1)S(1)}, u32[]{:S(2)}, u32[]{:S(2)}) collective-permute-start(bf16[2,480,128]{2,1,0:T(8,128)(2,1)} %get-tuple-element.59), channel_id=1, source_target_pairs={{0,7},{1,0},{2,1},{3,2},{4,3},{5,4},{6,5},{7,6},{8,15},{9,8},{10,9... | collective-permute-start | bytes 737288 | tf_op jit(solution)/shard_map/ppermute | solution.py:521
  87.9 3.5 %collective-permute-done.10 = bf16[2,480,128]{2,1,0:T(8,128)(2,1)S(1)} collective-permute-done((bf16[2,480,128]{2,1,0:T(8,128)(2,1)}, bf16[2,480,128]{2,1,0:T(8,128)(2,1)S(1)}, u32[]{:S(2)}, u32[]{:S(2)}) %collective-permute-start.10) | collective-permute-done | bytes 245792 | tf_op jit(solution)/shard_map/ppermute | solution.py:521
  91.4 1.7 %fusion.5 = bf16[4,480,128]{2,1,0:T(8,128)(2,1)} fusion(bf16[4,480,128]{2,1,0:T(8,128)(2,1)} %get-tuple-element.58, bf16[2,480,128]{2,1,0:T(8,128)(2,1)S(1)} %collective-permute-done.10), kind=kLoop, calls=%fused_computation.14 | loop fusion | flops 491520 | bytes 737280 | tf_op jit(solution)/shard_map/dynamic_update_slice | solution.py:554
  93.1 3.0 %collective-permute-start.11 = (bf16[4,480,128]{2,1,0:T(8,128)(2,1)}, bf16[4,480,128]{2,1,0:T(8,128)(2,1)S(1)}, u32[]{:S(2)}, u32[]{:S(2)}) collective-permute-start(bf16[4,480,128]{2,1,0:T(8,128)(2,1)} %fusion.5), channel_id=1, source_target_pairs={{0,7},{1,0},{2,1},{3,2},{4,3},{5,4},{6,5},{7,6},{8,15},{9,8},{10,9... | collective-permute-start | bytes 1474568 | tf_op jit(solution)/shard_map/ppermute | solution.py:521
  96.1 1.7 %fusion.4 = bf16[4,480,128]{2,1,0:T(8,128)(2,1)} fusion(bf16[4,480,128]{2,1,0:T(8,128)(2,1)} %get-tuple-element.55, bf16[2,480,128]{2,1,0:T(8,128)(2,1)S(1)} %collective-permute-done.8), kind=kLoop, calls=%fused_computation.13 | loop fusion | flops 491520 | bytes 737280 | tf_op jit(solution)/shard_map/dynamic_update_slice | solution.py:554
  97.8 5.0 %collective-permute-done.11 = bf16[4,480,128]{2,1,0:T(8,128)(2,1)S(1)} collective-permute-done((bf16[4,480,128]{2,1,0:T(8,128)(2,1)}, bf16[4,480,128]{2,1,0:T(8,128)(2,1)S(1)}, u32[]{:S(2)}, u32[]{:S(2)}) %collective-permute-start.11) | collective-permute-done | bytes 491552 | tf_op jit(solution)/shard_map/ppermute | solution.py:521
  102.9 1.2 add_convert_fusion.2
  104.0 3.6 %collective-permute-done.9 = bf16[4,480,128]{2,1,0:T(8,128)(2,1)S(1)} collective-permute-done((bf16[4,480,128]{2,1,0:T(8,128)(2,1)}, bf16[4,480,128]{2,1,0:T(8,128)(2,1)S(1)}, u32[]{:S(2)}, u32[]{:S(2)}) %collective-permute-start.9) | collective-permute-done | bytes 491552 | tf_op jit(solution)/shard_map/ppermute | solution.py:517
  107.6 0.9 add_convert_fusion.3
  108.5 1.5 collective-permute-start.12
  110.0 12.8 %all-to-all-start.1 = ((bf16[32,16,256]{2,1,0:T(8,128)(2,1)}), bf16[32,16,256]{2,1,0:T(8,128)(2,1)S(1)}, u32[]{:S(2)}, u32[]{:S(2)}) async-start(bf16[32,16,256]{2,1,0:T(8,128)(2,1)} %get-tuple-element.64), calls=%async_computation.1 | async-start | bytes 524288 | tf_op jit(solution)/shard_map/all_to_all | solution.py:513
  122.9 1.2 add_convert_fusion
  124.1 1.9 %add_convert_fusion.1 = bf16[4,480,128]{2,1,0:T(8,128)(2,1)} fusion(bf16[4,480,128]{2,1,0:T(8,128)(2,1)} %collective-permute-done.12, bf16[4,480,128]{2,1,0:T(8,128)(2,1)S(1)} %copy-done.3), kind=kLoop, calls=%fused_computation.6 | loop fusion | flops 983040 | bytes 1474560 | tf_op jit(solution)/shard_map/convert_element_type | solution.py:525
  126.0 5.8 %all-to-all-done.1.extra_ref = bf16[32,16,256]{2,1,0:T(8,128)(2,1)S(1)} async-done(((bf16[32,16,256]{2,1,0:T(8,128)(2,1)}), bf16[32,16,256]{2,1,0:T(8,128)(2,1)S(1)}, u32[]{:S(2)}, u32[]{:S(2)}) %all-to-all-start.1) | async-done | bytes 262176 | tf_op jit(solution)/shard_map/all_to_all | solution.py:513
  131.9 2.7 %collective-permute-start.15 = (bf16[4,480,128]{2,1,0:T(8,128)(2,1)S(1)}, bf16[4,480,128]{2,1,0:T(8,128)(2,1)S(1)}, u32[]{:S(2)}, u32[]{:S(2)}) collective-permute-start(bf16[4,480,128]{2,1,0:T(8,128)(2,1)S(1)} %add_convert_fusion), channel_id=1, source_target_pairs={{0,7},{1,0},{2,1},{3,2},{4,3},{5,4},{6,5},{7,6},{8,15},{9,8},{10,9... | collective-permute-start | bytes 1474568 | tf_op jit(solution)/shard_map/ppermute | solution.py:521
  134.5 8.4 %assemble_cache.1 = bf16[32,160,512]{2,1,0:T(8,128)(2,1)} custom-call(bf16[32,160,512]{2,1,0:T(8,128)(2,1)} %all-to-all-done.cache_ref, bf16[32,16,256]{2,1,0:T(8,128)(2,1)} %copy-done.1), custom_call_target="tpu_custom_call" | custom-call | tf_op jit(solution)/shard_map/assemble_cache/pallas_call | solution.py:496
  142.9 3.0 %collective-permute-done.14.up_ref = bf16[4,480,128]{2,1,0:T(8,128)(2,1)S(1)} collective-permute-done((bf16[4,480,128]{2,1,0:T(8,128)(2,1)}, bf16[4,480,128]{2,1,0:T(8,128)(2,1)S(1)}, u32[]{:S(2)}, u32[]{:S(2)}) %collective-permute-start.14) | collective-permute-done | bytes 491552 | tf_op jit(solution)/shard_map/ppermute | solution.py:517
  145.9 0.8 copy-done.6
  146.7 0.2 copy-done.7
  146.9 2.6 %finish_rows.1 = bf16[768,320]{1,0:T(8,128)(2,1)} custom-call(s32[1]{0:T(128)} %bitcast.parity.me, bf16[4,480,128]{2,1,0:T(8,128)(2,1)} %get-tuple-element.52.own_ref, bf16[4,480,128]{2,1,0:T(8,128)(2,1)} %copy-done.6, bf16[4,480,128]{2,1,0:T(8,128)(2,1)} %copy-done.7, bf16[768,320]{1,0:T(8,128)(2,1)} %bitcast.10), custom_call_target="tpu_custom_call" | custom-call | tf_op jit(solution)/shard_map/finish_rows/pallas_call | solution.py:129
  (54 shorter events, 0.3 us)
Async XLA Ops:
  0.6 28.9 %copy-start = (bf16[2560,320]{0,1:T(8,128)(2,1)S(1)}, bf16[2560,320]{0,1:T(8,128)(2,1)}, u32[]{:S(2)}) copy-start(bf16[2560,320]{0,1:T(8,128)(2,1)} %param.12) | copy-start | bytes 4915204
  2.8 22.0 %collective-permute-start = (bf16[4,480,128]{2,1,0:T(8,128)(2,1)}, bf16[4,480,128]{2,1,0:T(8,128)(2,1)S(1)}, u32[]{:S(2)}, u32[]{:S(2)}) collective-permute-start(bf16[4,480,128]{2,1,0:T(8,128)(2,1)} %pack_rows.1.refs_0_), channel_id=1, source_target_pairs={{0,1},{1,2},{2,3},{3,4},{4,5},{5,6},{6,7},{7,0},{8,9},{9,10},{10,1... | collective-permute-start | bytes 1474568 | tf_op jit(solution)/shard_map/ppermute | solution.py:517
  5.4 19.5 %collective-permute-start.2 = (bf16[4,480,128]{2,1,0:T(8,128)(2,1)}, bf16[4,480,128]{2,1,0:T(8,128)(2,1)}, u32[]{:S(2)}, u32[]{:S(2)}) collective-permute-start(bf16[4,480,128]{2,1,0:T(8,128)(2,1)} %pack_rows.1.refs_0_), channel_id=1, source_target_pairs={{0,7},{1,0},{2,1},{3,2},{4,3},{5,4},{6,5},{7,6},{8,15},{9,8},{10,9... | collective-permute-start | bytes 1474568 | tf_op jit(solution)/shard_map/ppermute | solution.py:521
  10.0 6.5 %copy-start.17 = (s32[32]{0:T(128)}, s32[32]{0:T(128)S(1)}, u32[]{:S(2)}) copy-start(s32[32]{0:T(128)S(1)} %and_select_fusion.destination) | copy-start | bytes 388
  16.5 11.1 %copy-start.2 = (bf16[160,2560]{1,0:T(8,128)(2,1)S(1)}, bf16[160,2560]{1,0:T(8,128)(2,1)}, u32[]{:S(2)}) copy-start(bf16[160,2560]{1,0:T(8,128)(2,1)} %param.13) | copy-start | bytes 2457604
  16.5 11.1 %copy-start.10 = (f32[2560]{0:T(1024)S(1)}, f32[2560]{0:T(1024)}, u32[]{:S(2)}) copy-start(f32[2560]{0:T(1024)} %param.11) | copy-start | bytes 30724
  16.5 92.1 %all-to-all-start = ((bf16[32,160,512]{2,1,0:T(8,128)(2,1)}), bf16[32,160,512]{2,1,0:T(8,128)(2,1)}, u32[]{:S(2)}, u32[]{:S(2)}) async-start(bf16[32,160,512]{2,1,0:T(8,128)(2,1)} %order_cache.1), calls=%async_computation | async-start | bytes 10485760 | tf_op jit(solution)/shard_map/all_to_all | solution.py:513
  24.8 7.9 %copy-start.13 = (bf16[4,480,128]{2,1,0:T(8,128)(2,1)}, bf16[4,480,128]{2,1,0:T(8,128)(2,1)S(1)}, u32[]{:S(2)}) copy-start(bf16[4,480,128]{2,1,0:T(8,128)(2,1)S(1)} %collective-permute-done.refs_7_) | copy-start | bytes 1474564
  24.8 14.0 %collective-permute-start.1 = (bf16[4,480,128]{2,1,0:T(8,128)(2,1)S(1)}, bf16[4,480,128]{2,1,0:T(8,128)(2,1)}, u32[]{:S(2)}, u32[]{:S(2)}) collective-permute-start(bf16[4,480,128]{2,1,0:T(8,128)(2,1)S(1)} %collective-permute-done.refs_7_), channel_id=1, source_target_pairs={{0,1},{1,2},{2,3},{3,4},{4,5},{5,6},{6,7},{7,0},{8,9},{9,10},{10,1... | collective-permute-start | bytes 1474568 | tf_op jit(solution)/shard_map/ppermute | solution.py:517
  24.9 13.9 %collective-permute-start.3 = (bf16[4,480,128]{2,1,0:T(8,128)(2,1)}, bf16[4,480,128]{2,1,0:T(8,128)(2,1)}, u32[]{:S(2)}, u32[]{:S(2)}) collective-permute-start(bf16[4,480,128]{2,1,0:T(8,128)(2,1)} %collective-permute-done.2.refs_1_), channel_id=1, source_target_pairs={{0,7},{1,0},{2,1},{3,2},{4,3},{5,4},{6,5},{7,6},{8,15},{9,8},{10,9... | collective-permute-start | bytes 1474568 | tf_op jit(solution)/shard_map/ppermute | solution.py:521
  32.7 8.8 %copy-start.16 = (s32[32]{0:T(128)S(1)}, s32[32]{0:T(128)}, u32[]{:S(2)}) copy-start(s32[32]{0:T(128)} %lengths.1) | copy-start | bytes 388
  32.7 8.9 %copy-start.11 = (s32[32,24]{0,1:T(8,128)S(1)}, s32[32,24]{0,1:T(8,128)}, u32[]{:S(2)}) copy-start(s32[32,24]{0,1:T(8,128)} %param.17) | copy-start | bytes 9220
  32.7 9.5 %copy-start.12 = (s32[32,4]{0,1:T(4,128)S(1)}, s32[32,4]{0,1:T(4,128)}, u32[]{:S(2)}) copy-start(s32[32,4]{0,1:T(4,128)} %param.18) | copy-start | bytes 1540
  38.7 13.3 %collective-permute-start.4 = (bf16[4,480,128]{2,1,0:T(8,128)(2,1)}, bf16[4,480,128]{2,1,0:T(8,128)(2,1)S(1)}, u32[]{:S(2)}, u32[]{:S(2)}) collective-permute-start(bf16[4,480,128]{2,1,0:T(8,128)(2,1)} %collective-permute-done.1.refs_6_), channel_id=1, source_target_pairs={{0,1},{1,2},{2,3},{3,4},{4,5},{5,6},{6,7},{7,0},{8,9},{9,10},{10,1... | collective-permute-start | bytes 1474568 | tf_op jit(solution)/shard_map/ppermute | solution.py:517
  38.8 13.2 %collective-permute-start.5 = (bf16[4,480,128]{2,1,0:T(8,128)(2,1)}, bf16[4,480,128]{2,1,0:T(8,128)(2,1)S(1)}, u32[]{:S(2)}, u32[]{:S(2)}) collective-permute-start(bf16[4,480,128]{2,1,0:T(8,128)(2,1)} %collective-permute-done.3.refs_2_), channel_id=1, source_target_pairs={{0,7},{1,0},{2,1},{3,2},{4,3},{5,4},{6,5},{7,6},{8,15},{9,8},{10,9... | collective-permute-start | bytes 1474568 | tf_op jit(solution)/shard_map/ppermute | solution.py:521
  52.1 7.4 %copy-start.8 = (bf16[4,480,128]{2,1,0:T(8,128)(2,1)}, bf16[4,480,128]{2,1,0:T(8,128)(2,1)S(1)}, u32[]{:S(2)}) copy-start(bf16[4,480,128]{2,1,0:T(8,128)(2,1)S(1)} %collective-permute-done.4.refs_5_) | copy-start | bytes 1474564
  52.1 7.4 %copy-start.9 = (bf16[4,480,128]{2,1,0:T(8,128)(2,1)}, bf16[4,480,128]{2,1,0:T(8,128)(2,1)S(1)}, u32[]{:S(2)}) copy-start(bf16[4,480,128]{2,1,0:T(8,128)(2,1)S(1)} %collective-permute-done.5.refs_3_) | copy-start | bytes 1474564
  52.1 7.0 %collective-permute-start.6 = (bf16[2,480,128]{2,1,0:T(8,128)(2,1)S(1)}, bf16[2,480,128]{2,1,0:T(8,128)(2,1)S(1)}, u32[]{:S(2)}, u32[]{:S(2)}) collective-permute-start(bf16[2,480,128]{2,1,0:T(8,128)(2,1)S(1)} %slice.12), channel_id=1, source_target_pairs={{0,1},{1,2},{2,3},{3,4},{4,5},{5,6},{6,7},{7,0},{8,9},{9,10},{10,1... | collective-permute-start | bytes 737288 | tf_op jit(solution)/shard_map/ppermute | solution.py:517
  53.8 5.7 %collective-permute-start.7 = (bf16[2,480,128]{2,1,0:T(8,128)(2,1)S(1)}, bf16[2,480,128]{2,1,0:T(8,128)(2,1)S(1)}, u32[]{:S(2)}, u32[]{:S(2)}) collective-permute-start(bf16[2,480,128]{2,1,0:T(8,128)(2,1)S(1)} %slice.13), channel_id=1, source_target_pairs={{0,7},{1,0},{2,1},{3,2},{4,3},{5,4},{6,5},{7,6},{8,15},{9,8},{10,9... | collective-permute-start | bytes 737288 | tf_op jit(solution)/shard_map/ppermute | solution.py:521
  59.1 0.7 copy-start.14
  59.8 0.7 copy-start.15
  85.8 21.8 %copy-start.5 = (bf16[4,480,128]{2,1,0:T(8,128)(2,1)S(1)}, bf16[4,480,128]{2,1,0:T(8,128)(2,1)}, u32[]{:S(2)}) copy-start(bf16[4,480,128]{2,1,0:T(8,128)(2,1)} %get-tuple-element.54) | copy-start | bytes 1474564
  85.8 37.0 %copy-start.4 = (bf16[4,480,128]{2,1,0:T(8,128)(2,1)S(1)}, bf16[4,480,128]{2,1,0:T(8,128)(2,1)}, u32[]{:S(2)}) copy-start(bf16[4,480,128]{2,1,0:T(8,128)(2,1)} %get-tuple-element.62) | copy-start | bytes 1474564
  85.8 5.5 %collective-permute-start.10 = (bf16[2,480,128]{2,1,0:T(8,128)(2,1)}, bf16[2,480,128]{2,1,0:T(8,128)(2,1)S(1)}, u32[]{:S(2)}, u32[]{:S(2)}) collective-permute-start(bf16[2,480,128]{2,1,0:T(8,128)(2,1)} %get-tuple-element.59), channel_id=1, source_target_pairs={{0,7},{1,0},{2,1},{3,2},{4,3},{5,4},{6,5},{7,6},{8,15},{9,8},{10,9... | collective-permute-start | bytes 737288 | tf_op jit(solution)/shard_map/ppermute | solution.py:521
  87.9 8.2 %collective-permute-start.8 = (bf16[2,480,128]{2,1,0:T(8,128)(2,1)}, bf16[2,480,128]{2,1,0:T(8,128)(2,1)S(1)}, u32[]{:S(2)}, u32[]{:S(2)}) collective-permute-start(bf16[2,480,128]{2,1,0:T(8,128)(2,1)} %get-tuple-element.56), channel_id=1, source_target_pairs={{0,1},{1,2},{2,3},{3,4},{4,5},{5,6},{6,7},{7,0},{8,9},{9,10},{10,1... | collective-permute-start | bytes 737288 | tf_op jit(solution)/shard_map/ppermute | solution.py:517
  93.1 9.8 %collective-permute-start.11 = (bf16[4,480,128]{2,1,0:T(8,128)(2,1)}, bf16[4,480,128]{2,1,0:T(8,128)(2,1)S(1)}, u32[]{:S(2)}, u32[]{:S(2)}) collective-permute-start(bf16[4,480,128]{2,1,0:T(8,128)(2,1)} %fusion.5), channel_id=1, source_target_pairs={{0,7},{1,0},{2,1},{3,2},{4,3},{5,4},{6,5},{7,6},{8,15},{9,8},{10,9... | collective-permute-start | bytes 1474568 | tf_op jit(solution)/shard_map/ppermute | solution.py:521
  97.8 26.2 %copy-start.3 = (bf16[4,480,128]{2,1,0:T(8,128)(2,1)S(1)}, bf16[4,480,128]{2,1,0:T(8,128)(2,1)}, u32[]{:S(2)}) copy-start(bf16[4,480,128]{2,1,0:T(8,128)(2,1)} %get-tuple-element.53) | copy-start | bytes 1474564
  97.8 9.8 %collective-permute-start.9 = (bf16[4,480,128]{2,1,0:T(8,128)(2,1)}, bf16[4,480,128]{2,1,0:T(8,128)(2,1)S(1)}, u32[]{:S(2)}, u32[]{:S(2)}) collective-permute-start(bf16[4,480,128]{2,1,0:T(8,128)(2,1)} %fusion.4), channel_id=1, source_target_pairs={{0,1},{1,2},{2,3},{3,4},{4,5},{5,6},{6,7},{7,0},{8,9},{9,10},{10,1... | collective-permute-start | bytes 1474568 | tf_op jit(solution)/shard_map/ppermute | solution.py:517
  108.5 14.3 %collective-permute-start.13 = (bf16[4,480,128]{2,1,0:T(8,128)(2,1)S(1)}, bf16[4,480,128]{2,1,0:T(8,128)(2,1)}, u32[]{:S(2)}, u32[]{:S(2)}) collective-permute-start(bf16[4,480,128]{2,1,0:T(8,128)(2,1)S(1)} %add_convert_fusion.2), channel_id=1, source_target_pairs={{0,7},{1,0},{2,1},{3,2},{4,3},{5,4},{6,5},{7,6},{8,15},{9,8},{10,9... | collective-permute-start | bytes 1474568 | tf_op jit(solution)/shard_map/ppermute | solution.py:521
  108.5 15.5 %collective-permute-start.12 = (bf16[4,480,128]{2,1,0:T(8,128)(2,1)}, bf16[4,480,128]{2,1,0:T(8,128)(2,1)}, u32[]{:S(2)}, u32[]{:S(2)}) collective-permute-start(bf16[4,480,128]{2,1,0:T(8,128)(2,1)} %add_convert_fusion.3), channel_id=1, source_target_pairs={{0,1},{1,2},{2,3},{3,4},{4,5},{5,6},{6,7},{7,0},{8,9},{9,10},{10,1... | collective-permute-start | bytes 1474568 | tf_op jit(solution)/shard_map/ppermute | solution.py:517
  110.0 21.8 %all-to-all-start.1 = ((bf16[32,16,256]{2,1,0:T(8,128)(2,1)}), bf16[32,16,256]{2,1,0:T(8,128)(2,1)S(1)}, u32[]{:S(2)}, u32[]{:S(2)}) async-start(bf16[32,16,256]{2,1,0:T(8,128)(2,1)} %get-tuple-element.64), calls=%async_computation.1 | async-start | bytes 524288 | tf_op jit(solution)/shard_map/all_to_all | solution.py:513
  131.8 2.7 %copy-start.1 = (bf16[32,16,256]{2,1,0:T(8,128)(2,1)}, bf16[32,16,256]{2,1,0:T(8,128)(2,1)S(1)}, u32[]{:S(2)}) copy-start(bf16[32,16,256]{2,1,0:T(8,128)(2,1)S(1)} %all-to-all-done.1.extra_ref) | copy-start | bytes 786436
  131.8 14.1 %collective-permute-start.14 = (bf16[4,480,128]{2,1,0:T(8,128)(2,1)}, bf16[4,480,128]{2,1,0:T(8,128)(2,1)S(1)}, u32[]{:S(2)}, u32[]{:S(2)}) collective-permute-start(bf16[4,480,128]{2,1,0:T(8,128)(2,1)} %add_convert_fusion.1), channel_id=1, source_target_pairs={{0,1},{1,2},{2,3},{3,4},{4,5},{5,6},{6,7},{7,0},{8,9},{9,10},{10,1... | collective-permute-start | bytes 1474568 | tf_op jit(solution)/shard_map/ppermute | solution.py:517
  131.9 14.1 %collective-permute-start.15 = (bf16[4,480,128]{2,1,0:T(8,128)(2,1)S(1)}, bf16[4,480,128]{2,1,0:T(8,128)(2,1)S(1)}, u32[]{:S(2)}, u32[]{:S(2)}) collective-permute-start(bf16[4,480,128]{2,1,0:T(8,128)(2,1)S(1)} %add_convert_fusion), channel_id=1, source_target_pairs={{0,7},{1,0},{2,1},{3,2},{4,3},{5,4},{6,5},{7,6},{8,15},{9,8},{10,9... | collective-permute-start | bytes 1474568 | tf_op jit(solution)/shard_map/ppermute | solution.py:521
  145.9 0.8 copy-start.6
  145.9 1.0 copy-start.7

commit v6 on v5

--- a/solution.py
+++ b/solution.py
@@ -23,7 +23,7 @@
 PACKED = 2 * ROWS + HALF
 WIDTH = D // N_TP
 NEG = -1e30
-EXTRA = 16
+EXTRA = 8
 HALF_BLOCKS = 2
 BF = jnp.bfloat16
 F32 = jnp.float32
@@ -283,7 +283,6 @@
     @pl.when(b == 0)
     def _():
         ctx[...] = jnp.zeros_like(ctx)
-        extra[...] = jnp.zeros_like(extra)
 
     def received(k, first, last):
         piece = x_refs[k][0, first:last]
@@ -358,8 +357,9 @@
         q = jnp.concatenate(
             [qkv[rows, h * LANES : (h + 1) * LANES] for h in range(GROUP)], axis=0
         ).astype(BF)
-        k = qkv[rows, GROUP * LANES : (GROUP + 1) * LANES].astype(BF)
-        v = qkv[rows, (GROUP + 1) * LANES :].astype(BF)
+        fresh_rows = qkv[rows, GROUP * LANES :].astype(BF)
+        k = fresh_rows[:, :LANES]
+        v = fresh_rows[:, LANES:]
         cached = jnp.dot(q[:, :HD], cache_ref[i, 0:HD], preferred_element_type=F32)
         cached = jnp.where(column < length, cached * factor, NEG)
         fresh = lax.dot_general(q, k, (((1,), (1,)), ((), ())), preferred_element_type=F32)
@@ -383,20 +383,24 @@
 
         wanted = jnp.full((EXTRA, TREE), -1, jnp.int32)
         for m in range(DEPTH):
-            wanted = jnp.where(pick_row == m, accepted[r * DEPTH + m], wanted)
+            here = jnp.bitwise_and(pick_row, DEPTH - 1) == m
+            wanted = jnp.where(here, accepted[r * DEPTH + m], wanted)
         pick = jnp.where(pick_column == wanted, 1.0, 0.0).astype(BF)
-        new_keys = jnp.dot(pick, k, preferred_element_type=F32)
-        new_values = jnp.dot(pick, v, preferred_element_type=F32)
+        new = jnp.dot(pick, fresh_rows, preferred_element_type=F32)
+        shifted = pltpu.roll(new[:, LANES:], HD, 1)
+        tile = jnp.where(
+            extra_row < DEPTH,
+            jnp.where(extra_lane < HD, new[:, :LANES], shifted),
+            jnp.where(extra_lane < 2 * HD - LANES, shifted, 0.0),
+        )
         coarse = (length // 16).astype(F32)
         fine = (length % 16).astype(F32)
-        shifted = pltpu.roll(new_values, HD, 1)
-        new_keys = jnp.where(extra_lane < HD, new_keys, shifted)
-        extra[i, :, 0:LANES] = jnp.where(
-            extra_row == 8, coarse, jnp.where(extra_row == 9, fine, new_keys)
-        ).astype(BF)
-        extra[i, :, LANES : 2 * LANES] = jnp.where(
-            extra_lane < 2 * HD - LANES, shifted, 0.0
-        ).astype(BF)
+        marker = jnp.where(extra_row == DEPTH, coarse, fine)
+        marked = jnp.logical_and(
+            extra_lane >= 64,
+            jnp.logical_or(extra_row == DEPTH, extra_row == DEPTH + 1),
+        )
+        extra[i] = jnp.where(marked, marker, tile).astype(BF)
         copies.append(
             pltpu.make_async_copy(
                 extra.at[i], extra_out.at[destination[r]], sems.at[i]
@@ -440,7 +444,7 @@
             )
             for k in range(N_TP + 1)
         ]
-        + [jax.ShapeDtypeStruct((held, EXTRA, 2 * LANES), BF)],
+        + [jax.ShapeDtypeStruct((held, EXTRA, LANES), BF)],
         grid_spec=pltpu.PrefetchScalarGridSpec(
             num_scalar_prefetch=3,
             grid=(blocks,),
@@ -458,49 +462,58 @@
                 pltpu.VMEM((ROWS, D), BF),
                 pltpu.VMEM((ROWS, (GROUP + 2) * LANES), F32),
                 pltpu.VMEM((ROWS, GROUP * LANES), F32),
-                pltpu.VMEM((REQ_BLOCK, EXTRA, 2 * LANES), BF),
+                pltpu.VMEM((REQ_BLOCK, EXTRA, LANES), BF),
                 pltpu.SemaphoreType.DMA((REQ_BLOCK,)),
             ],
         ),
         compiler_params=pltpu.CompilerParams(vmem_limit_bytes=VMEM_LIMIT),
         cost_estimate=pl.CostEstimate(
-            flops=30_000_000_000, transcendentals=0, bytes_accessed=10_000_000
+            flops=1_000_000_000, transcendentals=0, bytes_accessed=10_000_000
         ),
         name="verify_layer",
     )(lengths, accepted, destination, *parts, w, wo, kv_cache, *tables)
 
 
-def assemble_kernel(cache_ref, extra_ref, o_ref):
+def assemble_kernel(me, cache_ref, extra_ref, o_ref):
     place_row = lax.broadcasted_iota(jnp.int32, (EXTRA, CACHE), 0)
     place_column = lane_index((EXTRA, CACHE))
+    upper = lane_index((1, LANES)) >= 64
     for i in range(cache_ref.shape[0]):
-        extra = extra_ref[i]
-        wide = extra[:, :LANES].astype(F32)
-        length = (wide[8:9] * 16.0 + wide[9:10]).astype(jnp.int32)
+        extra = extra_ref[i, 0]
+        wide = extra.astype(F32)
+        length = wide[DEPTH : DEPTH + 1] * 16.0 + wide[DEPTH + 1 : DEPTH + 2]
+        length = jnp.where(upper, length, swap_halves(length)).astype(jnp.int32)
         length = jnp.concatenate([length] * (CACHE // LANES), axis=1)
         offset = place_column - length
-        place = jnp.where(
-            jnp.logical_and(offset == place_row, place_row < DEPTH), 1.0, 0.0
-        ).astype(BF)
+        first = jnp.logical_and(offset == place_row, place_row < DEPTH)
+        second = jnp.logical_and(offset == place_row - DEPTH, place_row >= DEPTH)
         live = jnp.where(offset[0:1] < 0, 1.0, 0.0).astype(BF)
+        contract = (((0,), (0,)), ((), ()))
         new = lax.dot_general(
-            extra, place, (((0,), (0,)), ((), ())), preferred_element_type=F32
-        ).astype(BF)
-        o_ref[i] = cache_ref[i] * live + new[: 2 * HD]
-
-
-def assemble_cache(cached, extra):
+            extra, jnp.where(first, 1.0, 0.0).astype(BF), contract, preferred_element_type=F32
+        )
+        rest = lax.dot_general(
+            extra, jnp.where(second, 1.0, 0.0).astype(BF), contract, preferred_element_type=F32
+        )[: 2 * HD - LANES]
+        o_ref[i, :LANES] = cache_ref[i, :LANES] * live + new.astype(BF)
+        o_ref[i, LANES:] = cache_ref[i, LANES:] * live + rest.astype(BF)
+
+
+def assemble_cache(cached, extra, me):
     step = 4
-    cache_spec = pl.BlockSpec((step,) + cached.shape[1:], lambda s: (s, 0, 0))
-    extra_spec = pl.BlockSpec((step,) + extra.shape[1:], lambda s: (s, 0, 0))
+    cache_spec = pl.BlockSpec((step,) + cached.shape[1:], lambda s, me: (s, 0, 0))
+    extra_spec = pl.BlockSpec((step, 1, EXTRA, LANES), lambda s, me: (s, me[0], 0, 0))
     return pl.pallas_call(
         assemble_kernel,
         out_shape=jax.ShapeDtypeStruct(cached.shape, BF),
-        grid=(cached.shape[0] // step,),
-        in_specs=[cache_spec, extra_spec],
-        out_specs=cache_spec,
+        grid_spec=pltpu.PrefetchScalarGridSpec(
+            num_scalar_prefetch=1,
+            grid=(cached.shape[0] // step,),
+            in_specs=[cache_spec, extra_spec],
+            out_specs=cache_spec,
+        ),
         name="assemble_cache",
-    )(cached, extra)
+    )(me, cached, extra)
 
 
 def spread_heads(heads):
@@ -525,30 +538,6 @@
     return (a.astype(F32) + b.astype(F32)).astype(BF)
 
 
-def gather_ring(packed, weights, tables):
-    parts = [packed] * (N_TP + 1)
-    from_below = go_up(packed)
-    from_above = go_down(packed)
-    for step in range(1, N_TP // 2):
-        parts[N_TP - step] = from_below
-        parts[step] = from_above
-        if step == 2:
-            from_below, from_above, weights = lax.optimization_barrier(
-                (from_below, from_above, weights)
-            )
-        if step == 3:
-            from_below, from_above, tables = lax.optimization_barrier(
-                (from_below, from_above, tables)
-            )
-            from_below = from_below[:HALF_BLOCKS]
-            from_above = from_above[HALF_BLOCKS:]
-        from_below = go_up(from_below)
-        from_above = go_down(from_above)
-    parts[N_TP // 2] = from_below
-    parts[N_TP] = from_above
-    return parts, weights, tables
-
-
 def add_blocks(values, more, first):
     picked = values[first : first + HALF_BLOCKS]
     return lax.dynamic_update_slice(values, add_up(picked, more), (first, 0, 0))
@@ -558,6 +547,7 @@
     half = N_TP // 2
     up = go_up(targets[half])
     down = go_down(targets[N_TP])
+    extra = lax.all_gather(extra, "req", axis=0, tiled=False)
     for step in range(1, half):
         above, below = targets[half - step], targets[half + step]
         if step == 1:
@@ -565,14 +555,12 @@
             below = add_blocks(below, down, HALF_BLOCKS)
         else:
             above, below = add_up(above, up), add_up(below, down)
-        if step == 2:
+        if step == 3:
             above, below, cached, extra = lax.optimization_barrier(
                 (above, below, cached, extra)
             )
-            extra = exchange(extra)
-        if step == 3:
-            above, below, extra = lax.optimization_barrier((above, below, extra))
-            new_cache = assemble_cache(cached, extra)
+            me = lax.axis_index("req").astype(jnp.int32).reshape(1)
+            new_cache = assemble_cache(cached, extra, me)
         up = go_up(above)
         down = go_down(below)
     up, down, new_cache = lax.optimization_barrier((up, down, new_cache))
@@ -585,25 +573,39 @@
     held = hidden.shape[0]
     rows = hidden.reshape(held * TREE, WIDTH)
     me = lax.axis_index("tp").astype(jnp.int32).reshape(1)
-    packed = pack_rows(rows, me)
-
+    barrier = lax.optimization_barrier
+
+    parts = [pack_rows(rows, me)] * (N_TP + 1)
     destination = slot_of // held
     peer_index = jnp.arange(held, dtype=jnp.int32)
     matches = (destination[None, :] == peer_index[:, None]).astype(jnp.int32)
     send_order = jnp.sum(matches * peer_index[None, :], axis=1)
-    cached = exchange(order_cache(kv_cache, send_order))
-
-    tables = prepare_tables(parents, lengths)
+    ordered = order_cache(kv_cache, send_order)
+    below, above = go_up(parts[0]), go_down(parts[0])
+
+    below, above, w_keyval, ordered = barrier((below, above, w_keyval, ordered))
+    parts[7], parts[1] = below, above
     gain = norm_gain[:, None]
-    wq = (jnp.dot(w_query, spread_heads(GROUP), preferred_element_type=F32) * gain).astype(BF)
     wkv = lax.dot_general(
         w_keyval, spread_heads(2), (((0,), (0,)), ((), ())), preferred_element_type=F32
     )
     wkv = (wkv * gain).astype(BF)
+    ordered, wkv = barrier((ordered, wkv))
+    cached = exchange(ordered)
+    below, above = go_up(below), go_down(above)
+
+    below, above, w_query, wkv = barrier((below, above, w_query, wkv))
+    parts[6], parts[2] = below, above
+    wq = (jnp.dot(w_query, spread_heads(GROUP), preferred_element_type=F32) * gain).astype(BF)
     weights = arrange_weights(wq, wkv, w_out, me)
-    parts, weights, (tables, picks) = gather_ring(
-        packed, weights, (tables, accepted.reshape(-1))
-    )
+    below, above = go_up(below), go_down(above)
+
+    below, above, weights, parents = barrier((below, above, weights, parents))
+    parts[5], parts[3] = below, above
+    tables = prepare_tables(parents, lengths)
+    parts[4] = go_up(below[:HALF_BLOCKS])
+    parts[8] = go_down(above[HALF_BLOCKS:])
+    picks = accepted.reshape(-1)
 
     *targets, extra = verify_layer(
         parts, *weights, kv_cache, tables, lengths, picks, destination

time: 150 us -> 166 us (1.11)
  waiting for transfers between devices: 30.4 us -> 49 us
  between operations: 0.88 us -> 14.3 us
  starting transfers between devices: 45.4 us -> 32 us
  other arithmetic: 10.8 us -> 7.19 us
    all_gather x0 -> x1, waiting for transfers between devices: none -> 17.6 us  [scatter_ring(): extra = lax.all_gather(extra, 'req', axis=0, tiled=False)]
    all_to_all x2 -> x1, starting transfers between devices: 21.1 us -> 9.56 us  [exchange(): lax.all_to_all(values, 'req', split_axis=0, concat_axis=0, tiled=True)]
    ppermute x8, waiting for transfers between devices: 8.88 us -> 18.5 us  [go_down(): lax.ppermute(values, 'tp', [(i, (i - 1) % N_TP) for i in range(N_TP)])]
    all_to_all x2 -> x1, waiting for transfers between devices: 5.85 us -> 0.01 us  [exchange(): lax.all_to_all(values, 'req', split_axis=0, concat_axis=0, tiled=True)]
    convert_element_type x4, other arithmetic: 5.16 us -> 1.55 us  [add_up(): return (a.astype(F32) + b.astype(F32)).astype(BF)]
    ppermute x8, starting transfers between devices: 5.94 us -> 2.96 us  [go_up(): lax.ppermute(values, 'tp', [(i, (i + 1) % N_TP) for i in range(N_TP)])]
    ppermute x8, waiting for transfers between devices: 15.7 us -> 12.9 us  [go_up(): lax.ppermute(values, 'tp', [(i, (i + 1) % N_TP) for i in range(N_TP)])]
  transfers between devices with their start and end apart: 18 -> 18, of which waited for: 8 -> 11; matrix products, arithmetic and copies ran while one was open for 12% -> 9% of each run, Pallas kernels for 32% -> 29%
where the time goes in v6:
time: 166 us; the launch traced here: 165 us
  Pallas kernels  53.2 us (32%)
  waiting for transfers between devices  49 us (30%)
  starting transfers between devices  32 us (19%)
  between operations  14.3 us (9%)
  other arithmetic  7.19 us (4%)
  matrix products  5.06 us (3%)
  local copies, waits for them, and re-layouts  4.49 us (3%)
    pallas_call x1, Pallas kernels, verify_layer(): pl.pallas_call(layer_kernel, out_shape=[jax.ShapeDtypeStruct((HALF_BLOCKS...  25.4 us
    ppermute x8, starting transfers between devices, go_down(): lax.ppermute(values, 'tp', [(i, (i - 1) % N_TP) for i in range(N_TP)])  19.4 us
    ppermute x8, waiting for transfers between devices, go_down(): lax.ppermute(values, 'tp', [(i, (i - 1) % N_TP) for i in range(N_TP)])  18.5 us
    all_gather x1, waiting for transfers between devices, scatter_ring(): extra = lax.all_gather(extra, 'req', axis=0, tiled=False)  17.6 us
    ppermute x8, waiting for transfers between devices, go_up(): lax.ppermute(values, 'tp', [(i, (i + 1) % N_TP) for i in range(N_TP)])  12.9 us
    all_to_all x1, starting transfers between devices, exchange(): lax.all_to_all(values, 'req', split_axis=0, concat_axis=0, tiled=True)  9.56 us
    pallas_call x1, Pallas kernels, assemble_cache(): pl.pallas_call(assemble_kernel, out_shape=jax.ShapeDtypeStruct(cached.sha...  8.48 us
    pallas_call x1, Pallas kernels, arrange_weights(): pl.pallas_call(arrange_kernel, out_shape=(jax.ShapeDtypeStruct((D, (GROUP...  6.02 us
  transfers between devices with their start and end apart: 18, of which 11 were waited for; matrix products, arithmetic and copies ran while one was open for 9% of the time, Pallas kernels for 29%

profile of v6, /device:TPU:1, one launch (start us, length us, event | category | flops | bytes accessed | tf_op | source)
XLA Modules:
  0.0 165.2 jit_solution(7565886847025722871)
XLA Ops:
  7.2 2.1 %pack_rows.1.refs_0_ = bf16[4,480,128]{2,1,0:T(8,128)(2,1)} custom-call(s32[1]{0:T(128)} %bitcast.parity.me, bf16[768,320]{1,0:T(8,128)(2,1)} %bitcast.7), custom_call_target="tpu_custom_call" | custom-call | tf_op jit(solution)/shard_map/pack_rows/pallas_call | solution.py:73
  9.3 6.6 %collective-permute-start.1 = (bf16[4,480,128]{2,1,0:T(8,128)(2,1)}, bf16[4,480,128]{2,1,0:T(8,128)(2,1)S(1)}, u32[]{:S(2)}, u32[]{:S(2)}) collective-permute-start(bf16[4,480,128]{2,1,0:T(8,128)(2,1)} %pack_rows.1.refs_0_), channel_id=1, source_target_pairs={{0,7},{1,0},{2,1},{3,2},{4,3},{5,4},{6,5},{7,6},{8,15},{9,8},{10,9... | collective-permute-start | bytes 1474568 | tf_op jit(solution)/shard_map/ppermute | solution.py:534
  15.9 0.7 and_select_fusion.2.destination
  16.5 0.7 select_reduce_fusion.order
  17.2 6.0 %order_cache.1 = bf16[32,160,512]{2,1,0:T(8,128)(2,1)} custom-call(s32[32]{0:T(128)} %select_reduce_fusion.order, bf16[32,160,512]{2,1,0:T(8,128)(2,1)} %refs_11_.1), custom_call_target="tpu_custom_call" | custom-call | tf_op jit(solution)/shard_map/order_cache/pallas_call | solution.py:257
  23.2 2.9 %collective-permute-done.1.refs_1_ = bf16[4,480,128]{2,1,0:T(8,128)(2,1)S(1)} collective-permute-done((bf16[4,480,128]{2,1,0:T(8,128)(2,1)}, bf16[4,480,128]{2,1,0:T(8,128)(2,1)S(1)}, u32[]{:S(2)}, u32[]{:S(2)}) %collective-permute-start.1) | collective-permute-done | bytes 491552 | tf_op jit(solution)/shard_map/ppermute | solution.py:534
  26.1 3.0 %collective-permute-done.refs_7_ = bf16[4,480,128]{2,1,0:T(8,128)(2,1)S(1)} collective-permute-done((bf16[4,480,128]{2,1,0:T(8,128)(2,1)}, bf16[4,480,128]{2,1,0:T(8,128)(2,1)S(1)}, u32[]{:S(2)}, u32[]{:S(2)}) %collective-permute-start) | collective-permute-done | bytes 491552 | tf_op jit(solution)/shard_map/ppermute | solution.py:530
  29.1 0.4 collective-permute-start.3
  29.5 1.1 collective-permute-start.2
  30.6 1.9 %fusion.wkv_ref = bf16[2560,256]{1,0:T(8,128)(2,1)} fusion(bf16[160,2560]{1,0:T(8,128)(2,1)S(1)} %copy-done.16, f32[2560]{0:T(1024)S(1)} %copy-done.17, s32[160]{0:T(256)S(1)} %fusion.16), kind=kOutput, calls=%fused_computation.2 | convolution fusion | flops 211066880 | bytes 2140800 | tf_op jit(solution)/shard_map/dot_general | solution.py:589
  32.4 9.6 %all-to-all-start = ((bf16[32,160,512]{2,1,0:T(8,128)(2,1)}), bf16[32,160,512]{2,1,0:T(8,128)(2,1)}, u32[]{:S(2)}, u32[]{:S(2)}) async-start(bf16[32,160,512]{2,1,0:T(8,128)(2,1)} %order_cache.1), calls=%async_computation | async-start | bytes 10485760 | tf_op jit(solution)/shard_map/all_to_all | solution.py:526
  42.1 1.4 collective-permute-start.5
  43.5 0.2 collective-permute-start.4
  43.8 3.2 %multiply_convert_fusion.wq_ref = bf16[2560,512]{1,0:T(8,128)(2,1)} fusion(bf16[2560,320]{0,1:T(8,128)(2,1)S(1)} %copy-done, f32[2560]{0:T(1024)S(1)} %copy-done.17, s32[320]{0:T(512)S(1)} %fusion.10), kind=kOutput, calls=%fused_computation | convolution fusion | flops 841646080 | bytes 4271360 | tf_op jit(solution)/shard_map/dot_general | solution.py:599
  47.0 6.0 %arrange_weights.1 = (bf16[2560,768]{1,0:T(8,128)(2,1)}, bf16[512,2560]{1,0:T(8,128)(2,1)}) custom-call(s32[1]{0:T(128)} %bitcast.parity.me, bf16[2560,512]{1,0:T(8,128)(2,1)} %multiply_convert_fusion.wq_ref, bf16[2560,256]{1,0:T(8,128)(2,1)} %fusion.wkv_ref, bf16[320,2560]{1,0:T(8,128)(2,1)} %wo_ref.1), custom_call_target="tpu_custom_call" | custom-call | tf_op jit(solution)/shard_map/arrange_weights/pallas_call | solution.py:182
  53.0 0.5 collective-permute-done.5.refs_3_
  53.4 2.9 %collective-permute-done.4.refs_5_ = bf16[4,480,128]{2,1,0:T(8,128)(2,1)S(1)} collective-permute-done((bf16[4,480,128]{2,1,0:T(8,128)(2,1)S(1)}, bf16[4,480,128]{2,1,0:T(8,128)(2,1)S(1)}, u32[]{:S(2)}, u32[]{:S(2)}) %collective-permute-start.4) | collective-permute-done | bytes 491552 | tf_op jit(solution)/shard_map/ppermute | solution.py:530
  56.4 0.8 slice.12
  57.2 2.7 %collective-permute-start.7 = (bf16[2,480,128]{2,1,0:T(8,128)(2,1)S(1)}, bf16[2,480,128]{2,1,0:T(8,128)(2,1)S(1)}, u32[]{:S(2)}, u32[]{:S(2)}) collective-permute-start(bf16[2,480,128]{2,1,0:T(8,128)(2,1)S(1)} %slice.13), channel_id=1, source_target_pairs={{0,7},{1,0},{2,1},{3,2},{4,3},{5,4},{6,5},{7,6},{8,15},{9,8},{10,9... | collective-permute-start | bytes 737288 | tf_op jit(solution)/shard_map/ppermute | solution.py:534
  60.0 0.7 reshape.149.accepted
  60.6 0.6 stack.2.step_ref
  61.2 0.7 multiply_sine_fusion
  62.0 0.7 copy.19.parents_ref
  62.7 2.6 %prepare_tables.1 = (f32[32,24,128]{2,1,0:T(8,128)}, f32[32,24,128]{2,1,0:T(8,128)}, f32[32,24,128]{2,1,0:T(8,128)}) custom-call(s32[32,24]{1,0:T(8,128)} %copy.19.parents_ref, f32[32,128]{1,0:T(8,128)} %get-tuple-element.77.cos_ref, f32[32,128]{1,0:T(8,128)} %get-tuple-element.76.sin_ref, f32[8,128]{1,0:T(8,128)} %stack.2.step_ref), custom_call_target="tpu_custom_call" | custom-call | tf_op jit(solution)/shard_map/prepare_tables/pallas_call | solution.py:235
  65.3 0.6 copy-done.10
  66.1 25.4 %verify_layer.1 = (bf16[4,480,128]{2,1,0:T(8,128)(2,1)}, bf16[4,480,128]{2,1,0:T(8,128)(2,1)}, bf16[4,480,128]{2,1,0:T(8,128)(2,1)}, bf16[4,480,128]{2,1,0:T(8,1...) custom-call(s32[32]{0:T(128)} %lengths.1, ...), custom_call_target="tpu_custom_call" | custom-call | flops 1000000000 | bytes 10000000 | tf_op jit(solution)/shard_map/verify_layer/pallas_call | solution.py:439
  91.6 1.2 collective-permute-start.11
  92.8 0.3 collective-permute-start.8
  93.1 4.2 %collective-permute-done.11 = bf16[2,480,128]{2,1,0:T(8,128)(2,1)S(1)} collective-permute-done((bf16[2,480,128]{2,1,0:T(8,128)(2,1)}, bf16[2,480,128]{2,1,0:T(8,128)(2,1)S(1)}, u32[]{:S(2)}, u32[]{:S(2)}) %collective-permute-start.11) | collective-permute-done | bytes 245792 | tf_op jit(solution)/shard_map/ppermute | solution.py:534
  97.3 1.7 %fusion.3 = bf16[4,480,128]{2,1,0:T(8,128)(2,1)} fusion(bf16[4,480,128]{2,1,0:T(8,128)(2,1)} %get-tuple-element.65, bf16[2,480,128]{2,1,0:T(8,128)(2,1)S(1)} %collective-permute-done.11), kind=kLoop, calls=%fused_computation.12 | loop fusion | flops 491520 | bytes 737280 | tf_op jit(solution)/shard_map/dynamic_update_slice | solution.py:543
  99.0 2.3 %collective-permute-start.12 = (bf16[4,480,128]{2,1,0:T(8,128)(2,1)}, bf16[4,480,128]{2,1,0:T(8,128)(2,1)S(1)}, u32[]{:S(2)}, u32[]{:S(2)}) collective-permute-start(bf16[4,480,128]{2,1,0:T(8,128)(2,1)} %fusion.3), channel_id=1, source_target_pairs={{0,7},{1,0},{2,1},{3,2},{4,3},{5,4},{6,5},{7,6},{8,15},{9,8},{10,9... | collective-permute-start | bytes 1474568 | tf_op jit(solution)/shard_map/ppermute | solution.py:534
  101.4 1.7 %fusion.2 = bf16[4,480,128]{2,1,0:T(8,128)(2,1)} fusion(bf16[4,480,128]{2,1,0:T(8,128)(2,1)} %get-tuple-element.61, bf16[2,480,128]{2,1,0:T(8,128)(2,1)S(1)} %collective-permute-done.8), kind=kLoop, calls=%fused_computation.11 | loop fusion | flops 491520 | bytes 737280 | tf_op jit(solution)/shard_map/dynamic_update_slice | solution.py:543
  103.1 5.6 %collective-permute-done.12 = bf16[4,480,128]{2,1,0:T(8,128)(2,1)S(1)} collective-permute-done((bf16[4,480,128]{2,1,0:T(8,128)(2,1)}, bf16[4,480,128]{2,1,0:T(8,128)(2,1)S(1)}, u32[]{:S(2)}, u32[]{:S(2)}) %collective-permute-start.12) | collective-permute-done | bytes 491552 | tf_op jit(solution)/shard_map/ppermute | solution.py:534
  108.7 1.2 add_convert_fusion.1
  109.9 3.1 %collective-permute-start.13 = (bf16[4,480,128]{2,1,0:T(8,128)(2,1)S(1)}, bf16[4,480,128]{2,1,0:T(8,128)(2,1)S(1)}, u32[]{:S(2)}, u32[]{:S(2)}) collective-permute-start(bf16[4,480,128]{2,1,0:T(8,128)(2,1)S(1)} %add_convert_fusion.1), channel_id=1, source_target_pairs={{0,7},{1,0},{2,1},{3,2},{4,3},{5,4},{6,5},{7,6},{8,15},{9,8},{10,9... | collective-permute-start | bytes 1474568 | tf_op jit(solution)/shard_map/ppermute | solution.py:534
  113.0 0.2 collective-permute-done.9
  113.3 0.1 add_convert_fusion.3
  113.5 5.3 %collective-permute-done.13 = bf16[4,480,128]{2,1,0:T(8,128)(2,1)S(1)} collective-permute-done((bf16[4,480,128]{2,1,0:T(8,128)(2,1)S(1)}, bf16[4,480,128]{2,1,0:T(8,128)(2,1)S(1)}, u32[]{:S(2)}, u32[]{:S(2)}) %collective-permute-start.13) | collective-permute-done | bytes 491552 | tf_op jit(solution)/shard_map/ppermute | solution.py:534
  118.8 0.1 add_convert_fusion
  118.9 3.8 %collective-permute-done.10 = bf16[4,480,128]{2,1,0:T(8,128)(2,1)S(1)} collective-permute-done((bf16[4,480,128]{2,1,0:T(8,128)(2,1)S(1)}, bf16[4,480,128]{2,1,0:T(8,128)(2,1)S(1)}, u32[]{:S(2)}, u32[]{:S(2)}) %collective-permute-start.10) | collective-permute-done | bytes 491552 | tf_op jit(solution)/shard_map/ppermute | solution.py:530
  122.7 0.1 add_convert_fusion.2
  122.9 17.6 %all-gather.3.cloned.1.call-done = bf16[1024,8,128]{2,1,0:T(8,128)(2,1)} async-done(((bf16[32,8,128]{2,1,0:T(8,128)(2,1)}), bf16[1024,8,128]{2,1,0:T(8,128)(2,1)}) %all-gather.3.cloned.1.call-update) | async-done | bytes 2097168 | tf_op jit(solution)/shard_map/all_gather | solution.py:550
  140.5 1.3 collective-permute-start.14
  141.8 1.8 %collective-permute-start.15 = (bf16[4,480,128]{2,1,0:T(8,128)(2,1)S(1)}, bf16[4,480,128]{2,1,0:T(8,128)(2,1)}, u32[]{:S(2)}, u32[]{:S(2)}) collective-permute-start(bf16[4,480,128]{2,1,0:T(8,128)(2,1)S(1)} %add_convert_fusion), channel_id=1, source_target_pairs={{0,7},{1,0},{2,1},{3,2},{4,3},{5,4},{6,5},{7,6},{8,15},{9,8},{10,9... | collective-permute-start | bytes 1474568 | tf_op jit(solution)/shard_map/ppermute | solution.py:534
  143.5 8.5 %assemble_cache.1 = bf16[32,160,512]{2,1,0:T(8,128)(2,1)} custom-call(s32[1]{0:T(128)} %bitcast.3.me, bf16[32,160,512]{2,1,0:T(8,128)(2,1)} %all-to-all-done.cache_ref, bf16[32,32,8,128]{3,2,1,0:T(8,128)(2,1)} %bitcast.9), custom_call_target="tpu_custom_call" | custom-call | tf_op jit(solution)/shard_map/assemble_cache/pallas_call | solution.py:506
  152.0 2.9 %collective-permute-done.14.up_ref = bf16[4,480,128]{2,1,0:T(8,128)(2,1)S(1)} collective-permute-done((bf16[4,480,128]{2,1,0:T(8,128)(2,1)S(1)}, bf16[4,480,128]{2,1,0:T(8,128)(2,1)S(1)}, u32[]{:S(2)}, u32[]{:S(2)}) %collective-permute-start.14) | collective-permute-done | bytes 491552 | tf_op jit(solution)/shard_map/ppermute | solution.py:530
  154.9 0.8 copy-done.9
  155.8 2.6 %finish_rows.1 = bf16[768,320]{1,0:T(8,128)(2,1)} custom-call(s32[1]{0:T(128)} %bitcast.parity.me, bf16[4,480,128]{2,1,0:T(8,128)(2,1)} %get-tuple-element.58.own_ref, bf16[4,480,128]{2,1,0:T(8,128)(2,1)} %copy-done.9, bf16[4,480,128]{2,1,0:T(8,128)(2,1)} %collective-permute-done.15.down_ref, bf16[768,320]{1,0:T(8,128)(2,1)} %bitcast.8), custom_call_target="tpu_custom_call" | custom-call | tf_op jit(solution)/shard_map/finish_rows/pallas_call | solution.py:129
  (55 shorter events, 0.6 us)
Async XLA Ops:
  7.2 36.6 %copy-start = (bf16[2560,320]{0,1:T(8,128)(2,1)S(1)}, bf16[2560,320]{0,1:T(8,128)(2,1)}, u32[]{:S(2)}) copy-start(bf16[2560,320]{0,1:T(8,128)(2,1)} %param.12) | copy-start | bytes 4915204
  9.3 16.8 %collective-permute-start.1 = (bf16[4,480,128]{2,1,0:T(8,128)(2,1)}, bf16[4,480,128]{2,1,0:T(8,128)(2,1)S(1)}, u32[]{:S(2)}, u32[]{:S(2)}) collective-permute-start(bf16[4,480,128]{2,1,0:T(8,128)(2,1)} %pack_rows.1.refs_0_), channel_id=1, source_target_pairs={{0,7},{1,0},{2,1},{3,2},{4,3},{5,4},{6,5},{7,6},{8,15},{9,8},{10,9... | collective-permute-start | bytes 1474568 | tf_op jit(solution)/shard_map/ppermute | solution.py:534
  15.9 13.2 %collective-permute-start = (bf16[4,480,128]{2,1,0:T(8,128)(2,1)}, bf16[4,480,128]{2,1,0:T(8,128)(2,1)S(1)}, u32[]{:S(2)}, u32[]{:S(2)}) collective-permute-start(bf16[4,480,128]{2,1,0:T(8,128)(2,1)} %pack_rows.1.refs_0_), channel_id=1, source_target_pairs={{0,1},{1,2},{2,3},{3,4},{4,5},{5,6},{6,7},{7,0},{8,9},{9,10},{10,1... | collective-permute-start | bytes 1474568 | tf_op jit(solution)/shard_map/ppermute | solution.py:530
  16.5 6.6 %copy-start.15 = (s32[32]{0:T(128)}, s32[32]{0:T(128)S(1)}, u32[]{:S(2)}) copy-start(s32[32]{0:T(128)S(1)} %and_select_fusion.2.destination) | copy-start | bytes 388
  17.2 13.4 %copy-start.16 = (bf16[160,2560]{1,0:T(8,128)(2,1)S(1)}, bf16[160,2560]{1,0:T(8,128)(2,1)}, u32[]{:S(2)}) copy-start(bf16[160,2560]{1,0:T(8,128)(2,1)} %param.13) | copy-start | bytes 2457604
  17.2 13.4 %copy-start.17 = (f32[2560]{0:T(1024)S(1)}, f32[2560]{0:T(1024)}, u32[]{:S(2)}) copy-start(f32[2560]{0:T(1024)} %param.11) | copy-start | bytes 30724
  26.1 6.4 %copy-start.3 = (bf16[4,480,128]{2,1,0:T(8,128)(2,1)}, bf16[4,480,128]{2,1,0:T(8,128)(2,1)S(1)}, u32[]{:S(2)}) copy-start(bf16[4,480,128]{2,1,0:T(8,128)(2,1)S(1)} %collective-permute-done.1.refs_1_) | copy-start | bytes 1474564
  29.1 3.4 %copy-start.4 = (bf16[4,480,128]{2,1,0:T(8,128)(2,1)}, bf16[4,480,128]{2,1,0:T(8,128)(2,1)S(1)}, u32[]{:S(2)}) copy-start(bf16[4,480,128]{2,1,0:T(8,128)(2,1)S(1)} %collective-permute-done.refs_7_) | copy-start | bytes 1474564
  29.1 13.0 %collective-permute-start.3 = (bf16[4,480,128]{2,1,0:T(8,128)(2,1)S(1)}, bf16[4,480,128]{2,1,0:T(8,128)(2,1)}, u32[]{:S(2)}, u32[]{:S(2)}) collective-permute-start(bf16[4,480,128]{2,1,0:T(8,128)(2,1)S(1)} %collective-permute-done.1.refs_1_), channel_id=1, source_target_pairs={{0,7},{1,0},{2,1},{3,2},{4,3},{5,4},{6,5},{7,6},{8,15},{9,8},{10,9... | collective-permute-start | bytes 1474568 | tf_op jit(solution)/shard_map/ppermute | solution.py:534
  29.5 12.7 %collective-permute-start.2 = (bf16[4,480,128]{2,1,0:T(8,128)(2,1)S(1)}, bf16[4,480,128]{2,1,0:T(8,128)(2,1)S(1)}, u32[]{:S(2)}, u32[]{:S(2)}) collective-permute-start(bf16[4,480,128]{2,1,0:T(8,128)(2,1)S(1)} %collective-permute-done.refs_7_), channel_id=1, source_target_pairs={{0,1},{1,2},{2,3},{3,4},{4,5},{5,6},{6,7},{7,0},{8,9},{9,10},{10,1... | collective-permute-start | bytes 1474568 | tf_op jit(solution)/shard_map/ppermute | solution.py:530
  32.4 90.4 %all-to-all-start = ((bf16[32,160,512]{2,1,0:T(8,128)(2,1)}), bf16[32,160,512]{2,1,0:T(8,128)(2,1)}, u32[]{:S(2)}, u32[]{:S(2)}) async-start(bf16[32,160,512]{2,1,0:T(8,128)(2,1)} %order_cache.1), calls=%async_computation | async-start | bytes 10485760 | tf_op jit(solution)/shard_map/all_to_all | solution.py:526
  42.0 98.5 %all-gather.3.cloned.1.call-start = ((), (), s32[]{:S(2)}) async-start(), calls=%async_computation.1 | async-start | bytes 2162688 | tf_op jit(solution)/shard_map/all_gather | solution.py:550
  42.1 10.8 %copy-start.5 = (bf16[4,480,128]{2,1,0:T(8,128)(2,1)}, bf16[4,480,128]{2,1,0:T(8,128)(2,1)S(1)}, u32[]{:S(2)}) copy-start(bf16[4,480,128]{2,1,0:T(8,128)(2,1)S(1)} %collective-permute-done.2.refs_6_) | copy-start | bytes 1474564
  42.1 11.3 %collective-permute-start.5 = (bf16[4,480,128]{2,1,0:T(8,128)(2,1)}, bf16[4,480,128]{2,1,0:T(8,128)(2,1)S(1)}, u32[]{:S(2)}, u32[]{:S(2)}) collective-permute-start(bf16[4,480,128]{2,1,0:T(8,128)(2,1)} %collective-permute-done.3.refs_2_), channel_id=1, source_target_pairs={{0,7},{1,0},{2,1},{3,2},{4,3},{5,4},{6,5},{7,6},{8,15},{9,8},{10,9... | collective-permute-start | bytes 1474568 | tf_op jit(solution)/shard_map/ppermute | solution.py:534
  43.5 12.8 %collective-permute-start.4 = (bf16[4,480,128]{2,1,0:T(8,128)(2,1)S(1)}, bf16[4,480,128]{2,1,0:T(8,128)(2,1)S(1)}, u32[]{:S(2)}, u32[]{:S(2)}) collective-permute-start(bf16[4,480,128]{2,1,0:T(8,128)(2,1)S(1)} %collective-permute-done.2.refs_6_), channel_id=1, source_target_pairs={{0,1},{1,2},{2,3},{3,4},{4,5},{5,6},{6,7},{7,0},{8,9},{9,10},{10,1... | collective-permute-start | bytes 1474568 | tf_op jit(solution)/shard_map/ppermute | solution.py:530
  47.0 12.9 %copy-start.14 = (s32[32]{0:T(128)S(1)}, s32[32]{0:T(128)}, u32[]{:S(2)}) copy-start(s32[32]{0:T(128)} %lengths.1) | copy-start | bytes 388
  47.0 12.9 %copy-start.13 = (s32[32,4]{0,1:T(4,128)S(1)}, s32[32,4]{0,1:T(4,128)}, u32[]{:S(2)}) copy-start(s32[32,4]{0,1:T(4,128)} %param.18) | copy-start | bytes 1540
  47.0 15.0 %copy-start.12 = (s32[32,24]{0,1:T(8,128)S(1)}, s32[32,24]{0,1:T(8,128)}, u32[]{:S(2)}) copy-start(s32[32,24]{0,1:T(8,128)} %param.17) | copy-start | bytes 9220
  53.4 11.9 %copy-start.1 = (bf16[4,480,128]{2,1,0:T(8,128)(2,1)}, bf16[4,480,128]{2,1,0:T(8,128)(2,1)S(1)}, u32[]{:S(2)}) copy-start(bf16[4,480,128]{2,1,0:T(8,128)(2,1)S(1)} %collective-permute-done.5.refs_3_) | copy-start | bytes 1474564
  56.3 9.0 %copy-start.2 = (bf16[4,480,128]{2,1,0:T(8,128)(2,1)}, bf16[4,480,128]{2,1,0:T(8,128)(2,1)S(1)}, u32[]{:S(2)}) copy-start(bf16[4,480,128]{2,1,0:T(8,128)(2,1)S(1)} %collective-permute-done.4.refs_5_) | copy-start | bytes 1474564
  57.2 8.1 %collective-permute-start.6 = (bf16[2,480,128]{2,1,0:T(8,128)(2,1)}, bf16[2,480,128]{2,1,0:T(8,128)(2,1)S(1)}, u32[]{:S(2)}, u32[]{:S(2)}) collective-permute-start(bf16[2,480,128]{2,1,0:T(8,128)(2,1)} %slice.12), channel_id=1, source_target_pairs={{0,1},{1,2},{2,3},{3,4},{4,5},{5,6},{6,7},{7,0},{8,9},{9,10},{10,1... | collective-permute-start | bytes 737288 | tf_op jit(solution)/shard_map/ppermute | solution.py:530
  57.2 8.1 %collective-permute-start.7 = (bf16[2,480,128]{2,1,0:T(8,128)(2,1)S(1)}, bf16[2,480,128]{2,1,0:T(8,128)(2,1)S(1)}, u32[]{:S(2)}, u32[]{:S(2)}) collective-permute-start(bf16[2,480,128]{2,1,0:T(8,128)(2,1)S(1)} %slice.13), channel_id=1, source_target_pairs={{0,7},{1,0},{2,1},{3,2},{4,3},{5,4},{6,5},{7,6},{8,15},{9,8},{10,9... | collective-permute-start | bytes 737288 | tf_op jit(solution)/shard_map/ppermute | solution.py:534
  65.3 0.7 copy-start.10
  65.3 0.8 copy-start.11
  91.5 21.7 %copy-start.8 = (bf16[4,480,128]{2,1,0:T(8,128)(2,1)S(1)}, bf16[4,480,128]{2,1,0:T(8,128)(2,1)}, u32[]{:S(2)}) copy-start(bf16[4,480,128]{2,1,0:T(8,128)(2,1)} %get-tuple-element.60) | copy-start | bytes 1474564
  91.5 27.3 %copy-start.7 = (bf16[4,480,128]{2,1,0:T(8,128)(2,1)S(1)}, bf16[4,480,128]{2,1,0:T(8,128)(2,1)}, u32[]{:S(2)}) copy-start(bf16[4,480,128]{2,1,0:T(8,128)(2,1)} %get-tuple-element.63) | copy-start | bytes 1474564
  91.6 5.7 %collective-permute-start.11 = (bf16[2,480,128]{2,1,0:T(8,128)(2,1)}, bf16[2,480,128]{2,1,0:T(8,128)(2,1)S(1)}, u32[]{:S(2)}, u32[]{:S(2)}) collective-permute-start(bf16[2,480,128]{2,1,0:T(8,128)(2,1)} %get-tuple-element.66), channel_id=1, source_target_pairs={{0,7},{1,0},{2,1},{3,2},{4,3},{5,4},{6,5},{7,6},{8,15},{9,8},{10,9... | collective-permute-start | bytes 737288 | tf_op jit(solution)/shard_map/ppermute | solution.py:534
  92.8 8.6 %collective-permute-start.8 = (bf16[2,480,128]{2,1,0:T(8,128)(2,1)}, bf16[2,480,128]{2,1,0:T(8,128)(2,1)S(1)}, u32[]{:S(2)}, u32[]{:S(2)}) collective-permute-start(bf16[2,480,128]{2,1,0:T(8,128)(2,1)} %get-tuple-element.62), channel_id=1, source_target_pairs={{0,1},{1,2},{2,3},{3,4},{4,5},{5,6},{6,7},{7,0},{8,9},{9,10},{10,1... | collective-permute-start | bytes 737288 | tf_op jit(solution)/shard_map/ppermute | solution.py:530
  99.0 23.7 %copy-start.6 = (bf16[4,480,128]{2,1,0:T(8,128)(2,1)S(1)}, bf16[4,480,128]{2,1,0:T(8,128)(2,1)}, u32[]{:S(2)}) copy-start(bf16[4,480,128]{2,1,0:T(8,128)(2,1)} %get-tuple-element.59) | copy-start | bytes 1474564
  99.0 9.7 %collective-permute-start.12 = (bf16[4,480,128]{2,1,0:T(8,128)(2,1)}, bf16[4,480,128]{2,1,0:T(8,128)(2,1)S(1)}, u32[]{:S(2)}, u32[]{:S(2)}) collective-permute-start(bf16[4,480,128]{2,1,0:T(8,128)(2,1)} %fusion.3), channel_id=1, source_target_pairs={{0,7},{1,0},{2,1},{3,2},{4,3},{5,4},{6,5},{7,6},{8,15},{9,8},{10,9... | collective-permute-start | bytes 1474568 | tf_op jit(solution)/shard_map/ppermute | solution.py:534
  103.1 10.2 %collective-permute-start.9 = (bf16[4,480,128]{2,1,0:T(8,128)(2,1)}, bf16[4,480,128]{2,1,0:T(8,128)(2,1)S(1)}, u32[]{:S(2)}, u32[]{:S(2)}) collective-permute-start(bf16[4,480,128]{2,1,0:T(8,128)(2,1)} %fusion.2), channel_id=1, source_target_pairs={{0,1},{1,2},{2,3},{3,4},{4,5},{5,6},{6,7},{7,0},{8,9},{9,10},{10,1... | collective-permute-start | bytes 1474568 | tf_op jit(solution)/shard_map/ppermute | solution.py:530
  109.9 8.9 %collective-permute-start.13 = (bf16[4,480,128]{2,1,0:T(8,128)(2,1)S(1)}, bf16[4,480,128]{2,1,0:T(8,128)(2,1)S(1)}, u32[]{:S(2)}, u32[]{:S(2)}) collective-permute-start(bf16[4,480,128]{2,1,0:T(8,128)(2,1)S(1)} %add_convert_fusion.1), channel_id=1, source_target_pairs={{0,7},{1,0},{2,1},{3,2},{4,3},{5,4},{6,5},{7,6},{8,15},{9,8},{10,9... | collective-permute-start | bytes 1474568 | tf_op jit(solution)/shard_map/ppermute | solution.py:534
  113.4 9.3 %collective-permute-start.10 = (bf16[4,480,128]{2,1,0:T(8,128)(2,1)S(1)}, bf16[4,480,128]{2,1,0:T(8,128)(2,1)S(1)}, u32[]{:S(2)}, u32[]{:S(2)}) collective-permute-start(bf16[4,480,128]{2,1,0:T(8,128)(2,1)S(1)} %add_convert_fusion.3), channel_id=1, source_target_pairs={{0,1},{1,2},{2,3},{3,4},{4,5},{5,6},{6,7},{7,0},{8,9},{9,10},{10,1... | collective-permute-start | bytes 1474568 | tf_op jit(solution)/shard_map/ppermute | solution.py:530
  140.5 14.5 %collective-permute-start.14 = (bf16[4,480,128]{2,1,0:T(8,128)(2,1)S(1)}, bf16[4,480,128]{2,1,0:T(8,128)(2,1)S(1)}, u32[]{:S(2)}, u32[]{:S(2)}) collective-permute-start(bf16[4,480,128]{2,1,0:T(8,128)(2,1)S(1)} %add_convert_fusion.2), channel_id=1, source_target_pairs={{0,1},{1,2},{2,3},{3,4},{4,5},{5,6},{6,7},{7,0},{8,9},{9,10},{10,1... | collective-permute-start | bytes 1474568 | tf_op jit(solution)/shard_map/ppermute | solution.py:530
  141.8 13.2 %collective-permute-start.15 = (bf16[4,480,128]{2,1,0:T(8,128)(2,1)S(1)}, bf16[4,480,128]{2,1,0:T(8,128)(2,1)}, u32[]{:S(2)}, u32[]{:S(2)}) collective-permute-start(bf16[4,480,128]{2,1,0:T(8,128)(2,1)S(1)} %add_convert_fusion), channel_id=1, source_target_pairs={{0,7},{1,0},{2,1},{3,2},{4,3},{5,4},{6,5},{7,6},{8,15},{9,8},{10,9... | collective-permute-start | bytes 1474568 | tf_op jit(solution)/shard_map/ppermute | solution.py:534
  154.9 0.8 copy-start.9
Sparse Core Ops, SparseCore 0:
  91.7 48.7 all-gather.2

commit v7 on v6

--- a/solution.py
+++ b/solution.py
@@ -273,36 +273,16 @@
     )(send_order, kv_cache)
 
 
-def layer_kernel(lengths, accepted, destination, *refs):
+def project_kernel(lengths, accepted, destination, *refs):
     x_refs = refs[: N_TP + 1]
-    w_ref, wo_ref, cache_ref, bias_ref, cos_ref, sin_ref = refs[N_TP + 1 : N_TP + 7]
-    out_refs = refs[N_TP + 7 : 2 * N_TP + 8]
-    extra_out, xs, qkv, ctx, extra, sems = refs[2 * N_TP + 8 :]
+    w_ref, cos_ref, sin_ref, qkv, extra_out, xs, extra, sems = refs[N_TP + 1 :]
     b = pl.program_id(0)
-
-    @pl.when(b == 0)
-    def _():
-        ctx[...] = jnp.zeros_like(ctx)
 
     def received(k, first, last):
         piece = x_refs[k][0, first:last]
         if k == N_TP // 2:
             piece = jnp.where(b < HALF_BLOCKS, piece, x_refs[N_TP][0, first:last])
         return piece
-
-    def deliver(k, first, last, values):
-        values = values.astype(BF)
-        if k != N_TP // 2:
-            out_refs[k][0, first:last] = values
-            return
-
-        @pl.when(b < HALF_BLOCKS)
-        def _():
-            out_refs[k][0, first:last] = values
-
-        @pl.when(b >= HALF_BLOCKS)
-        def _():
-            out_refs[N_TP][0, first:last] = values
 
     low_half = lane_index((HALF, LANES)) < 64
     squares = jnp.zeros((ROWS, LANES), F32)
@@ -343,13 +323,71 @@
         qkv[:, head] = rotate(projected[:, head])
     qkv[:, (GROUP + 1) * LANES :] = projected[:, (GROUP + 1) * LANES :]
 
-    factor = math.log2(math.e) / math.sqrt(HD)
-    column = lane_index((GROUP * TREE, CACHE))
     extra_row = lax.broadcasted_iota(jnp.int32, (EXTRA, LANES), 0)
     extra_lane = lane_index((EXTRA, LANES))
     pick_row = lax.broadcasted_iota(jnp.int32, (EXTRA, TREE), 0)
     pick_column = lane_index((EXTRA, TREE))
     copies = []
+    for i in range(REQ_BLOCK):
+        r = b * REQ_BLOCK + i
+        length = lengths[r]
+        fresh_rows = qkv[i * TREE : (i + 1) * TREE, GROUP * LANES :].astype(BF)
+        wanted = jnp.full((EXTRA, TREE), -1, jnp.int32)
+        for m in range(DEPTH):
+            here = jnp.bitwise_and(pick_row, DEPTH - 1) == m
+            wanted = jnp.where(here, accepted[r * DEPTH + m], wanted)
+        pick = jnp.where(pick_column == wanted, 1.0, 0.0).astype(BF)
+        new = jnp.dot(pick, fresh_rows, preferred_element_type=F32)
+        shifted = pltpu.roll(new[:, LANES:], HD, 1)
+        tile = jnp.where(
+            extra_row < DEPTH,
+            jnp.where(extra_lane < HD, new[:, :LANES], shifted),
+            jnp.where(extra_lane < 2 * HD - LANES, shifted, 0.0),
+        )
+        coarse = (length // 16).astype(F32)
+        fine = (length % 16).astype(F32)
+        marker = jnp.where(extra_row == DEPTH, coarse, fine)
+        marked = jnp.logical_and(
+            extra_lane >= 64,
+            jnp.logical_or(extra_row == DEPTH, extra_row == DEPTH + 1),
+        )
+        extra[i] = jnp.where(marked, marker, tile).astype(BF)
+        copies.append(
+            pltpu.make_async_copy(
+                extra.at[i], extra_out.at[destination[r]], sems.at[i]
+            )
+        )
+        copies[-1].start()
+    for copy in copies:
+        copy.wait()
+
+
+def attend_kernel(lengths, qkv, wo_ref, cache_ref, bias_ref, *refs):
+    out_refs = refs[: N_TP + 1]
+    ctx = refs[N_TP + 1]
+    b = pl.program_id(0)
+
+    @pl.when(b == 0)
+    def _():
+        ctx[...] = jnp.zeros_like(ctx)
+
+    def deliver(k, first, last, values):
+        values = values.astype(BF)
+        if k != N_TP // 2:
+            out_refs[k][0, first:last] = values
+            return
+
+        @pl.when(b < HALF_BLOCKS)
+        def _():
+            out_refs[k][0, first:last] = values
+
+        @pl.when(b >= HALF_BLOCKS)
+        def _():
+            out_refs[N_TP][0, first:last] = values
+
+    low_half = lane_index((HALF, LANES)) < 64
+    factor = math.log2(math.e) / math.sqrt(HD)
+    column = lane_index((GROUP * TREE, CACHE))
     for i in range(REQ_BLOCK):
         r = b * REQ_BLOCK + i
         length = lengths[r]
@@ -381,33 +419,6 @@
         for h in range(GROUP):
             ctx[rows, h * LANES : h * LANES + HD] = mixed[h * TREE : (h + 1) * TREE]
 
-        wanted = jnp.full((EXTRA, TREE), -1, jnp.int32)
-        for m in range(DEPTH):
-            here = jnp.bitwise_and(pick_row, DEPTH - 1) == m
-            wanted = jnp.where(here, accepted[r * DEPTH + m], wanted)
-        pick = jnp.where(pick_column == wanted, 1.0, 0.0).astype(BF)
-        new = jnp.dot(pick, fresh_rows, preferred_element_type=F32)
-        shifted = pltpu.roll(new[:, LANES:], HD, 1)
-        tile = jnp.where(
-            extra_row < DEPTH,
-            jnp.where(extra_lane < HD, new[:, :LANES], shifted),
-            jnp.where(extra_lane < 2 * HD - LANES, shifted, 0.0),
-        )
-        coarse = (length // 16).astype(F32)
-        fine = (length % 16).astype(F32)
-        marker = jnp.where(extra_row == DEPTH, coarse, fine)
-        marked = jnp.logical_and(
-            extra_lane >= 64,
-            jnp.logical_or(extra_row == DEPTH, extra_row == DEPTH + 1),
-        )
-        extra[i] = jnp.where(marked, marker, tile).astype(BF)
-        copies.append(
-            pltpu.make_async_copy(
-                extra.at[i], extra_out.at[destination[r]], sems.at[i]
-            )
-        )
-        copies[-1].start()
-
     partial = jnp.dot(ctx[...].astype(BF), wo_ref[...], preferred_element_type=F32)
     for j in range(N_TP // 2):
         base = j * 5 * LANES
@@ -419,49 +430,37 @@
         top, bottom = tail[:HALF], tail[HALF:]
         deliver(2 * j, 2 * ROWS, PACKED, jnp.where(low_half, top, swap_halves(bottom)))
         deliver(2 * j + 1, 2 * ROWS, PACKED, jnp.where(low_half, swap_halves(top), bottom))
-    for copy in copies:
-        copy.wait()
-
-
-def verify_layer(parts, w, wo, kv_cache, tables, lengths, accepted, destination):
-    held = kv_cache.shape[0]
+
+
+def project_rows(parts, w, cosines, sines, lengths, accepted, destination):
+    held = lengths.shape[0]
     blocks = held // REQ_BLOCK
-    full = lambda b, *_: (0, 0)
     packed = pl.BlockSpec((1, PACKED, LANES), lambda b, *_: (b, 0, 0))
     table = pl.BlockSpec((REQ_BLOCK, TREE, LANES), lambda b, *_: (b, 0, 0))
-    in_specs = [packed] * (N_TP + 1)
-    in_specs[N_TP // 2] = pl.BlockSpec(
+    x_specs = [packed] * (N_TP + 1)
+    x_specs[N_TP // 2] = pl.BlockSpec(
         (1, PACKED, LANES), lambda b, *_: (jnp.minimum(b, HALF_BLOCKS - 1), 0, 0)
     )
-    in_specs[N_TP] = pl.BlockSpec(
+    x_specs[N_TP] = pl.BlockSpec(
         (1, PACKED, LANES), lambda b, *_: (jnp.maximum(b - HALF_BLOCKS, 0), 0, 0)
     )
-    return pl.pallas_call(
-        layer_kernel,
-        out_shape=[
-            jax.ShapeDtypeStruct(
-                (HALF_BLOCKS if k % (N_TP // 2) == 0 and k > 0 else blocks, PACKED, LANES), BF
-            )
-            for k in range(N_TP + 1)
-        ]
-        + [jax.ShapeDtypeStruct((held, EXTRA, LANES), BF)],
+    width = w.shape[1]
+    return pl.pallas_call(
+        project_kernel,
+        out_shape=(
+            jax.ShapeDtypeStruct((held * TREE, width), F32),
+            jax.ShapeDtypeStruct((held, EXTRA, LANES), BF),
+        ),
         grid_spec=pltpu.PrefetchScalarGridSpec(
             num_scalar_prefetch=3,
             grid=(blocks,),
-            in_specs=in_specs
-            + [
-                pl.BlockSpec(w.shape, full),
-                pl.BlockSpec(wo.shape, full),
-                pl.BlockSpec((REQ_BLOCK, 2 * HD, CACHE), lambda b, *_: (b, 0, 0)),
-                table,
-                table,
-                table,
-            ],
-            out_specs=in_specs + [pl.BlockSpec(memory_space=pl.ANY)],
+            in_specs=x_specs + [pl.BlockSpec(w.shape, lambda b, *_: (0, 0)), table, table],
+            out_specs=(
+                pl.BlockSpec((ROWS, width), lambda b, *_: (b, 0)),
+                pl.BlockSpec(memory_space=pl.ANY),
+            ),
             scratch_shapes=[
                 pltpu.VMEM((ROWS, D), BF),
-                pltpu.VMEM((ROWS, (GROUP + 2) * LANES), F32),
-                pltpu.VMEM((ROWS, GROUP * LANES), F32),
                 pltpu.VMEM((REQ_BLOCK, EXTRA, LANES), BF),
                 pltpu.SemaphoreType.DMA((REQ_BLOCK,)),
             ],
@@ -470,8 +469,44 @@
         cost_estimate=pl.CostEstimate(
             flops=1_000_000_000, transcendentals=0, bytes_accessed=10_000_000
         ),
-        name="verify_layer",
-    )(lengths, accepted, destination, *parts, w, wo, kv_cache, *tables)
+        name="project_rows",
+    )(lengths, accepted, destination, *parts, w, cosines, sines)
+
+
+def attend_cache(qkv, wo, kv_cache, bias, lengths):
+    held = kv_cache.shape[0]
+    blocks = held // REQ_BLOCK
+    packed = pl.BlockSpec((1, PACKED, LANES), lambda b, *_: (b, 0, 0))
+    out_specs = [packed] * (N_TP + 1)
+    out_specs[N_TP // 2] = pl.BlockSpec(
+        (1, PACKED, LANES), lambda b, *_: (jnp.minimum(b, HALF_BLOCKS - 1), 0, 0)
+    )
+    out_specs[N_TP] = pl.BlockSpec(
+        (1, PACKED, LANES), lambda b, *_: (jnp.maximum(b - HALF_BLOCKS, 0), 0, 0)
+    )
+    out_blocks = [blocks] * (N_TP + 1)
+    out_blocks[N_TP // 2] = out_blocks[N_TP] = HALF_BLOCKS
+    return pl.pallas_call(
+        attend_kernel,
+        out_shape=[jax.ShapeDtypeStruct((n, PACKED, LANES), BF) for n in out_blocks],
+        grid_spec=pltpu.PrefetchScalarGridSpec(
+            num_scalar_prefetch=1,
+            grid=(blocks,),
+            in_specs=[
+                pl.BlockSpec((ROWS, qkv.shape[1]), lambda b, *_: (b, 0)),
+                pl.BlockSpec(wo.shape, lambda b, *_: (0, 0)),
+                pl.BlockSpec((REQ_BLOCK, 2 * HD, CACHE), lambda b, *_: (b, 0, 0)),
+                pl.BlockSpec((REQ_BLOCK, TREE, LANES), lambda b, *_: (b, 0, 0)),
+            ],
+            out_specs=out_specs,
+            scratch_shapes=[pltpu.VMEM((ROWS, GROUP * LANES), F32)],
+        ),
+        compiler_params=pltpu.CompilerParams(vmem_limit_bytes=VMEM_LIMIT),
+        cost_estimate=pl.CostEstimate(
+            flops=1_000_000_000, transcendentals=0, bytes_accessed=10_000_000
+        ),
+        name="attend_cache",
+    )(lengths, qkv, wo, kv_cache, bias)
 
 
 def assemble_kernel(me, cache_ref, extra_ref, o_ref):
@@ -547,7 +582,6 @@
     half = N_TP // 2
     up = go_up(targets[half])
     down = go_down(targets[N_TP])
-    extra = lax.all_gather(extra, "req", axis=0, tiled=False)
     for step in range(1, half):
         above, below = targets[half - step], targets[half + step]
         if step == 1:
@@ -607,9 +641,11 @@
     parts[8] = go_down(above[HALF_BLOCKS:])
     picks = accepted.reshape(-1)
 
-    *targets, extra = verify_layer(
-        parts, *weights, kv_cache, tables, lengths, picks, destination
-    )
+    bias, cosines, sines = tables
+    w, wo = weights
+    qkv, extra = project_rows(parts, w, cosines, sines, lengths, picks, destination)
+    extra = lax.all_gather(extra, "req", axis=0, tiled=False)
+    targets = attend_cache(qkv, wo, kv_cache, bias, lengths)
     up, down, new_cache = scatter_ring(targets, cached, extra)
     out_rows = finish_rows(targets[0], up, down, rows, me)
     return (out_rows.reshape(hidden.shape), new_cache)

time: 166 us -> 158 us (0.952)
  waiting for transfers between devices: 49 us -> 37.6 us
  Pallas kernels: 53.2 us -> 57.8 us
    all_gather x1, waiting for transfers between devices: 17.6 us -> 5.96 us  [per_device(): extra = lax.all_gather(extra, 'req', axis=0, tiled=False)]
    pallas_call x1 -> x2, Pallas kernels: 25.4 us -> 29.9 us  [the longest x1 17.4 us: attend_cache(): pl.pallas_call(attend_kernel, out_shape=[jax.ShapeDtypeStruct((n, PACKED,...]
  transfers between devices with their start and end apart: 18 -> 18, of which waited for: 11 -> 11; matrix products, arithmetic and copies ran while one was open for 9% -> 10% of each run, Pallas kernels for 29% -> 34%
where the time goes in v7:
time: 158 us
  Pallas kernels  57.8 us (37%)
  waiting for transfers between devices  37.6 us (24%)
  starting transfers between devices  31.5 us (20%)
  between operations  14.3 us (9%)
  other arithmetic  7.16 us (5%)
  matrix products  5.05 us (3%)
  local copies, waits for them, and re-layouts  4.49 us (3%)
    ppermute x8, starting transfers between devices, go_down(): lax.ppermute(values, 'tp', [(i, (i - 1) % N_TP) for i in range(N_TP)])  18.9 us
    ppermute x8, waiting for transfers between devices, go_down(): lax.ppermute(values, 'tp', [(i, (i - 1) % N_TP) for i in range(N_TP)])  18.7 us
    pallas_call x1, Pallas kernels, attend_cache(): pl.pallas_call(attend_kernel, out_shape=[jax.ShapeDtypeStruct((n, PACKED,...  17.4 us
    ppermute x8, waiting for transfers between devices, go_up(): lax.ppermute(values, 'tp', [(i, (i + 1) % N_TP) for i in range(N_TP)])  13 us
    pallas_call x1, Pallas kernels, project_rows(): pl.pallas_call(project_kernel, out_shape=(jax.ShapeDtypeStruct((held * TR...  12.5 us
    all_to_all x1, starting transfers between devices, exchange(): lax.all_to_all(values, 'req', split_axis=0, concat_axis=0, tiled=True)  9.56 us
    pallas_call x1, Pallas kernels, assemble_cache(): pl.pallas_call(assemble_kernel, out_shape=jax.ShapeDtypeStruct(cached.sha...  8.49 us
    pallas_call x1, Pallas kernels, arrange_weights(): pl.pallas_call(arrange_kernel, out_shape=(jax.ShapeDtypeStruct((D, (GROUP...  6.02 us
  transfers between devices with their start and end apart: 18, of which 11 were waited for; matrix products, arithmetic and copies ran while one was open for 10% of the time, Pallas kernels for 34%

profile of v7, /device:TPU:1, one launch (start us, length us, event | category | flops | bytes accessed | tf_op | source)
XLA Modules:
  0.0 157.9 jit_solution(4062043677299014383)
XLA Ops:
  7.2 2.1 %pack_rows.1.refs_0_ = bf16[4,480,128]{2,1,0:T(8,128)(2,1)} custom-call(s32[1]{0:T(128)} %bitcast.parity.me, bf16[768,320]{1,0:T(8,128)(2,1)} %bitcast.7), custom_call_target="tpu_custom_call" | custom-call | tf_op jit(solution)/shard_map/pack_rows/pallas_call | solution.py:73
  9.3 6.6 %collective-permute-start.1 = (bf16[4,480,128]{2,1,0:T(8,128)(2,1)}, bf16[4,480,128]{2,1,0:T(8,128)(2,1)S(1)}, u32[]{:S(2)}, u32[]{:S(2)}) collective-permute-start(bf16[4,480,128]{2,1,0:T(8,128)(2,1)} %pack_rows.1.refs_0_), channel_id=1, source_target_pairs={{0,7},{1,0},{2,1},{3,2},{4,3},{5,4},{6,5},{7,6},{8,15},{9,8},{10,9... | collective-permute-start | bytes 1474568 | tf_op jit(solution)/shard_map/ppermute | solution.py:569
  15.9 0.7 and_select_fusion.2.destination
  16.5 0.7 select_reduce_fusion.order
  17.2 6.0 %order_cache.1 = bf16[32,160,512]{2,1,0:T(8,128)(2,1)} custom-call(s32[32]{0:T(128)} %select_reduce_fusion.order, bf16[32,160,512]{2,1,0:T(8,128)(2,1)} %cache_ref.3), custom_call_target="tpu_custom_call" | custom-call | tf_op jit(solution)/shard_map/order_cache/pallas_call | solution.py:257
  23.2 2.9 %collective-permute-done.1.refs_1_ = bf16[4,480,128]{2,1,0:T(8,128)(2,1)S(1)} collective-permute-done((bf16[4,480,128]{2,1,0:T(8,128)(2,1)}, bf16[4,480,128]{2,1,0:T(8,128)(2,1)S(1)}, u32[]{:S(2)}, u32[]{:S(2)}) %collective-permute-start.1) | collective-permute-done | bytes 491552 | tf_op jit(solution)/shard_map/ppermute | solution.py:569
  26.1 3.0 %collective-permute-done.refs_7_ = bf16[4,480,128]{2,1,0:T(8,128)(2,1)S(1)} collective-permute-done((bf16[4,480,128]{2,1,0:T(8,128)(2,1)}, bf16[4,480,128]{2,1,0:T(8,128)(2,1)S(1)}, u32[]{:S(2)}, u32[]{:S(2)}) %collective-permute-start) | collective-permute-done | bytes 491552 | tf_op jit(solution)/shard_map/ppermute | solution.py:565
  29.1 0.4 collective-permute-start.3
  29.5 1.1 collective-permute-start.2
  30.6 1.9 %fusion.wkv_ref = bf16[2560,256]{1,0:T(8,128)(2,1)} fusion(bf16[160,2560]{1,0:T(8,128)(2,1)S(1)} %copy-done.16, f32[2560]{0:T(1024)S(1)} %copy-done.17, s32[160]{0:T(256)S(1)} %fusion.16), kind=kOutput, calls=%fused_computation.2 | convolution fusion | flops 211066880 | bytes 2140800 | tf_op jit(solution)/shard_map/dot_general | solution.py:623
  32.5 9.6 %all-to-all-start = ((bf16[32,160,512]{2,1,0:T(8,128)(2,1)}), bf16[32,160,512]{2,1,0:T(8,128)(2,1)}, u32[]{:S(2)}, u32[]{:S(2)}) async-start(bf16[32,160,512]{2,1,0:T(8,128)(2,1)} %order_cache.1), calls=%async_computation | async-start | bytes 10485760 | tf_op jit(solution)/shard_map/all_to_all | solution.py:561
  42.1 1.4 collective-permute-start.5
  43.5 0.2 collective-permute-start.4
  43.8 3.2 %multiply_convert_fusion.wq_ref = bf16[2560,512]{1,0:T(8,128)(2,1)} fusion(bf16[2560,320]{0,1:T(8,128)(2,1)S(1)} %copy-done, f32[2560]{0:T(1024)S(1)} %copy-done.17, s32[320]{0:T(512)S(1)} %fusion.10), kind=kOutput, calls=%fused_computation | convolution fusion | flops 841646080 | bytes 4271360 | tf_op jit(solution)/shard_map/dot_general | solution.py:633
  46.9 6.0 %arrange_weights.1 = (bf16[2560,768]{1,0:T(8,128)(2,1)}, bf16[512,2560]{1,0:T(8,128)(2,1)}) custom-call(s32[1]{0:T(128)} %bitcast.parity.me, bf16[2560,512]{1,0:T(8,128)(2,1)} %multiply_convert_fusion.wq_ref, bf16[2560,256]{1,0:T(8,128)(2,1)} %fusion.wkv_ref, bf16[320,2560]{1,0:T(8,128)(2,1)} %wo_ref.1), custom_call_target="tpu_custom_call" | custom-call | tf_op jit(solution)/shard_map/arrange_weights/pallas_call | solution.py:182
  53.0 0.5 collective-permute-done.5.refs_3_
  53.5 2.9 %collective-permute-done.4.refs_5_ = bf16[4,480,128]{2,1,0:T(8,128)(2,1)S(1)} collective-permute-done((bf16[4,480,128]{2,1,0:T(8,128)(2,1)S(1)}, bf16[4,480,128]{2,1,0:T(8,128)(2,1)S(1)}, u32[]{:S(2)}, u32[]{:S(2)}) %collective-permute-start.4) | collective-permute-done | bytes 491552 | tf_op jit(solution)/shard_map/ppermute | solution.py:565
  56.4 0.8 slice.12
  57.2 2.7 %collective-permute-start.7 = (bf16[2,480,128]{2,1,0:T(8,128)(2,1)S(1)}, bf16[2,480,128]{2,1,0:T(8,128)(2,1)S(1)}, u32[]{:S(2)}, u32[]{:S(2)}) collective-permute-start(bf16[2,480,128]{2,1,0:T(8,128)(2,1)S(1)} %slice.13), channel_id=1, source_target_pairs={{0,7},{1,0},{2,1},{3,2},{4,3},{5,4},{6,5},{7,6},{8,15},{9,8},{10,9... | collective-permute-start | bytes 737288 | tf_op jit(solution)/shard_map/ppermute | solution.py:569
  60.0 0.7 reshape.149.accepted
  60.7 0.6 stack.2.step_ref
  61.3 0.8 multiply_sine_fusion
  62.0 0.7 copy.19.parents_ref
  62.7 2.6 %prepare_tables.1 = (f32[32,24,128]{2,1,0:T(8,128)}, f32[32,24,128]{2,1,0:T(8,128)}, f32[32,24,128]{2,1,0:T(8,128)}) custom-call(s32[32,24]{1,0:T(8,128)} %copy.19.parents_ref, f32[32,128]{1,0:T(8,128)} %get-tuple-element.79.cos_ref, f32[32,128]{1,0:T(8,128)} %get-tuple-element.78.sin_ref, f32[8,128]{1,0:T(8,128)} %stack.2.step_ref), custom_call_target="tpu_custom_call" | custom-call | tf_op jit(solution)/shard_map/prepare_tables/pallas_call | solution.py:235
  65.4 0.6 copy-done.10
  66.1 12.5 %project_rows.1 = (f32[768,768]{1,0:T(8,128)}, bf16[32,8,128]{2,1,0:T(8,128)(2,1)}) custom-call(s32[32]{0:T(128)} %lengths.3, s32[128]{0:T(128)} %reshape.149.accepted, s32[32]{0:T(128)} %copy-done.15, bf16[4,480,128]{2,1,0:T(8,128)(2,1)} %pack_rows.1.refs_0_, bf16[4,480,128]{2,1,0:T(8,128)(2,1)} %copy-done.3, ...), custom_call_target="tpu_custom_call" | custom-call | flops 1000000000 | bytes 10000000 | tf_op jit(solution)/shard_map/project_rows/pallas_call | solution.py:448
  78.6 17.4 %attend_cache.1 = (bf16[4,480,128]{2,1,0:T(8,128)(2,1)}, bf16[4,480,128]{2,1,0:T(8,128)(2,1)}, bf16[4,480,128]{2,1,0:T(8,128)(2,1)}, bf16[4,480,128]{2,1,0:T(8,1...) custom-call(s32[32]{0:T(128)} %lengths.3, ...), custom_call_target="tpu_custom_call" | custom-call | flops 1000000000 | bytes 10000000 | tf_op jit(solution)/shard_map/attend_cache/pallas_call | solution.py:489
  96.1 1.2 collective-permute-start.11
  97.3 0.4 collective-permute-start.8
  97.7 4.2 %collective-permute-done.11 = bf16[2,480,128]{2,1,0:T(8,128)(2,1)S(1)} collective-permute-done((bf16[2,480,128]{2,1,0:T(8,128)(2,1)}, bf16[2,480,128]{2,1,0:T(8,128)(2,1)S(1)}, u32[]{:S(2)}, u32[]{:S(2)}) %collective-permute-start.11) | collective-permute-done | bytes 245792 | tf_op jit(solution)/shard_map/ppermute | solution.py:569
  101.8 1.7 %fusion.3 = bf16[4,480,128]{2,1,0:T(8,128)(2,1)} fusion(bf16[4,480,128]{2,1,0:T(8,128)(2,1)} %get-tuple-element.67, bf16[2,480,128]{2,1,0:T(8,128)(2,1)S(1)} %collective-permute-done.11), kind=kLoop, calls=%fused_computation.12 | loop fusion | flops 491520 | bytes 737280 | tf_op jit(solution)/shard_map/dynamic_update_slice | solution.py:578
  103.5 2.2 %collective-permute-start.12 = (bf16[4,480,128]{2,1,0:T(8,128)(2,1)}, bf16[4,480,128]{2,1,0:T(8,128)(2,1)S(1)}, u32[]{:S(2)}, u32[]{:S(2)}) collective-permute-start(bf16[4,480,128]{2,1,0:T(8,128)(2,1)} %fusion.3), channel_id=1, source_target_pairs={{0,7},{1,0},{2,1},{3,2},{4,3},{5,4},{6,5},{7,6},{8,15},{9,8},{10,9... | collective-permute-start | bytes 1474568 | tf_op jit(solution)/shard_map/ppermute | solution.py:569
  105.7 1.7 %fusion.2 = bf16[4,480,128]{2,1,0:T(8,128)(2,1)} fusion(bf16[4,480,128]{2,1,0:T(8,128)(2,1)} %get-tuple-element.63, bf16[2,480,128]{2,1,0:T(8,128)(2,1)S(1)} %collective-permute-done.8), kind=kLoop, calls=%fused_computation.11 | loop fusion | flops 491520 | bytes 737280 | tf_op jit(solution)/shard_map/dynamic_update_slice | solution.py:578
  107.4 5.7 %collective-permute-done.12 = bf16[4,480,128]{2,1,0:T(8,128)(2,1)S(1)} collective-permute-done((bf16[4,480,128]{2,1,0:T(8,128)(2,1)}, bf16[4,480,128]{2,1,0:T(8,128)(2,1)S(1)}, u32[]{:S(2)}, u32[]{:S(2)}) %collective-permute-start.12) | collective-permute-done | bytes 491552 | tf_op jit(solution)/shard_map/ppermute | solution.py:569
  113.2 1.2 add_convert_fusion.1
  114.3 2.8 %collective-permute-start.13 = (bf16[4,480,128]{2,1,0:T(8,128)(2,1)S(1)}, bf16[4,480,128]{2,1,0:T(8,128)(2,1)S(1)}, u32[]{:S(2)}, u32[]{:S(2)}) collective-permute-start(bf16[4,480,128]{2,1,0:T(8,128)(2,1)S(1)} %add_convert_fusion.1), channel_id=1, source_target_pairs={{0,7},{1,0},{2,1},{3,2},{4,3},{5,4},{6,5},{7,6},{8,15},{9,8},{10,9... | collective-permute-start | bytes 1474568 | tf_op jit(solution)/shard_map/ppermute | solution.py:569
  117.1 0.2 collective-permute-done.9
  117.3 0.1 add_convert_fusion.3
  117.6 5.4 %collective-permute-done.13 = bf16[4,480,128]{2,1,0:T(8,128)(2,1)S(1)} collective-permute-done((bf16[4,480,128]{2,1,0:T(8,128)(2,1)S(1)}, bf16[4,480,128]{2,1,0:T(8,128)(2,1)S(1)}, u32[]{:S(2)}, u32[]{:S(2)}) %collective-permute-start.13) | collective-permute-done | bytes 491552 | tf_op jit(solution)/shard_map/ppermute | solution.py:569
  122.9 0.1 add_convert_fusion
  123.1 4.0 %collective-permute-done.10 = bf16[4,480,128]{2,1,0:T(8,128)(2,1)S(1)} collective-permute-done((bf16[4,480,128]{2,1,0:T(8,128)(2,1)S(1)}, bf16[4,480,128]{2,1,0:T(8,128)(2,1)S(1)}, u32[]{:S(2)}, u32[]{:S(2)}) %collective-permute-start.10) | collective-permute-done | bytes 491552 | tf_op jit(solution)/shard_map/ppermute | solution.py:565
  127.2 6.0 %all-gather.3.cloned.1.call-done = bf16[1024,8,128]{2,1,0:T(8,128)(2,1)} async-done(((bf16[32,8,128]{2,1,0:T(8,128)(2,1)}), bf16[1024,8,128]{2,1,0:T(8,128)(2,1)}) %all-gather.3.cloned.1.call-update) | async-done | bytes 2097168 | tf_op jit(solution)/shard_map/all_gather | solution.py:647
  133.2 1.3 collective-permute-start.14
  134.4 1.8 %collective-permute-start.15 = (bf16[4,480,128]{2,1,0:T(8,128)(2,1)S(1)}, bf16[4,480,128]{2,1,0:T(8,128)(2,1)}, u32[]{:S(2)}, u32[]{:S(2)}) collective-permute-start(bf16[4,480,128]{2,1,0:T(8,128)(2,1)S(1)} %add_convert_fusion), channel_id=1, source_target_pairs={{0,7},{1,0},{2,1},{3,2},{4,3},{5,4},{6,5},{7,6},{8,15},{9,8},{10,9... | collective-permute-start | bytes 1474568 | tf_op jit(solution)/shard_map/ppermute | solution.py:569
  136.2 8.5 %assemble_cache.1 = bf16[32,160,512]{2,1,0:T(8,128)(2,1)} custom-call(s32[1]{0:T(128)} %bitcast.3.me, bf16[32,160,512]{2,1,0:T(8,128)(2,1)} %all-to-all-done.cache_ref, bf16[32,32,8,128]{3,2,1,0:T(8,128)(2,1)} %bitcast.9), custom_call_target="tpu_custom_call" | custom-call | tf_op jit(solution)/shard_map/assemble_cache/pallas_call | solution.py:541
  144.7 2.9 %collective-permute-done.14.up_ref = bf16[4,480,128]{2,1,0:T(8,128)(2,1)S(1)} collective-permute-done((bf16[4,480,128]{2,1,0:T(8,128)(2,1)S(1)}, bf16[4,480,128]{2,1,0:T(8,128)(2,1)S(1)}, u32[]{:S(2)}, u32[]{:S(2)}) %collective-permute-start.14) | collective-permute-done | bytes 491552 | tf_op jit(solution)/shard_map/ppermute | solution.py:565
  147.6 0.8 copy-done.9
  148.4 2.6 %finish_rows.1 = bf16[768,320]{1,0:T(8,128)(2,1)} custom-call(s32[1]{0:T(128)} %bitcast.parity.me, bf16[4,480,128]{2,1,0:T(8,128)(2,1)} %get-tuple-element.60.own_ref, bf16[4,480,128]{2,1,0:T(8,128)(2,1)} %copy-done.9, bf16[4,480,128]{2,1,0:T(8,128)(2,1)} %collective-permute-done.15.down_ref, bf16[768,320]{1,0:T(8,128)(2,1)} %bitcast.8), custom_call_target="tpu_custom_call" | custom-call | tf_op jit(solution)/shard_map/finish_rows/pallas_call | solution.py:129
  (56 shorter events, 0.7 us)
Async XLA Ops:
  7.2 36.6 %copy-start = (bf16[2560,320]{0,1:T(8,128)(2,1)S(1)}, bf16[2560,320]{0,1:T(8,128)(2,1)}, u32[]{:S(2)}) copy-start(bf16[2560,320]{0,1:T(8,128)(2,1)} %param.12) | copy-start | bytes 4915204
  9.3 16.8 %collective-permute-start.1 = (bf16[4,480,128]{2,1,0:T(8,128)(2,1)}, bf16[4,480,128]{2,1,0:T(8,128)(2,1)S(1)}, u32[]{:S(2)}, u32[]{:S(2)}) collective-permute-start(bf16[4,480,128]{2,1,0:T(8,128)(2,1)} %pack_rows.1.refs_0_), channel_id=1, source_target_pairs={{0,7},{1,0},{2,1},{3,2},{4,3},{5,4},{6,5},{7,6},{8,15},{9,8},{10,9... | collective-permute-start | bytes 1474568 | tf_op jit(solution)/shard_map/ppermute | solution.py:569
  15.9 13.2 %collective-permute-start = (bf16[4,480,128]{2,1,0:T(8,128)(2,1)}, bf16[4,480,128]{2,1,0:T(8,128)(2,1)S(1)}, u32[]{:S(2)}, u32[]{:S(2)}) collective-permute-start(bf16[4,480,128]{2,1,0:T(8,128)(2,1)} %pack_rows.1.refs_0_), channel_id=1, source_target_pairs={{0,1},{1,2},{2,3},{3,4},{4,5},{5,6},{6,7},{7,0},{8,9},{9,10},{10,1... | collective-permute-start | bytes 1474568 | tf_op jit(solution)/shard_map/ppermute | solution.py:565
  16.5 6.6 %copy-start.15 = (s32[32]{0:T(128)}, s32[32]{0:T(128)S(1)}, u32[]{:S(2)}) copy-start(s32[32]{0:T(128)S(1)} %and_select_fusion.2.destination) | copy-start | bytes 388
  17.2 13.3 %copy-start.16 = (bf16[160,2560]{1,0:T(8,128)(2,1)S(1)}, bf16[160,2560]{1,0:T(8,128)(2,1)}, u32[]{:S(2)}) copy-start(bf16[160,2560]{1,0:T(8,128)(2,1)} %param.13) | copy-start | bytes 2457604
  17.2 13.4 %copy-start.17 = (f32[2560]{0:T(1024)S(1)}, f32[2560]{0:T(1024)}, u32[]{:S(2)}) copy-start(f32[2560]{0:T(1024)} %param.11) | copy-start | bytes 30724
  26.1 6.4 %copy-start.3 = (bf16[4,480,128]{2,1,0:T(8,128)(2,1)}, bf16[4,480,128]{2,1,0:T(8,128)(2,1)S(1)}, u32[]{:S(2)}) copy-start(bf16[4,480,128]{2,1,0:T(8,128)(2,1)S(1)} %collective-permute-done.1.refs_1_) | copy-start | bytes 1474564
  29.1 3.4 %copy-start.4 = (bf16[4,480,128]{2,1,0:T(8,128)(2,1)}, bf16[4,480,128]{2,1,0:T(8,128)(2,1)S(1)}, u32[]{:S(2)}) copy-start(bf16[4,480,128]{2,1,0:T(8,128)(2,1)S(1)} %collective-permute-done.refs_7_) | copy-start | bytes 1474564
  29.1 13.1 %collective-permute-start.3 = (bf16[4,480,128]{2,1,0:T(8,128)(2,1)S(1)}, bf16[4,480,128]{2,1,0:T(8,128)(2,1)}, u32[]{:S(2)}, u32[]{:S(2)}) collective-permute-start(bf16[4,480,128]{2,1,0:T(8,128)(2,1)S(1)} %collective-permute-done.1.refs_1_), channel_id=1, source_target_pairs={{0,7},{1,0},{2,1},{3,2},{4,3},{5,4},{6,5},{7,6},{8,15},{9,8},{10,9... | collective-permute-start | bytes 1474568 | tf_op jit(solution)/shard_map/ppermute | solution.py:569
  29.5 12.7 %collective-permute-start.2 = (bf16[4,480,128]{2,1,0:T(8,128)(2,1)S(1)}, bf16[4,480,128]{2,1,0:T(8,128)(2,1)S(1)}, u32[]{:S(2)}, u32[]{:S(2)}) collective-permute-start(bf16[4,480,128]{2,1,0:T(8,128)(2,1)S(1)} %collective-permute-done.refs_7_), channel_id=1, source_target_pairs={{0,1},{1,2},{2,3},{3,4},{4,5},{5,6},{6,7},{7,0},{8,9},{9,10},{10,1... | collective-permute-start | bytes 1474568 | tf_op jit(solution)/shard_map/ppermute | solution.py:565
  32.5 94.7 %all-to-all-start = ((bf16[32,160,512]{2,1,0:T(8,128)(2,1)}), bf16[32,160,512]{2,1,0:T(8,128)(2,1)}, u32[]{:S(2)}, u32[]{:S(2)}) async-start(bf16[32,160,512]{2,1,0:T(8,128)(2,1)} %order_cache.1), calls=%async_computation | async-start | bytes 10485760 | tf_op jit(solution)/shard_map/all_to_all | solution.py:561
  42.0 91.1 %all-gather.3.cloned.1.call-start = ((), (), s32[]{:S(2)}) async-start(), calls=%async_computation.1 | async-start | bytes 2162688 | tf_op jit(solution)/shard_map/all_gather | solution.py:647
  42.1 10.8 %copy-start.5 = (bf16[4,480,128]{2,1,0:T(8,128)(2,1)}, bf16[4,480,128]{2,1,0:T(8,128)(2,1)S(1)}, u32[]{:S(2)}) copy-start(bf16[4,480,128]{2,1,0:T(8,128)(2,1)S(1)} %collective-permute-done.2.refs_6_) | copy-start | bytes 1474564
  42.1 11.3 %collective-permute-start.5 = (bf16[4,480,128]{2,1,0:T(8,128)(2,1)}, bf16[4,480,128]{2,1,0:T(8,128)(2,1)S(1)}, u32[]{:S(2)}, u32[]{:S(2)}) collective-permute-start(bf16[4,480,128]{2,1,0:T(8,128)(2,1)} %collective-permute-done.3.refs_2_), channel_id=1, source_target_pairs={{0,7},{1,0},{2,1},{3,2},{4,3},{5,4},{6,5},{7,6},{8,15},{9,8},{10,9... | collective-permute-start | bytes 1474568 | tf_op jit(solution)/shard_map/ppermute | solution.py:569
  43.5 12.8 %collective-permute-start.4 = (bf16[4,480,128]{2,1,0:T(8,128)(2,1)S(1)}, bf16[4,480,128]{2,1,0:T(8,128)(2,1)S(1)}, u32[]{:S(2)}, u32[]{:S(2)}) collective-permute-start(bf16[4,480,128]{2,1,0:T(8,128)(2,1)S(1)} %collective-permute-done.2.refs_6_), channel_id=1, source_target_pairs={{0,1},{1,2},{2,3},{3,4},{4,5},{5,6},{6,7},{7,0},{8,9},{9,10},{10,1... | collective-permute-start | bytes 1474568 | tf_op jit(solution)/shard_map/ppermute | solution.py:565
  46.9 12.9 %copy-start.13 = (s32[32]{0:T(128)S(1)}, s32[32]{0:T(128)}, u32[]{:S(2)}) copy-start(s32[32]{0:T(128)} %lengths.3) | copy-start | bytes 388
  46.9 13.0 %copy-start.14 = (s32[32,4]{0,1:T(4,128)S(1)}, s32[32,4]{0,1:T(4,128)}, u32[]{:S(2)}) copy-start(s32[32,4]{0,1:T(4,128)} %param.18) | copy-start | bytes 1540
  46.9 15.1 %copy-start.12 = (s32[32,24]{0,1:T(8,128)S(1)}, s32[32,24]{0,1:T(8,128)}, u32[]{:S(2)}) copy-start(s32[32,24]{0,1:T(8,128)} %param.17) | copy-start | bytes 9220
  53.5 11.9 %copy-start.1 = (bf16[4,480,128]{2,1,0:T(8,128)(2,1)}, bf16[4,480,128]{2,1,0:T(8,128)(2,1)S(1)}, u32[]{:S(2)}) copy-start(bf16[4,480,128]{2,1,0:T(8,128)(2,1)S(1)} %collective-permute-done.5.refs_3_) | copy-start | bytes 1474564
  56.4 9.0 %copy-start.2 = (bf16[4,480,128]{2,1,0:T(8,128)(2,1)}, bf16[4,480,128]{2,1,0:T(8,128)(2,1)S(1)}, u32[]{:S(2)}) copy-start(bf16[4,480,128]{2,1,0:T(8,128)(2,1)S(1)} %collective-permute-done.4.refs_5_) | copy-start | bytes 1474564
  57.2 8.1 %collective-permute-start.6 = (bf16[2,480,128]{2,1,0:T(8,128)(2,1)}, bf16[2,480,128]{2,1,0:T(8,128)(2,1)S(1)}, u32[]{:S(2)}, u32[]{:S(2)}) collective-permute-start(bf16[2,480,128]{2,1,0:T(8,128)(2,1)} %slice.12), channel_id=1, source_target_pairs={{0,1},{1,2},{2,3},{3,4},{4,5},{5,6},{6,7},{7,0},{8,9},{9,10},{10,1... | collective-permute-start | bytes 737288 | tf_op jit(solution)/shard_map/ppermute | solution.py:565
  57.2 8.1 %collective-permute-start.7 = (bf16[2,480,128]{2,1,0:T(8,128)(2,1)S(1)}, bf16[2,480,128]{2,1,0:T(8,128)(2,1)S(1)}, u32[]{:S(2)}, u32[]{:S(2)}) collective-permute-start(bf16[2,480,128]{2,1,0:T(8,128)(2,1)S(1)} %slice.13), channel_id=1, source_target_pairs={{0,7},{1,0},{2,1},{3,2},{4,3},{5,4},{6,5},{7,6},{8,15},{9,8},{10,9... | collective-permute-start | bytes 737288 | tf_op jit(solution)/shard_map/ppermute | solution.py:569
  65.3 0.7 copy-start.10
  65.3 0.8 copy-start.11
  96.1 21.3 %copy-start.8 = (bf16[4,480,128]{2,1,0:T(8,128)(2,1)S(1)}, bf16[4,480,128]{2,1,0:T(8,128)(2,1)}, u32[]{:S(2)}) copy-start(bf16[4,480,128]{2,1,0:T(8,128)(2,1)} %get-tuple-element.62) | copy-start | bytes 1474564
  96.1 26.8 %copy-start.7 = (bf16[4,480,128]{2,1,0:T(8,128)(2,1)S(1)}, bf16[4,480,128]{2,1,0:T(8,128)(2,1)}, u32[]{:S(2)}) copy-start(bf16[4,480,128]{2,1,0:T(8,128)(2,1)} %get-tuple-element.65) | copy-start | bytes 1474564
  96.1 5.7 %collective-permute-start.11 = (bf16[2,480,128]{2,1,0:T(8,128)(2,1)}, bf16[2,480,128]{2,1,0:T(8,128)(2,1)S(1)}, u32[]{:S(2)}, u32[]{:S(2)}) collective-permute-start(bf16[2,480,128]{2,1,0:T(8,128)(2,1)} %get-tuple-element.68), channel_id=1, source_target_pairs={{0,7},{1,0},{2,1},{3,2},{4,3},{5,4},{6,5},{7,6},{8,15},{9,8},{10,9... | collective-permute-start | bytes 737288 | tf_op jit(solution)/shard_map/ppermute | solution.py:569
  97.3 8.4 %collective-permute-start.8 = (bf16[2,480,128]{2,1,0:T(8,128)(2,1)}, bf16[2,480,128]{2,1,0:T(8,128)(2,1)S(1)}, u32[]{:S(2)}, u32[]{:S(2)}) collective-permute-start(bf16[2,480,128]{2,1,0:T(8,128)(2,1)} %get-tuple-element.64), channel_id=1, source_target_pairs={{0,1},{1,2},{2,3},{3,4},{4,5},{5,6},{6,7},{7,0},{8,9},{9,10},{10,1... | collective-permute-start | bytes 737288 | tf_op jit(solution)/shard_map/ppermute | solution.py:565
  103.5 23.5 %copy-start.6 = (bf16[4,480,128]{2,1,0:T(8,128)(2,1)S(1)}, bf16[4,480,128]{2,1,0:T(8,128)(2,1)}, u32[]{:S(2)}) copy-start(bf16[4,480,128]{2,1,0:T(8,128)(2,1)} %get-tuple-element.61) | copy-start | bytes 1474564
  103.5 9.6 %collective-permute-start.12 = (bf16[4,480,128]{2,1,0:T(8,128)(2,1)}, bf16[4,480,128]{2,1,0:T(8,128)(2,1)S(1)}, u32[]{:S(2)}, u32[]{:S(2)}) collective-permute-start(bf16[4,480,128]{2,1,0:T(8,128)(2,1)} %fusion.3), channel_id=1, source_target_pairs={{0,7},{1,0},{2,1},{3,2},{4,3},{5,4},{6,5},{7,6},{8,15},{9,8},{10,9... | collective-permute-start | bytes 1474568 | tf_op jit(solution)/shard_map/ppermute | solution.py:569
  107.4 9.9 %collective-permute-start.9 = (bf16[4,480,128]{2,1,0:T(8,128)(2,1)}, bf16[4,480,128]{2,1,0:T(8,128)(2,1)S(1)}, u32[]{:S(2)}, u32[]{:S(2)}) collective-permute-start(bf16[4,480,128]{2,1,0:T(8,128)(2,1)} %fusion.2), channel_id=1, source_target_pairs={{0,1},{1,2},{2,3},{3,4},{4,5},{5,6},{6,7},{7,0},{8,9},{9,10},{10,1... | collective-permute-start | bytes 1474568 | tf_op jit(solution)/shard_map/ppermute | solution.py:565
  114.3 8.6 %collective-permute-start.13 = (bf16[4,480,128]{2,1,0:T(8,128)(2,1)S(1)}, bf16[4,480,128]{2,1,0:T(8,128)(2,1)S(1)}, u32[]{:S(2)}, u32[]{:S(2)}) collective-permute-start(bf16[4,480,128]{2,1,0:T(8,128)(2,1)S(1)} %add_convert_fusion.1), channel_id=1, source_target_pairs={{0,7},{1,0},{2,1},{3,2},{4,3},{5,4},{6,5},{7,6},{8,15},{9,8},{10,9... | collective-permute-start | bytes 1474568 | tf_op jit(solution)/shard_map/ppermute | solution.py:569
  117.5 9.6 %collective-permute-start.10 = (bf16[4,480,128]{2,1,0:T(8,128)(2,1)S(1)}, bf16[4,480,128]{2,1,0:T(8,128)(2,1)S(1)}, u32[]{:S(2)}, u32[]{:S(2)}) collective-permute-start(bf16[4,480,128]{2,1,0:T(8,128)(2,1)S(1)} %add_convert_fusion.3), channel_id=1, source_target_pairs={{0,1},{1,2},{2,3},{3,4},{4,5},{5,6},{6,7},{7,0},{8,9},{9,10},{10,1... | collective-permute-start | bytes 1474568 | tf_op jit(solution)/shard_map/ppermute | solution.py:565
  133.2 14.4 %collective-permute-start.14 = (bf16[4,480,128]{2,1,0:T(8,128)(2,1)S(1)}, bf16[4,480,128]{2,1,0:T(8,128)(2,1)S(1)}, u32[]{:S(2)}, u32[]{:S(2)}) collective-permute-start(bf16[4,480,128]{2,1,0:T(8,128)(2,1)S(1)} %add_convert_fusion.2), channel_id=1, source_target_pairs={{0,1},{1,2},{2,3},{3,4},{4,5},{5,6},{6,7},{7,0},{8,9},{9,10},{10,1... | collective-permute-start | bytes 1474568 | tf_op jit(solution)/shard_map/ppermute | solution.py:565
  134.4 13.2 %collective-permute-start.15 = (bf16[4,480,128]{2,1,0:T(8,128)(2,1)S(1)}, bf16[4,480,128]{2,1,0:T(8,128)(2,1)}, u32[]{:S(2)}, u32[]{:S(2)}) collective-permute-start(bf16[4,480,128]{2,1,0:T(8,128)(2,1)S(1)} %add_convert_fusion), channel_id=1, source_target_pairs={{0,7},{1,0},{2,1},{3,2},{4,3},{5,4},{6,5},{7,6},{8,15},{9,8},{10,9... | collective-permute-start | bytes 1474568 | tf_op jit(solution)/shard_map/ppermute | solution.py:569
  147.6 0.8 copy-start.9
Sparse Core Ops, SparseCore 0:
  78.8 54.3 all-gather.2

commit v8 on v6

--- a/solution.py
+++ b/solution.py
@@ -468,18 +468,18 @@
         ),
         compiler_params=pltpu.CompilerParams(vmem_limit_bytes=VMEM_LIMIT),
         cost_estimate=pl.CostEstimate(
-            flops=1_000_000_000, transcendentals=0, bytes_accessed=10_000_000
+            flops=30_000_000_000, transcendentals=0, bytes_accessed=10_000_000
         ),
         name="verify_layer",
     )(lengths, accepted, destination, *parts, w, wo, kv_cache, *tables)
 
 
-def assemble_kernel(me, cache_ref, extra_ref, o_ref):
+def assemble_kernel(cache_ref, extra_ref, o_ref):
     place_row = lax.broadcasted_iota(jnp.int32, (EXTRA, CACHE), 0)
     place_column = lane_index((EXTRA, CACHE))
     upper = lane_index((1, LANES)) >= 64
     for i in range(cache_ref.shape[0]):
-        extra = extra_ref[i, 0]
+        extra = extra_ref[i]
         wide = extra.astype(F32)
         length = wide[DEPTH : DEPTH + 1] * 16.0 + wide[DEPTH + 1 : DEPTH + 2]
         length = jnp.where(upper, length, swap_halves(length)).astype(jnp.int32)
@@ -499,21 +499,18 @@
         o_ref[i, LANES:] = cache_ref[i, LANES:] * live + rest.astype(BF)
 
 
-def assemble_cache(cached, extra, me):
+def assemble_cache(cached, extra):
     step = 4
-    cache_spec = pl.BlockSpec((step,) + cached.shape[1:], lambda s, me: (s, 0, 0))
-    extra_spec = pl.BlockSpec((step, 1, EXTRA, LANES), lambda s, me: (s, me[0], 0, 0))
+    cache_spec = pl.BlockSpec((step,) + cached.shape[1:], lambda s: (s, 0, 0))
+    extra_spec = pl.BlockSpec((step,) + extra.shape[1:], lambda s: (s, 0, 0))
     return pl.pallas_call(
         assemble_kernel,
         out_shape=jax.ShapeDtypeStruct(cached.shape, BF),
-        grid_spec=pltpu.PrefetchScalarGridSpec(
-            num_scalar_prefetch=1,
-            grid=(cached.shape[0] // step,),
-            in_specs=[cache_spec, extra_spec],
-            out_specs=cache_spec,
-        ),
+        grid=(cached.shape[0] // step,),
+        in_specs=[cache_spec, extra_spec],
+        out_specs=cache_spec,
         name="assemble_cache",
-    )(me, cached, extra)
+    )(cached, extra)
 
 
 def spread_heads(heads):
@@ -547,7 +544,6 @@
     half = N_TP // 2
     up = go_up(targets[half])
     down = go_down(targets[N_TP])
-    extra = lax.all_gather(extra, "req", axis=0, tiled=False)
     for step in range(1, half):
         above, below = targets[half - step], targets[half + step]
         if step == 1:
@@ -555,12 +551,14 @@
             below = add_blocks(below, down, HALF_BLOCKS)
         else:
             above, below = add_up(above, up), add_up(below, down)
-        if step == 3:
+        if step == 2:
             above, below, cached, extra = lax.optimization_barrier(
                 (above, below, cached, extra)
             )
-            me = lax.axis_index("req").astype(jnp.int32).reshape(1)
-            new_cache = assemble_cache(cached, extra, me)
+            extra = exchange(extra)
+        if step == 3:
+            above, below, extra = lax.optimization_barrier((above, below, extra))
+            new_cache = assemble_cache(cached, extra)
         up = go_up(above)
         down = go_down(below)
     up, down, new_cache = lax.optimization_barrier((up, down, new_cache))
@@ -583,24 +581,26 @@
     ordered = order_cache(kv_cache, send_order)
     below, above = go_up(parts[0]), go_down(parts[0])
 
-    below, above, w_keyval, ordered = barrier((below, above, w_keyval, ordered))
+    below, above, w_keyval, w_query, ordered = barrier(
+        (below, above, w_keyval, w_query, ordered)
+    )
     parts[7], parts[1] = below, above
     gain = norm_gain[:, None]
     wkv = lax.dot_general(
         w_keyval, spread_heads(2), (((0,), (0,)), ((), ())), preferred_element_type=F32
     )
     wkv = (wkv * gain).astype(BF)
+    wq = (jnp.dot(w_query, spread_heads(GROUP), preferred_element_type=F32) * gain).astype(BF)
     ordered, wkv = barrier((ordered, wkv))
     cached = exchange(ordered)
-    below, above = go_up(below), go_down(above)
-
-    below, above, w_query, wkv = barrier((below, above, w_query, wkv))
-    parts[6], parts[2] = below, above
-    wq = (jnp.dot(w_query, spread_heads(GROUP), preferred_element_type=F32) * gain).astype(BF)
     weights = arrange_weights(wq, wkv, w_out, me)
     below, above = go_up(below), go_down(above)
 
-    below, above, weights, parents = barrier((below, above, weights, parents))
+    below, above, weights = barrier((below, above, weights))
+    parts[6], parts[2] = below, above
+    below, above = go_up(below), go_down(above)
+
+    below, above, parents = barrier((below, above, parents))
     parts[5], parts[3] = below, above
     tables = prepare_tables(parents, lengths)
     parts[4] = go_up(below[:HALF_BLOCKS])

time: 166 us -> 152 us (0.916); the launches traced: 165 us -> 149 us
  waiting for transfers between devices: 49 us -> 34 us
  between operations: 14.3 us -> 0.83 us
  starting transfers between devices: 32 us -> 41.7 us
  other arithmetic: 7.19 us -> 10.9 us
    all_gather x1 -> x0, waiting for transfers between devices: 17.6 us -> none  [scatter_ring(): extra = lax.all_gather(extra, 'req', axis=0, tiled=False)]
    all_to_all x1 -> x2, waiting for transfers between devices: 0.01 us -> 11.2 us  [exchange(): lax.all_to_all(values, 'req', split_axis=0, concat_axis=0, tiled=True)]
    all_to_all x1 -> x2, starting transfers between devices: 9.56 us -> 20.7 us  [exchange(): lax.all_to_all(values, 'req', split_axis=0, concat_axis=0, tiled=True)]
    ppermute x8, waiting for transfers between devices: 18.5 us -> 11.9 us  [go_down(): lax.ppermute(values, 'tp', [(i, (i - 1) % N_TP) for i in range(N_TP)])]
    convert_element_type x4, other arithmetic: 1.55 us -> 5.16 us  [add_up(): return (a.astype(F32) + b.astype(F32)).astype(BF)]
    ppermute x8, waiting for transfers between devices: 12.9 us -> 10.9 us  [go_up(): lax.ppermute(values, 'tp', [(i, (i + 1) % N_TP) for i in range(N_TP)])]
  transfers between devices with their start and end apart: 18 -> 18, of which waited for: 11 -> 11; matrix products, arithmetic and copies ran while one was open for 9% -> 12% of each run, Pallas kernels for 29% -> 32%
where the time goes in v8:
time: 152 us; the launch traced here: 149 us
  Pallas kernels  53.2 us (35%)
  starting transfers between devices  41.7 us (27%)
  waiting for transfers between devices  34 us (22%)
  other arithmetic  10.9 us (7%)
  matrix products  5 us (3%)
  local copies, waits for them, and re-layouts  3.76 us (2%)
    pallas_call x1, Pallas kernels, verify_layer(): pl.pallas_call(layer_kernel, out_shape=[jax.ShapeDtypeStruct((HALF_BLOCKS...  25.5 us
    all_to_all x2, starting transfers between devices, exchange(): lax.all_to_all(values, 'req', split_axis=0, concat_axis=0, tiled=True)  20.7 us
    ppermute x8, starting transfers between devices, go_down(): lax.ppermute(values, 'tp', [(i, (i - 1) % N_TP) for i in range(N_TP)])  18.9 us
    ppermute x8, waiting for transfers between devices, go_down(): lax.ppermute(values, 'tp', [(i, (i - 1) % N_TP) for i in range(N_TP)])  11.9 us
    all_to_all x2, waiting for transfers between devices, exchange(): lax.all_to_all(values, 'req', split_axis=0, concat_axis=0, tiled=True)  11.2 us
    ppermute x8, waiting for transfers between devices, go_up(): lax.ppermute(values, 'tp', [(i, (i + 1) % N_TP) for i in range(N_TP)])  10.9 us
    pallas_call x1, Pallas kernels, assemble_cache(): pl.pallas_call(assemble_kernel, out_shape=jax.ShapeDtypeStruct(cached.sha...  8.49 us
    pallas_call x1, Pallas kernels, arrange_weights(): pl.pallas_call(arrange_kernel, out_shape=(jax.ShapeDtypeStruct((D, (GROUP...  5.98 us
  transfers between devices with their start and end apart: 18, of which 11 were waited for; matrix products, arithmetic and copies ran while one was open for 12% of the time, Pallas kernels for 32%

profile of v8, /device:TPU:1, one launch (start us, length us, event | category | flops | bytes accessed | tf_op | source)
XLA Modules:
  0.0 149.4 jit_solution(2899432503647084904)
XLA Ops:
  0.6 2.1 %pack_rows.1.refs_0_ = bf16[4,480,128]{2,1,0:T(8,128)(2,1)} custom-call(s32[1]{0:T(128)} %bitcast.parity.me, bf16[768,320]{1,0:T(8,128)(2,1)} %bitcast.5), custom_call_target="tpu_custom_call" | custom-call | tf_op jit(solution)/shard_map/pack_rows/pallas_call | solution.py:73
  2.8 6.6 %collective-permute-start.1 = (bf16[4,480,128]{2,1,0:T(8,128)(2,1)}, bf16[4,480,128]{2,1,0:T(8,128)(2,1)S(1)}, u32[]{:S(2)}, u32[]{:S(2)}) collective-permute-start(bf16[4,480,128]{2,1,0:T(8,128)(2,1)} %pack_rows.1.refs_0_), channel_id=1, source_target_pairs={{0,7},{1,0},{2,1},{3,2},{4,3},{5,4},{6,5},{7,6},{8,15},{9,8},{10,9... | collective-permute-start | bytes 1474568 | tf_op jit(solution)/shard_map/ppermute | solution.py:531
  9.3 0.7 and_select_fusion.2.destination
  10.0 0.7 select_reduce_fusion.order
  10.7 6.0 %order_cache.1 = bf16[32,160,512]{2,1,0:T(8,128)(2,1)} custom-call(s32[32]{0:T(128)} %select_reduce_fusion.order, bf16[32,160,512]{2,1,0:T(8,128)(2,1)} %refs_11_.1), custom_call_target="tpu_custom_call" | custom-call | tf_op jit(solution)/shard_map/order_cache/pallas_call | solution.py:257
  16.7 2.9 %collective-permute-done.1.refs_1_ = bf16[4,480,128]{2,1,0:T(8,128)(2,1)S(1)} collective-permute-done((bf16[4,480,128]{2,1,0:T(8,128)(2,1)}, bf16[4,480,128]{2,1,0:T(8,128)(2,1)S(1)}, u32[]{:S(2)}, u32[]{:S(2)}) %collective-permute-start.1) | collective-permute-done | bytes 491552 | tf_op jit(solution)/shard_map/ppermute | solution.py:531
  19.5 3.0 %collective-permute-done.refs_7_ = bf16[4,480,128]{2,1,0:T(8,128)(2,1)S(1)} collective-permute-done((bf16[4,480,128]{2,1,0:T(8,128)(2,1)}, bf16[4,480,128]{2,1,0:T(8,128)(2,1)S(1)}, u32[]{:S(2)}, u32[]{:S(2)}) %collective-permute-start) | collective-permute-done | bytes 491552 | tf_op jit(solution)/shard_map/ppermute | solution.py:527
  22.5 0.4 collective-permute-start.3
  22.9 1.1 collective-permute-start.2
  24.0 1.9 %fusion.wkv_ref = bf16[2560,256]{1,0:T(8,128)(2,1)} fusion(bf16[160,2560]{1,0:T(8,128)(2,1)S(1)} %copy-done.11, f32[2560]{0:T(1024)S(1)} %copy-done.16, s32[160]{0:T(256)S(1)} %fusion.16), kind=kOutput, calls=%fused_computation.2 | convolution fusion | flops 211066880 | bytes 2140800 | tf_op jit(solution)/shard_map/dot_general | solution.py:589
  25.9 3.1 %multiply_convert_fusion.wq_ref = bf16[2560,512]{1,0:T(8,128)(2,1)} fusion(bf16[2560,320]{0,1:T(8,128)(2,1)S(1)} %copy-done, f32[2560]{0:T(1024)S(1)} %copy-done.16, s32[320]{0:T(512)S(1)} %fusion.10), kind=kOutput, calls=%fused_computation | convolution fusion | flops 841646080 | bytes 4271360 | tf_op jit(solution)/shard_map/dot_general | solution.py:593
  29.0 6.0 %arrange_weights.1 = (bf16[2560,768]{1,0:T(8,128)(2,1)}, bf16[512,2560]{1,0:T(8,128)(2,1)}) custom-call(s32[1]{0:T(128)} %bitcast.parity.me, bf16[2560,512]{1,0:T(8,128)(2,1)} %multiply_convert_fusion.wq_ref, bf16[2560,256]{1,0:T(8,128)(2,1)} %fusion.wkv_ref, bf16[320,2560]{1,0:T(8,128)(2,1)} %wo_ref.1), custom_call_target="tpu_custom_call" | custom-call | tf_op jit(solution)/shard_map/arrange_weights/pallas_call | solution.py:182
  35.0 0.1 collective-permute-done.2.refs_6_
  35.1 1.6 %collective-permute-start.5 = (bf16[4,480,128]{2,1,0:T(8,128)(2,1)S(1)}, bf16[4,480,128]{2,1,0:T(8,128)(2,1)S(1)}, u32[]{:S(2)}, u32[]{:S(2)}) collective-permute-start(bf16[4,480,128]{2,1,0:T(8,128)(2,1)S(1)} %collective-permute-done.3.refs_2_), channel_id=1, source_target_pairs={{0,7},{1,0},{2,1},{3,2},{4,3},{5,4},{6,5},{7,6},{8,15},{9,8},{10,9... | collective-permute-start | bytes 1474568 | tf_op jit(solution)/shard_map/ppermute | solution.py:531
  36.7 10.3 %all-to-all-start = ((bf16[32,160,512]{2,1,0:T(8,128)(2,1)}), bf16[32,160,512]{2,1,0:T(8,128)(2,1)}, u32[]{:S(2)}, u32[]{:S(2)}) async-start(bf16[32,160,512]{2,1,0:T(8,128)(2,1)} %order_cache.1), calls=%async_computation | async-start | bytes 10485760 | tf_op jit(solution)/shard_map/all_to_all | solution.py:523
  47.2 1.3 collective-permute-done.4.refs_5_
  48.6 2.7 %collective-permute-start.7 = (bf16[2,480,128]{2,1,0:T(8,128)(2,1)S(1)}, bf16[2,480,128]{2,1,0:T(8,128)(2,1)}, u32[]{:S(2)}, u32[]{:S(2)}) collective-permute-start(bf16[2,480,128]{2,1,0:T(8,128)(2,1)S(1)} %slice.13), channel_id=1, source_target_pairs={{0,7},{1,0},{2,1},{3,2},{4,3},{5,4},{6,5},{7,6},{8,15},{9,8},{10,9... | collective-permute-start | bytes 737288 | tf_op jit(solution)/shard_map/ppermute | solution.py:531
  51.3 0.1 copy.16
  51.4 0.7 reshape.146.accepted
  52.1 0.6 stack.2.step_ref
  52.7 0.8 multiply_sine_fusion
  53.5 0.7 copy.17.parents_ref
  54.1 2.6 %prepare_tables.1 = (f32[32,24,128]{2,1,0:T(8,128)}, f32[32,24,128]{2,1,0:T(8,128)}, f32[32,24,128]{2,1,0:T(8,128)}) custom-call(s32[32,24]{1,0:T(8,128)} %copy.17.parents_ref, f32[32,128]{1,0:T(8,128)} %get-tuple-element.81.cos_ref, f32[32,128]{1,0:T(8,128)} %get-tuple-element.80.sin_ref, f32[8,128]{1,0:T(8,128)} %stack.2.step_ref), custom_call_target="tpu_custom_call" | custom-call | tf_op jit(solution)/shard_map/prepare_tables/pallas_call | solution.py:235
  56.8 0.7 copy-done.15
  57.4 25.5 %verify_layer.1 = (bf16[4,480,128]{2,1,0:T(8,128)(2,1)}, bf16[4,480,128]{2,1,0:T(8,128)(2,1)}, bf16[4,480,128]{2,1,0:T(8,128)(2,1)}, bf16[4,480,128]{2,1,0:T(8,1...) custom-call(s32[32]{0:T(128)} %lengths.1, ...), custom_call_target="tpu_custom_call" | custom-call | flops 30000001024 | bytes 10000000 | tf_op jit(solution)/shard_map/verify_layer/pallas_call | solution.py:439
  82.9 0.6 collective-permute-start.10
  83.5 0.9 collective-permute-start.8
  84.5 4.2 %collective-permute-done.10 = bf16[2,480,128]{2,1,0:T(8,128)(2,1)S(1)} collective-permute-done((bf16[2,480,128]{2,1,0:T(8,128)(2,1)}, bf16[2,480,128]{2,1,0:T(8,128)(2,1)S(1)}, u32[]{:S(2)}, u32[]{:S(2)}) %collective-permute-start.10) | collective-permute-done | bytes 245792 | tf_op jit(solution)/shard_map/ppermute | solution.py:531
  88.7 1.7 %fusion.3 = bf16[4,480,128]{2,1,0:T(8,128)(2,1)} fusion(bf16[4,480,128]{2,1,0:T(8,128)(2,1)} %get-tuple-element.65, bf16[2,480,128]{2,1,0:T(8,128)(2,1)S(1)} %collective-permute-done.10), kind=kLoop, calls=%fused_computation.12 | loop fusion | flops 491520 | bytes 737280 | tf_op jit(solution)/shard_map/dynamic_update_slice | solution.py:540
  90.4 1.8 %collective-permute-start.11 = (bf16[4,480,128]{2,1,0:T(8,128)(2,1)}, bf16[4,480,128]{2,1,0:T(8,128)(2,1)S(1)}, u32[]{:S(2)}, u32[]{:S(2)}) collective-permute-start(bf16[4,480,128]{2,1,0:T(8,128)(2,1)} %fusion.3), channel_id=1, source_target_pairs={{0,7},{1,0},{2,1},{3,2},{4,3},{5,4},{6,5},{7,6},{8,15},{9,8},{10,9... | collective-permute-start | bytes 1474568 | tf_op jit(solution)/shard_map/ppermute | solution.py:531
  92.1 1.8 %fusion.2 = bf16[4,480,128]{2,1,0:T(8,128)(2,1)} fusion(bf16[4,480,128]{2,1,0:T(8,128)(2,1)} %get-tuple-element.62, bf16[2,480,128]{2,1,0:T(8,128)(2,1)S(1)} %collective-permute-done.8), kind=kLoop, calls=%fused_computation.11 | loop fusion | flops 491520 | bytes 737280 | tf_op jit(solution)/shard_map/dynamic_update_slice | solution.py:540
  93.9 4.9 %collective-permute-done.11 = bf16[4,480,128]{2,1,0:T(8,128)(2,1)S(1)} collective-permute-done((bf16[4,480,128]{2,1,0:T(8,128)(2,1)}, bf16[4,480,128]{2,1,0:T(8,128)(2,1)S(1)}, u32[]{:S(2)}, u32[]{:S(2)}) %collective-permute-start.11) | collective-permute-done | bytes 491552 | tf_op jit(solution)/shard_map/ppermute | solution.py:531
  98.8 1.2 add_convert_fusion.2
  99.9 3.5 %collective-permute-done.9 = bf16[4,480,128]{2,1,0:T(8,128)(2,1)S(1)} collective-permute-done((bf16[4,480,128]{2,1,0:T(8,128)(2,1)}, bf16[4,480,128]{2,1,0:T(8,128)(2,1)S(1)}, u32[]{:S(2)}, u32[]{:S(2)}) %collective-permute-start.9) | collective-permute-done | bytes 491552 | tf_op jit(solution)/shard_map/ppermute | solution.py:527
  103.4 0.9 add_convert_fusion.3
  104.3 7.3 %all-to-all-done.cache_ref = bf16[32,160,512]{2,1,0:T(8,128)(2,1)} async-done(((bf16[32,160,512]{2,1,0:T(8,128)(2,1)}), bf16[32,160,512]{2,1,0:T(8,128)(2,1)}, u32[]{:S(2)}, u32[]{:S(2)}) %all-to-all-start) | async-done | bytes 5242912 | tf_op jit(solution)/shard_map/all_to_all | solution.py:523
  111.6 2.7 %collective-permute-start.13 = (bf16[4,480,128]{2,1,0:T(8,128)(2,1)S(1)}, bf16[4,480,128]{2,1,0:T(8,128)(2,1)}, u32[]{:S(2)}, u32[]{:S(2)}) collective-permute-start(bf16[4,480,128]{2,1,0:T(8,128)(2,1)S(1)} %add_convert_fusion.2), channel_id=1, source_target_pairs={{0,7},{1,0},{2,1},{3,2},{4,3},{5,4},{6,5},{7,6},{8,15},{9,8},{10,9... | collective-permute-start | bytes 1474568 | tf_op jit(solution)/shard_map/ppermute | solution.py:531
  114.3 10.3 %all-to-all-start.1 = ((bf16[32,8,128]{2,1,0:T(8,128)(2,1)}), bf16[32,8,128]{2,1,0:T(8,128)(2,1)S(1)}, u32[]{:S(2)}, u32[]{:S(2)}) async-start(bf16[32,8,128]{2,1,0:T(8,128)(2,1)} %get-tuple-element.72), calls=%async_computation.1 | async-start | bytes 131072 | tf_op jit(solution)/shard_map/all_to_all | solution.py:523
  124.7 0.4 collective-permute-done.12
  125.0 1.9 %add_convert_fusion.1 = bf16[4,480,128]{2,1,0:T(8,128)(2,1)} fusion(bf16[4,480,128]{2,1,0:T(8,128)(2,1)} %collective-permute-done.12, bf16[4,480,128]{2,1,0:T(8,128)(2,1)S(1)} %copy-done.2), kind=kLoop, calls=%fused_computation.4 | loop fusion | flops 983040 | bytes 1474560 | tf_op jit(solution)/shard_map/convert_element_type | solution.py:535
  127.0 1.2 add_convert_fusion
  128.1 3.9 %all-to-all-done.1.extra_ref = bf16[32,8,128]{2,1,0:T(8,128)(2,1)S(1)} async-done(((bf16[32,8,128]{2,1,0:T(8,128)(2,1)}), bf16[32,8,128]{2,1,0:T(8,128)(2,1)S(1)}, u32[]{:S(2)}, u32[]{:S(2)}) %all-to-all-start.1) | async-done | bytes 65568 | tf_op jit(solution)/shard_map/all_to_all | solution.py:523
  132.0 2.7 %collective-permute-start.15 = (bf16[4,480,128]{2,1,0:T(8,128)(2,1)S(1)}, bf16[4,480,128]{2,1,0:T(8,128)(2,1)S(1)}, u32[]{:S(2)}, u32[]{:S(2)}) collective-permute-start(bf16[4,480,128]{2,1,0:T(8,128)(2,1)S(1)} %add_convert_fusion), channel_id=1, source_target_pairs={{0,7},{1,0},{2,1},{3,2},{4,3},{5,4},{6,5},{7,6},{8,15},{9,8},{10,9... | collective-permute-start | bytes 1474568 | tf_op jit(solution)/shard_map/ppermute | solution.py:531
  134.7 8.5 %assemble_cache.1 = bf16[32,160,512]{2,1,0:T(8,128)(2,1)} custom-call(bf16[32,160,512]{2,1,0:T(8,128)(2,1)} %all-to-all-done.cache_ref, bf16[32,8,128]{2,1,0:T(8,128)(2,1)} %copy-done.6), custom_call_target="tpu_custom_call" | custom-call | tf_op jit(solution)/shard_map/assemble_cache/pallas_call | solution.py:506
  143.2 2.7 %collective-permute-done.14.up_ref = bf16[4,480,128]{2,1,0:T(8,128)(2,1)S(1)} collective-permute-done((bf16[4,480,128]{2,1,0:T(8,128)(2,1)}, bf16[4,480,128]{2,1,0:T(8,128)(2,1)S(1)}, u32[]{:S(2)}, u32[]{:S(2)}) %collective-permute-start.14) | collective-permute-done | bytes 491552 | tf_op jit(solution)/shard_map/ppermute | solution.py:527
  145.9 0.8 copy-done.4
  146.6 0.2 copy-done.5
  146.8 2.6 %finish_rows.1 = bf16[768,320]{1,0:T(8,128)(2,1)} custom-call(s32[1]{0:T(128)} %bitcast.parity.me, bf16[4,480,128]{2,1,0:T(8,128)(2,1)} %get-tuple-element.59.own_ref, bf16[4,480,128]{2,1,0:T(8,128)(2,1)} %copy-done.4, bf16[4,480,128]{2,1,0:T(8,128)(2,1)} %copy-done.5, bf16[768,320]{1,0:T(8,128)(2,1)} %bitcast.6), custom_call_target="tpu_custom_call" | custom-call | tf_op jit(solution)/shard_map/finish_rows/pallas_call | solution.py:129
  (56 shorter events, 0.4 us)
Async XLA Ops:
  0.6 25.2 %copy-start = (bf16[2560,320]{0,1:T(8,128)(2,1)S(1)}, bf16[2560,320]{0,1:T(8,128)(2,1)}, u32[]{:S(2)}) copy-start(bf16[2560,320]{0,1:T(8,128)(2,1)} %param.12) | copy-start | bytes 4915204
  2.8 16.8 %collective-permute-start.1 = (bf16[4,480,128]{2,1,0:T(8,128)(2,1)}, bf16[4,480,128]{2,1,0:T(8,128)(2,1)S(1)}, u32[]{:S(2)}, u32[]{:S(2)}) collective-permute-start(bf16[4,480,128]{2,1,0:T(8,128)(2,1)} %pack_rows.1.refs_0_), channel_id=1, source_target_pairs={{0,7},{1,0},{2,1},{3,2},{4,3},{5,4},{6,5},{7,6},{8,15},{9,8},{10,9... | collective-permute-start | bytes 1474568 | tf_op jit(solution)/shard_map/ppermute | solution.py:531
  9.3 13.2 %collective-permute-start = (bf16[4,480,128]{2,1,0:T(8,128)(2,1)}, bf16[4,480,128]{2,1,0:T(8,128)(2,1)S(1)}, u32[]{:S(2)}, u32[]{:S(2)}) collective-permute-start(bf16[4,480,128]{2,1,0:T(8,128)(2,1)} %pack_rows.1.refs_0_), channel_id=1, source_target_pairs={{0,1},{1,2},{2,3},{3,4},{4,5},{5,6},{6,7},{7,0},{8,9},{9,10},{10,1... | collective-permute-start | bytes 1474568 | tf_op jit(solution)/shard_map/ppermute | solution.py:527
  10.0 6.6 %copy-start.18 = (s32[32]{0:T(128)}, s32[32]{0:T(128)S(1)}, u32[]{:S(2)}) copy-start(s32[32]{0:T(128)S(1)} %and_select_fusion.2.destination) | copy-start | bytes 388
  10.7 13.3 %copy-start.11 = (bf16[160,2560]{1,0:T(8,128)(2,1)S(1)}, bf16[160,2560]{1,0:T(8,128)(2,1)}, u32[]{:S(2)}) copy-start(bf16[160,2560]{1,0:T(8,128)(2,1)} %param.13) | copy-start | bytes 2457604
  10.7 13.3 %copy-start.16 = (f32[2560]{0:T(1024)S(1)}, f32[2560]{0:T(1024)}, u32[]{:S(2)}) copy-start(f32[2560]{0:T(1024)} %param.11) | copy-start | bytes 30724
  19.5 9.5 %copy-start.12 = (bf16[4,480,128]{2,1,0:T(8,128)(2,1)}, bf16[4,480,128]{2,1,0:T(8,128)(2,1)S(1)}, u32[]{:S(2)}) copy-start(bf16[4,480,128]{2,1,0:T(8,128)(2,1)S(1)} %collective-permute-done.1.refs_1_) | copy-start | bytes 1474564
  22.5 6.5 %copy-start.13 = (bf16[4,480,128]{2,1,0:T(8,128)(2,1)}, bf16[4,480,128]{2,1,0:T(8,128)(2,1)S(1)}, u32[]{:S(2)}) copy-start(bf16[4,480,128]{2,1,0:T(8,128)(2,1)S(1)} %collective-permute-done.refs_7_) | copy-start | bytes 1474564
  22.5 12.5 %collective-permute-start.3 = (bf16[4,480,128]{2,1,0:T(8,128)(2,1)S(1)}, bf16[4,480,128]{2,1,0:T(8,128)(2,1)S(1)}, u32[]{:S(2)}, u32[]{:S(2)}) collective-permute-start(bf16[4,480,128]{2,1,0:T(8,128)(2,1)S(1)} %collective-permute-done.1.refs_1_), channel_id=1, source_target_pairs={{0,7},{1,0},{2,1},{3,2},{4,3},{5,4},{6,5},{7,6},{8,15},{9,8},{10,9... | collective-permute-start | bytes 1474568 | tf_op jit(solution)/shard_map/ppermute | solution.py:531
  22.9 12.2 %collective-permute-start.2 = (bf16[4,480,128]{2,1,0:T(8,128)(2,1)S(1)}, bf16[4,480,128]{2,1,0:T(8,128)(2,1)}, u32[]{:S(2)}, u32[]{:S(2)}) collective-permute-start(bf16[4,480,128]{2,1,0:T(8,128)(2,1)S(1)} %collective-permute-done.refs_7_), channel_id=1, source_target_pairs={{0,1},{1,2},{2,3},{3,4},{4,5},{5,6},{6,7},{7,0},{8,9},{9,10},{10,1... | collective-permute-start | bytes 1474568 | tf_op jit(solution)/shard_map/ppermute | solution.py:527
  35.0 1.7 %copy-start.14 = (bf16[4,480,128]{2,1,0:T(8,128)(2,1)}, bf16[4,480,128]{2,1,0:T(8,128)(2,1)S(1)}, u32[]{:S(2)}) copy-start(bf16[4,480,128]{2,1,0:T(8,128)(2,1)S(1)} %collective-permute-done.3.refs_2_) | copy-start | bytes 1474564
  35.1 16.2 %copy-start.17 = (s32[32]{0:T(128)S(1)}, s32[32]{0:T(128)}, u32[]{:S(2)}) copy-start(s32[32]{0:T(128)} %lengths.1) | copy-start | bytes 388
  35.1 16.2 %copy-start.10 = (s32[32,4]{0,1:T(4,128)S(1)}, s32[32,4]{0,1:T(4,128)}, u32[]{:S(2)}) copy-start(s32[32,4]{0,1:T(4,128)} %param.18) | copy-start | bytes 1540
  35.1 18.3 %copy-start.9 = (s32[32,24]{0,1:T(8,128)S(1)}, s32[32,24]{0,1:T(8,128)}, u32[]{:S(2)}) copy-start(s32[32,24]{0,1:T(8,128)} %param.17) | copy-start | bytes 9220
  35.1 12.0 %collective-permute-start.5 = (bf16[4,480,128]{2,1,0:T(8,128)(2,1)S(1)}, bf16[4,480,128]{2,1,0:T(8,128)(2,1)S(1)}, u32[]{:S(2)}, u32[]{:S(2)}) collective-permute-start(bf16[4,480,128]{2,1,0:T(8,128)(2,1)S(1)} %collective-permute-done.3.refs_2_), channel_id=1, source_target_pairs={{0,7},{1,0},{2,1},{3,2},{4,3},{5,4},{6,5},{7,6},{8,15},{9,8},{10,9... | collective-permute-start | bytes 1474568 | tf_op jit(solution)/shard_map/ppermute | solution.py:531
  36.7 11.8 %collective-permute-start.4 = (bf16[4,480,128]{2,1,0:T(8,128)(2,1)}, bf16[4,480,128]{2,1,0:T(8,128)(2,1)S(1)}, u32[]{:S(2)}, u32[]{:S(2)}) collective-permute-start(bf16[4,480,128]{2,1,0:T(8,128)(2,1)} %collective-permute-done.2.refs_6_), channel_id=1, source_target_pairs={{0,1},{1,2},{2,3},{3,4},{4,5},{5,6},{6,7},{7,0},{8,9},{9,10},{10,1... | collective-permute-start | bytes 1474568 | tf_op jit(solution)/shard_map/ppermute | solution.py:527
  36.7 74.9 %all-to-all-start = ((bf16[32,160,512]{2,1,0:T(8,128)(2,1)}), bf16[32,160,512]{2,1,0:T(8,128)(2,1)}, u32[]{:S(2)}, u32[]{:S(2)}) async-start(bf16[32,160,512]{2,1,0:T(8,128)(2,1)} %order_cache.1), calls=%async_computation | async-start | bytes 10485760 | tf_op jit(solution)/shard_map/all_to_all | solution.py:523
  47.2 9.6 %copy-start.7 = (bf16[4,480,128]{2,1,0:T(8,128)(2,1)}, bf16[4,480,128]{2,1,0:T(8,128)(2,1)S(1)}, u32[]{:S(2)}) copy-start(bf16[4,480,128]{2,1,0:T(8,128)(2,1)S(1)} %collective-permute-done.5.refs_3_) | copy-start | bytes 1474564
  48.5 8.3 %copy-start.8 = (bf16[4,480,128]{2,1,0:T(8,128)(2,1)}, bf16[4,480,128]{2,1,0:T(8,128)(2,1)S(1)}, u32[]{:S(2)}) copy-start(bf16[4,480,128]{2,1,0:T(8,128)(2,1)S(1)} %collective-permute-done.4.refs_5_) | copy-start | bytes 1474564
  48.5 8.2 %collective-permute-start.6 = (bf16[2,480,128]{2,1,0:T(8,128)(2,1)S(1)}, bf16[2,480,128]{2,1,0:T(8,128)(2,1)S(1)}, u32[]{:S(2)}, u32[]{:S(2)}) collective-permute-start(bf16[2,480,128]{2,1,0:T(8,128)(2,1)S(1)} %slice.12), channel_id=1, source_target_pairs={{0,1},{1,2},{2,3},{3,4},{4,5},{5,6},{6,7},{7,0},{8,9},{9,10},{10,1... | collective-permute-start | bytes 737288 | tf_op jit(solution)/shard_map/ppermute | solution.py:527
  48.6 8.1 %collective-permute-start.7 = (bf16[2,480,128]{2,1,0:T(8,128)(2,1)S(1)}, bf16[2,480,128]{2,1,0:T(8,128)(2,1)}, u32[]{:S(2)}, u32[]{:S(2)}) collective-permute-start(bf16[2,480,128]{2,1,0:T(8,128)(2,1)S(1)} %slice.13), channel_id=1, source_target_pairs={{0,7},{1,0},{2,1},{3,2},{4,3},{5,4},{6,5},{7,6},{8,15},{9,8},{10,9... | collective-permute-start | bytes 737288 | tf_op jit(solution)/shard_map/ppermute | solution.py:531
  56.7 0.7 copy-start.15
  82.9 20.5 %copy-start.3 = (bf16[4,480,128]{2,1,0:T(8,128)(2,1)S(1)}, bf16[4,480,128]{2,1,0:T(8,128)(2,1)}, u32[]{:S(2)}) copy-start(bf16[4,480,128]{2,1,0:T(8,128)(2,1)} %get-tuple-element.61) | copy-start | bytes 1474564
  82.9 42.1 %copy-start.2 = (bf16[4,480,128]{2,1,0:T(8,128)(2,1)S(1)}, bf16[4,480,128]{2,1,0:T(8,128)(2,1)}, u32[]{:S(2)}) copy-start(bf16[4,480,128]{2,1,0:T(8,128)(2,1)} %get-tuple-element.60) | copy-start | bytes 1474564
  82.9 5.7 %collective-permute-start.10 = (bf16[2,480,128]{2,1,0:T(8,128)(2,1)}, bf16[2,480,128]{2,1,0:T(8,128)(2,1)S(1)}, u32[]{:S(2)}, u32[]{:S(2)}) collective-permute-start(bf16[2,480,128]{2,1,0:T(8,128)(2,1)} %get-tuple-element.66), channel_id=1, source_target_pairs={{0,7},{1,0},{2,1},{3,2},{4,3},{5,4},{6,5},{7,6},{8,15},{9,8},{10,9... | collective-permute-start | bytes 737288 | tf_op jit(solution)/shard_map/ppermute | solution.py:531
  83.5 8.6 %collective-permute-start.8 = (bf16[2,480,128]{2,1,0:T(8,128)(2,1)}, bf16[2,480,128]{2,1,0:T(8,128)(2,1)S(1)}, u32[]{:S(2)}, u32[]{:S(2)}) collective-permute-start(bf16[2,480,128]{2,1,0:T(8,128)(2,1)} %get-tuple-element.63), channel_id=1, source_target_pairs={{0,1},{1,2},{2,3},{3,4},{4,5},{5,6},{6,7},{7,0},{8,9},{9,10},{10,1... | collective-permute-start | bytes 737288 | tf_op jit(solution)/shard_map/ppermute | solution.py:527
  90.4 8.4 %collective-permute-start.11 = (bf16[4,480,128]{2,1,0:T(8,128)(2,1)}, bf16[4,480,128]{2,1,0:T(8,128)(2,1)S(1)}, u32[]{:S(2)}, u32[]{:S(2)}) collective-permute-start(bf16[4,480,128]{2,1,0:T(8,128)(2,1)} %fusion.3), channel_id=1, source_target_pairs={{0,7},{1,0},{2,1},{3,2},{4,3},{5,4},{6,5},{7,6},{8,15},{9,8},{10,9... | collective-permute-start | bytes 1474568 | tf_op jit(solution)/shard_map/ppermute | solution.py:531
  92.1 34.8 %copy-start.1 = (bf16[4,480,128]{2,1,0:T(8,128)(2,1)S(1)}, bf16[4,480,128]{2,1,0:T(8,128)(2,1)}, u32[]{:S(2)}) copy-start(bf16[4,480,128]{2,1,0:T(8,128)(2,1)} %get-tuple-element.70) | copy-start | bytes 1474564
  93.9 9.5 %collective-permute-start.9 = (bf16[4,480,128]{2,1,0:T(8,128)(2,1)}, bf16[4,480,128]{2,1,0:T(8,128)(2,1)S(1)}, u32[]{:S(2)}, u32[]{:S(2)}) collective-permute-start(bf16[4,480,128]{2,1,0:T(8,128)(2,1)} %fusion.2), channel_id=1, source_target_pairs={{0,1},{1,2},{2,3},{3,4},{4,5},{5,6},{6,7},{7,0},{8,9},{9,10},{10,1... | collective-permute-start | bytes 1474568 | tf_op jit(solution)/shard_map/ppermute | solution.py:527
  111.6 13.4 %collective-permute-start.12 = (bf16[4,480,128]{2,1,0:T(8,128)(2,1)}, bf16[4,480,128]{2,1,0:T(8,128)(2,1)}, u32[]{:S(2)}, u32[]{:S(2)}) collective-permute-start(bf16[4,480,128]{2,1,0:T(8,128)(2,1)} %add_convert_fusion.3), channel_id=1, source_target_pairs={{0,1},{1,2},{2,3},{3,4},{4,5},{5,6},{6,7},{7,0},{8,9},{9,10},{10,1... | collective-permute-start | bytes 1474568 | tf_op jit(solution)/shard_map/ppermute | solution.py:527
  111.6 15.3 %collective-permute-start.13 = (bf16[4,480,128]{2,1,0:T(8,128)(2,1)S(1)}, bf16[4,480,128]{2,1,0:T(8,128)(2,1)}, u32[]{:S(2)}, u32[]{:S(2)}) collective-permute-start(bf16[4,480,128]{2,1,0:T(8,128)(2,1)S(1)} %add_convert_fusion.2), channel_id=1, source_target_pairs={{0,7},{1,0},{2,1},{3,2},{4,3},{5,4},{6,5},{7,6},{8,15},{9,8},{10,9... | collective-permute-start | bytes 1474568 | tf_op jit(solution)/shard_map/ppermute | solution.py:531
  114.3 17.7 %all-to-all-start.1 = ((bf16[32,8,128]{2,1,0:T(8,128)(2,1)}), bf16[32,8,128]{2,1,0:T(8,128)(2,1)S(1)}, u32[]{:S(2)}, u32[]{:S(2)}) async-start(bf16[32,8,128]{2,1,0:T(8,128)(2,1)} %get-tuple-element.72), calls=%async_computation.1 | async-start | bytes 131072 | tf_op jit(solution)/shard_map/all_to_all | solution.py:523
  132.0 2.7 %copy-start.6 = (bf16[32,8,128]{2,1,0:T(8,128)(2,1)}, bf16[32,8,128]{2,1,0:T(8,128)(2,1)S(1)}, u32[]{:S(2)}) copy-start(bf16[32,8,128]{2,1,0:T(8,128)(2,1)S(1)} %all-to-all-done.1.extra_ref) | copy-start | bytes 196612
  132.0 13.8 %collective-permute-start.14 = (bf16[4,480,128]{2,1,0:T(8,128)(2,1)}, bf16[4,480,128]{2,1,0:T(8,128)(2,1)S(1)}, u32[]{:S(2)}, u32[]{:S(2)}) collective-permute-start(bf16[4,480,128]{2,1,0:T(8,128)(2,1)} %add_convert_fusion.1), channel_id=1, source_target_pairs={{0,1},{1,2},{2,3},{3,4},{4,5},{5,6},{6,7},{7,0},{8,9},{9,10},{10,1... | collective-permute-start | bytes 1474568 | tf_op jit(solution)/shard_map/ppermute | solution.py:527
  132.0 13.8 %collective-permute-start.15 = (bf16[4,480,128]{2,1,0:T(8,128)(2,1)S(1)}, bf16[4,480,128]{2,1,0:T(8,128)(2,1)S(1)}, u32[]{:S(2)}, u32[]{:S(2)}) collective-permute-start(bf16[4,480,128]{2,1,0:T(8,128)(2,1)S(1)} %add_convert_fusion), channel_id=1, source_target_pairs={{0,7},{1,0},{2,1},{3,2},{4,3},{5,4},{6,5},{7,6},{8,15},{9,8},{10,9... | collective-permute-start | bytes 1474568 | tf_op jit(solution)/shard_map/ppermute | solution.py:531
  145.9 0.8 copy-start.4
  145.9 0.9 copy-start.5

commit v9 on v8

--- a/solution.py
+++ b/solution.py
@@ -468,7 +468,7 @@
         ),
         compiler_params=pltpu.CompilerParams(vmem_limit_bytes=VMEM_LIMIT),
         cost_estimate=pl.CostEstimate(
-            flops=30_000_000_000, transcendentals=0, bytes_accessed=10_000_000
+            flops=24_000_000_000, transcendentals=0, bytes_accessed=10_000_000
         ),
         name="verify_layer",
     )(lengths, accepted, destination, *parts, w, wo, kv_cache, *tables)
@@ -551,18 +551,13 @@
             below = add_blocks(below, down, HALF_BLOCKS)
         else:
             above, below = add_up(above, up), add_up(below, down)
-        if step == 2:
+        if step == 3:
             above, below, cached, extra = lax.optimization_barrier(
                 (above, below, cached, extra)
             )
-            extra = exchange(extra)
-        if step == 3:
-            above, below, extra = lax.optimization_barrier((above, below, extra))
-            new_cache = assemble_cache(cached, extra)
         up = go_up(above)
         down = go_down(below)
-    up, down, new_cache = lax.optimization_barrier((up, down, new_cache))
-    return up, down, new_cache
+    return up, down, assemble_cache(cached, exchange(extra))
 
 
 def per_device(

time: 152 us -> 155 us (1.020); the launches traced: 149 us -> 154 us
  blocking collectives: 0 us -> 25.2 us
  starting transfers between devices: 41.7 us -> 31.9 us
  waiting for transfers between devices: 34 us -> 27.3 us
  other arithmetic: 10.9 us -> 7.18 us
    all_to_all x0 -> x1, blocking collectives: none -> 25.2 us  [exchange(): lax.all_to_all(values, 'req', split_axis=0, concat_axis=0, tiled=True)]
    all_to_all x2 -> x1, waiting for transfers between devices: 11.2 us -> 0.01 us  [exchange(): lax.all_to_all(values, 'req', split_axis=0, concat_axis=0, tiled=True)]
    all_to_all x2 -> x1, starting transfers between devices: 20.7 us -> 10.3 us  [exchange(): lax.all_to_all(values, 'req', split_axis=0, concat_axis=0, tiled=True)]
    ppermute x8, waiting for transfers between devices: 11.9 us -> 17.5 us  [go_down(): lax.ppermute(values, 'tp', [(i, (i - 1) % N_TP) for i in range(N_TP)])]
    convert_element_type x4, other arithmetic: 5.16 us -> 1.58 us  [add_up(): return (a.astype(F32) + b.astype(F32)).astype(BF)]
  transfers between devices with their start and end apart: 18 -> 17, of which waited for: 11 -> 9; matrix products, arithmetic and copies ran while one was open for 12% -> 9% of each run, Pallas kernels for 32% -> 31%
where the time goes in v9:
time: 155 us; the launch traced here: 154 us
  Pallas kernels  53.2 us (34%)
  starting transfers between devices  31.9 us (21%)
  waiting for transfers between devices  27.3 us (18%)
  blocking collectives  25.2 us (16%)
  other arithmetic  7.18 us (5%)
  matrix products  5.01 us (3%)
  local copies, waits for them, and re-layouts  3.56 us (2%)
    pallas_call x1, Pallas kernels, verify_layer(): pl.pallas_call(layer_kernel, out_shape=[jax.ShapeDtypeStruct((HALF_BLOCKS...  25.4 us
    all_to_all x1, blocking collectives, exchange(): lax.all_to_all(values, 'req', split_axis=0, concat_axis=0, tiled=True)  25.2 us
    ppermute x8, starting transfers between devices, go_down(): lax.ppermute(values, 'tp', [(i, (i - 1) % N_TP) for i in range(N_TP)])  19.4 us
    ppermute x8, waiting for transfers between devices, go_down(): lax.ppermute(values, 'tp', [(i, (i - 1) % N_TP) for i in range(N_TP)])  17.5 us
    all_to_all x1, starting transfers between devices, exchange(): lax.all_to_all(values, 'req', split_axis=0, concat_axis=0, tiled=True)  10.3 us
    ppermute x8, waiting for transfers between devices, go_up(): lax.ppermute(values, 'tp', [(i, (i + 1) % N_TP) for i in range(N_TP)])  9.74 us
    pallas_call x1, Pallas kernels, assemble_cache(): pl.pallas_call(assemble_kernel, out_shape=jax.ShapeDtypeStruct(cached.sha...  8.48 us
    pallas_call x1, Pallas kernels, arrange_weights(): pl.pallas_call(arrange_kernel, out_shape=(jax.ShapeDtypeStruct((D, (GROUP...  5.98 us
  transfers between devices with their start and end apart: 17, of which 9 were waited for; matrix products, arithmetic and copies ran while one was open for 9% of the time, Pallas kernels for 31%

profile of v9, /device:TPU:1, one launch (start us, length us, event | category | flops | bytes accessed | tf_op | source)
XLA Modules:
  0.0 154.2 jit_solution(2148802116753929700)
XLA Ops:
  0.6 2.1 %pack_rows.1.refs_0_ = bf16[4,480,128]{2,1,0:T(8,128)(2,1)} custom-call(s32[1]{0:T(128)} %bitcast.parity.me, bf16[768,320]{1,0:T(8,128)(2,1)} %bitcast.5), custom_call_target="tpu_custom_call" | custom-call | tf_op jit(solution)/shard_map/pack_rows/pallas_call | solution.py:73
  2.8 6.6 %collective-permute-start.1 = (bf16[4,480,128]{2,1,0:T(8,128)(2,1)}, bf16[4,480,128]{2,1,0:T(8,128)(2,1)S(1)}, u32[]{:S(2)}, u32[]{:S(2)}) collective-permute-start(bf16[4,480,128]{2,1,0:T(8,128)(2,1)} %pack_rows.1.refs_0_), channel_id=1, source_target_pairs={{0,7},{1,0},{2,1},{3,2},{4,3},{5,4},{6,5},{7,6},{8,15},{9,8},{10,9... | collective-permute-start | bytes 1474568 | tf_op jit(solution)/shard_map/ppermute | solution.py:531
  9.3 0.7 and_select_fusion.2.destination
  10.0 0.6 select_reduce_fusion.order
  10.6 6.0 %order_cache.1 = bf16[32,160,512]{2,1,0:T(8,128)(2,1)} custom-call(s32[32]{0:T(128)} %select_reduce_fusion.order, bf16[32,160,512]{2,1,0:T(8,128)(2,1)} %refs_11_.1), custom_call_target="tpu_custom_call" | custom-call | tf_op jit(solution)/shard_map/order_cache/pallas_call | solution.py:257
  16.6 2.9 %collective-permute-done.1.refs_1_ = bf16[4,480,128]{2,1,0:T(8,128)(2,1)S(1)} collective-permute-done((bf16[4,480,128]{2,1,0:T(8,128)(2,1)}, bf16[4,480,128]{2,1,0:T(8,128)(2,1)S(1)}, u32[]{:S(2)}, u32[]{:S(2)}) %collective-permute-start.1) | collective-permute-done | bytes 491552 | tf_op jit(solution)/shard_map/ppermute | solution.py:531
  19.5 3.0 %collective-permute-done.refs_7_ = bf16[4,480,128]{2,1,0:T(8,128)(2,1)S(1)} collective-permute-done((bf16[4,480,128]{2,1,0:T(8,128)(2,1)}, bf16[4,480,128]{2,1,0:T(8,128)(2,1)S(1)}, u32[]{:S(2)}, u32[]{:S(2)}) %collective-permute-start) | collective-permute-done | bytes 491552 | tf_op jit(solution)/shard_map/ppermute | solution.py:527
  22.5 0.4 collective-permute-start.3
  22.9 1.1 collective-permute-start.2
  24.0 1.9 %fusion.wkv_ref = bf16[2560,256]{1,0:T(8,128)(2,1)} fusion(bf16[160,2560]{1,0:T(8,128)(2,1)S(1)} %copy-done.10, f32[2560]{0:T(1024)S(1)} %copy-done.15, s32[160]{0:T(256)S(1)} %fusion.16), kind=kOutput, calls=%fused_computation.2 | convolution fusion | flops 211066880 | bytes 2140800 | tf_op jit(solution)/shard_map/dot_general | solution.py:584
  25.9 3.2 %multiply_convert_fusion.wq_ref = bf16[2560,512]{1,0:T(8,128)(2,1)} fusion(bf16[2560,320]{0,1:T(8,128)(2,1)S(1)} %copy-done, f32[2560]{0:T(1024)S(1)} %copy-done.15, s32[320]{0:T(512)S(1)} %fusion.10), kind=kOutput, calls=%fused_computation | convolution fusion | flops 841646080 | bytes 4271360 | tf_op jit(solution)/shard_map/dot_general | solution.py:588
  29.0 6.0 %arrange_weights.1 = (bf16[2560,768]{1,0:T(8,128)(2,1)}, bf16[512,2560]{1,0:T(8,128)(2,1)}) custom-call(s32[1]{0:T(128)} %bitcast.parity.me, bf16[2560,512]{1,0:T(8,128)(2,1)} %multiply_convert_fusion.wq_ref, bf16[2560,256]{1,0:T(8,128)(2,1)} %fusion.wkv_ref, bf16[320,2560]{1,0:T(8,128)(2,1)} %wo_ref.1), custom_call_target="tpu_custom_call" | custom-call | tf_op jit(solution)/shard_map/arrange_weights/pallas_call | solution.py:182
  35.0 0.1 collective-permute-done.2.refs_6_
  35.1 1.6 %collective-permute-start.5 = (bf16[4,480,128]{2,1,0:T(8,128)(2,1)S(1)}, bf16[4,480,128]{2,1,0:T(8,128)(2,1)S(1)}, u32[]{:S(2)}, u32[]{:S(2)}) collective-permute-start(bf16[4,480,128]{2,1,0:T(8,128)(2,1)S(1)} %collective-permute-done.3.refs_2_), channel_id=1, source_target_pairs={{0,7},{1,0},{2,1},{3,2},{4,3},{5,4},{6,5},{7,6},{8,15},{9,8},{10,9... | collective-permute-start | bytes 1474568 | tf_op jit(solution)/shard_map/ppermute | solution.py:531
  36.7 10.3 %all-to-all-start = ((bf16[32,160,512]{2,1,0:T(8,128)(2,1)}), bf16[32,160,512]{2,1,0:T(8,128)(2,1)}, u32[]{:S(2)}, u32[]{:S(2)}) async-start(bf16[32,160,512]{2,1,0:T(8,128)(2,1)} %order_cache.1), calls=%async_computation | async-start | bytes 10485760 | tf_op jit(solution)/shard_map/all_to_all | solution.py:523
  47.2 1.3 collective-permute-done.4.refs_5_
  48.5 0.1 collective-permute-start.6
  48.6 2.7 %collective-permute-start.7 = (bf16[2,480,128]{2,1,0:T(8,128)(2,1)S(1)}, bf16[2,480,128]{2,1,0:T(8,128)(2,1)}, u32[]{:S(2)}, u32[]{:S(2)}) collective-permute-start(bf16[2,480,128]{2,1,0:T(8,128)(2,1)S(1)} %slice.13), channel_id=1, source_target_pairs={{0,7},{1,0},{2,1},{3,2},{4,3},{5,4},{6,5},{7,6},{8,15},{9,8},{10,9... | collective-permute-start | bytes 737288 | tf_op jit(solution)/shard_map/ppermute | solution.py:531
  51.3 0.1 copy.16
  51.4 0.7 reshape.146.accepted
  52.1 0.6 stack.2.step_ref
  52.7 0.7 multiply_sine_fusion
  53.4 0.7 copy.17.parents_ref
  54.1 2.6 %prepare_tables.1 = (f32[32,24,128]{2,1,0:T(8,128)}, f32[32,24,128]{2,1,0:T(8,128)}, f32[32,24,128]{2,1,0:T(8,128)}) custom-call(s32[32,24]{1,0:T(8,128)} %copy.17.parents_ref, f32[32,128]{1,0:T(8,128)} %get-tuple-element.69.cos_ref, f32[32,128]{1,0:T(8,128)} %get-tuple-element.68.sin_ref, f32[8,128]{1,0:T(8,128)} %stack.2.step_ref), custom_call_target="tpu_custom_call" | custom-call | tf_op jit(solution)/shard_map/prepare_tables/pallas_call | solution.py:235
  56.7 0.7 copy-done.14
  57.4 25.4 %verify_layer.1 = (bf16[4,480,128]{2,1,0:T(8,128)(2,1)}, bf16[4,480,128]{2,1,0:T(8,128)(2,1)}, bf16[4,480,128]{2,1,0:T(8,128)(2,1)}, bf16[4,480,128]{2,1,0:T(8,1...) custom-call(s32[32]{0:T(128)} %lengths.1, ...), custom_call_target="tpu_custom_call" | custom-call | flops 24000000000 | bytes 10000000 | tf_op jit(solution)/shard_map/verify_layer/pallas_call | solution.py:439
  82.9 0.7 collective-permute-start.11
  83.5 0.9 collective-permute-start.8
  84.4 4.2 %collective-permute-done.11 = bf16[2,480,128]{2,1,0:T(8,128)(2,1)S(1)} collective-permute-done((bf16[2,480,128]{2,1,0:T(8,128)(2,1)}, bf16[2,480,128]{2,1,0:T(8,128)(2,1)S(1)}, u32[]{:S(2)}, u32[]{:S(2)}) %collective-permute-start.11) | collective-permute-done | bytes 245792 | tf_op jit(solution)/shard_map/ppermute | solution.py:531
  88.6 1.7 %fusion.3 = bf16[4,480,128]{2,1,0:T(8,128)(2,1)} fusion(bf16[4,480,128]{2,1,0:T(8,128)(2,1)} %get-tuple-element.60, bf16[2,480,128]{2,1,0:T(8,128)(2,1)S(1)} %collective-permute-done.11), kind=kLoop, calls=%fused_computation.12 | loop fusion | flops 491520 | bytes 737280 | tf_op jit(solution)/shard_map/dynamic_update_slice | solution.py:540
  90.3 1.8 %collective-permute-start.12 = (bf16[4,480,128]{2,1,0:T(8,128)(2,1)}, bf16[4,480,128]{2,1,0:T(8,128)(2,1)S(1)}, u32[]{:S(2)}, u32[]{:S(2)}) collective-permute-start(bf16[4,480,128]{2,1,0:T(8,128)(2,1)} %fusion.3), channel_id=1, source_target_pairs={{0,7},{1,0},{2,1},{3,2},{4,3},{5,4},{6,5},{7,6},{8,15},{9,8},{10,9... | collective-permute-start | bytes 1474568 | tf_op jit(solution)/shard_map/ppermute | solution.py:531
  92.1 1.7 %fusion.2 = bf16[4,480,128]{2,1,0:T(8,128)(2,1)} fusion(bf16[4,480,128]{2,1,0:T(8,128)(2,1)} %get-tuple-element.56, bf16[2,480,128]{2,1,0:T(8,128)(2,1)S(1)} %collective-permute-done.8), kind=kLoop, calls=%fused_computation.11 | loop fusion | flops 491520 | bytes 737280 | tf_op jit(solution)/shard_map/dynamic_update_slice | solution.py:540
  93.9 4.9 %collective-permute-done.12 = bf16[4,480,128]{2,1,0:T(8,128)(2,1)S(1)} collective-permute-done((bf16[4,480,128]{2,1,0:T(8,128)(2,1)}, bf16[4,480,128]{2,1,0:T(8,128)(2,1)S(1)}, u32[]{:S(2)}, u32[]{:S(2)}) %collective-permute-start.12) | collective-permute-done | bytes 491552 | tf_op jit(solution)/shard_map/ppermute | solution.py:531
  98.7 1.2 add_convert_fusion.1
  99.9 3.0 %collective-permute-start.13 = (bf16[4,480,128]{2,1,0:T(8,128)(2,1)S(1)}, bf16[4,480,128]{2,1,0:T(8,128)(2,1)S(1)}, u32[]{:S(2)}, u32[]{:S(2)}) collective-permute-start(bf16[4,480,128]{2,1,0:T(8,128)(2,1)S(1)} %add_convert_fusion.1), channel_id=1, source_target_pairs={{0,7},{1,0},{2,1},{3,2},{4,3},{5,4},{6,5},{7,6},{8,15},{9,8},{10,9... | collective-permute-start | bytes 1474568 | tf_op jit(solution)/shard_map/ppermute | solution.py:531
  102.9 0.4 collective-permute-done.9
  103.4 0.1 add_convert_fusion.3
  103.5 0.1 collective-permute-start.10
  103.6 5.6 %collective-permute-done.13 = bf16[4,480,128]{2,1,0:T(8,128)(2,1)S(1)} collective-permute-done((bf16[4,480,128]{2,1,0:T(8,128)(2,1)S(1)}, bf16[4,480,128]{2,1,0:T(8,128)(2,1)S(1)}, u32[]{:S(2)}, u32[]{:S(2)}) %collective-permute-start.13) | collective-permute-done | bytes 491552 | tf_op jit(solution)/shard_map/ppermute | solution.py:531
  109.1 0.1 add_convert_fusion
  109.3 4.9 %collective-permute-done.10 = bf16[4,480,128]{2,1,0:T(8,128)(2,1)S(1)} collective-permute-done((bf16[4,480,128]{2,1,0:T(8,128)(2,1)S(1)}, bf16[4,480,128]{2,1,0:T(8,128)(2,1)S(1)}, u32[]{:S(2)}, u32[]{:S(2)}) %collective-permute-start.10) | collective-permute-done | bytes 491552 | tf_op jit(solution)/shard_map/ppermute | solution.py:527
  114.2 0.1 add_convert_fusion.2
  114.3 0.1 collective-permute-start.14
  114.4 2.7 %collective-permute-start.15 = (bf16[4,480,128]{2,1,0:T(8,128)(2,1)S(1)}, bf16[4,480,128]{2,1,0:T(8,128)(2,1)}, u32[]{:S(2)}, u32[]{:S(2)}) collective-permute-start(bf16[4,480,128]{2,1,0:T(8,128)(2,1)S(1)} %add_convert_fusion), channel_id=1, source_target_pairs={{0,7},{1,0},{2,1},{3,2},{4,3},{5,4},{6,5},{7,6},{8,15},{9,8},{10,9... | collective-permute-start | bytes 1474568 | tf_op jit(solution)/shard_map/ppermute | solution.py:531
  117.1 25.2 %all_to_all.10.extra_ref = bf16[32,8,128]{2,1,0:T(8,128)(2,1)} all-to-all(bf16[32,8,128]{2,1,0:T(8,128)(2,1)S(1)} %copy-done.7), channel_id=1, replica_groups=mesh['req'=32,'tp'=8] {'req'}, dimensions={0} | all-to-all | bytes 131072 | tf_op jit(solution)/shard_map/all_to_all | solution.py:523
  142.3 8.5 %assemble_cache.1 = bf16[32,160,512]{2,1,0:T(8,128)(2,1)} custom-call(bf16[32,160,512]{2,1,0:T(8,128)(2,1)} %all-to-all-done.cache_ref, bf16[32,8,128]{2,1,0:T(8,128)(2,1)} %all_to_all.10.extra_ref), custom_call_target="tpu_custom_call" | custom-call | tf_op jit(solution)/shard_map/assemble_cache/pallas_call | solution.py:506
  150.8 0.8 copy-done.4
  151.5 2.6 %finish_rows.1 = bf16[768,320]{1,0:T(8,128)(2,1)} custom-call(s32[1]{0:T(128)} %bitcast.parity.me, bf16[4,480,128]{2,1,0:T(8,128)(2,1)} %get-tuple-element.53.own_ref, bf16[4,480,128]{2,1,0:T(8,128)(2,1)} %copy-done.4, bf16[4,480,128]{2,1,0:T(8,128)(2,1)} %collective-permute-done.15.down_ref, bf16[768,320]{1,0:T(8,128)(2,1)} %bitcast.6), custom_call_target="tpu_custom_call" | custom-call | tf_op jit(solution)/shard_map/finish_rows/pallas_call | solution.py:129
  (53 shorter events, 0.3 us)
Async XLA Ops:
  0.6 25.2 %copy-start = (bf16[2560,320]{0,1:T(8,128)(2,1)S(1)}, bf16[2560,320]{0,1:T(8,128)(2,1)}, u32[]{:S(2)}) copy-start(bf16[2560,320]{0,1:T(8,128)(2,1)} %param.12) | copy-start | bytes 4915204
  2.8 16.8 %collective-permute-start.1 = (bf16[4,480,128]{2,1,0:T(8,128)(2,1)}, bf16[4,480,128]{2,1,0:T(8,128)(2,1)S(1)}, u32[]{:S(2)}, u32[]{:S(2)}) collective-permute-start(bf16[4,480,128]{2,1,0:T(8,128)(2,1)} %pack_rows.1.refs_0_), channel_id=1, source_target_pairs={{0,7},{1,0},{2,1},{3,2},{4,3},{5,4},{6,5},{7,6},{8,15},{9,8},{10,9... | collective-permute-start | bytes 1474568 | tf_op jit(solution)/shard_map/ppermute | solution.py:531
  9.3 13.2 %collective-permute-start = (bf16[4,480,128]{2,1,0:T(8,128)(2,1)}, bf16[4,480,128]{2,1,0:T(8,128)(2,1)S(1)}, u32[]{:S(2)}, u32[]{:S(2)}) collective-permute-start(bf16[4,480,128]{2,1,0:T(8,128)(2,1)} %pack_rows.1.refs_0_), channel_id=1, source_target_pairs={{0,1},{1,2},{2,3},{3,4},{4,5},{5,6},{6,7},{7,0},{8,9},{9,10},{10,1... | collective-permute-start | bytes 1474568 | tf_op jit(solution)/shard_map/ppermute | solution.py:527
  10.0 6.6 %copy-start.17 = (s32[32]{0:T(128)}, s32[32]{0:T(128)S(1)}, u32[]{:S(2)}) copy-start(s32[32]{0:T(128)S(1)} %and_select_fusion.2.destination) | copy-start | bytes 388
  10.6 13.4 %copy-start.10 = (bf16[160,2560]{1,0:T(8,128)(2,1)S(1)}, bf16[160,2560]{1,0:T(8,128)(2,1)}, u32[]{:S(2)}) copy-start(bf16[160,2560]{1,0:T(8,128)(2,1)} %param.13) | copy-start | bytes 2457604
  10.6 13.4 %copy-start.15 = (f32[2560]{0:T(1024)S(1)}, f32[2560]{0:T(1024)}, u32[]{:S(2)}) copy-start(f32[2560]{0:T(1024)} %param.11) | copy-start | bytes 30724
  19.5 9.5 %copy-start.11 = (bf16[4,480,128]{2,1,0:T(8,128)(2,1)}, bf16[4,480,128]{2,1,0:T(8,128)(2,1)S(1)}, u32[]{:S(2)}) copy-start(bf16[4,480,128]{2,1,0:T(8,128)(2,1)S(1)} %collective-permute-done.1.refs_1_) | copy-start | bytes 1474564
  22.5 6.5 %copy-start.12 = (bf16[4,480,128]{2,1,0:T(8,128)(2,1)}, bf16[4,480,128]{2,1,0:T(8,128)(2,1)S(1)}, u32[]{:S(2)}) copy-start(bf16[4,480,128]{2,1,0:T(8,128)(2,1)S(1)} %collective-permute-done.refs_7_) | copy-start | bytes 1474564
  22.5 12.5 %collective-permute-start.3 = (bf16[4,480,128]{2,1,0:T(8,128)(2,1)S(1)}, bf16[4,480,128]{2,1,0:T(8,128)(2,1)S(1)}, u32[]{:S(2)}, u32[]{:S(2)}) collective-permute-start(bf16[4,480,128]{2,1,0:T(8,128)(2,1)S(1)} %collective-permute-done.1.refs_1_), channel_id=1, source_target_pairs={{0,7},{1,0},{2,1},{3,2},{4,3},{5,4},{6,5},{7,6},{8,15},{9,8},{10,9... | collective-permute-start | bytes 1474568 | tf_op jit(solution)/shard_map/ppermute | solution.py:531
  22.9 12.2 %collective-permute-start.2 = (bf16[4,480,128]{2,1,0:T(8,128)(2,1)S(1)}, bf16[4,480,128]{2,1,0:T(8,128)(2,1)}, u32[]{:S(2)}, u32[]{:S(2)}) collective-permute-start(bf16[4,480,128]{2,1,0:T(8,128)(2,1)S(1)} %collective-permute-done.refs_7_), channel_id=1, source_target_pairs={{0,1},{1,2},{2,3},{3,4},{4,5},{5,6},{6,7},{7,0},{8,9},{9,10},{10,1... | collective-permute-start | bytes 1474568 | tf_op jit(solution)/shard_map/ppermute | solution.py:527
  35.0 1.7 %copy-start.13 = (bf16[4,480,128]{2,1,0:T(8,128)(2,1)}, bf16[4,480,128]{2,1,0:T(8,128)(2,1)S(1)}, u32[]{:S(2)}) copy-start(bf16[4,480,128]{2,1,0:T(8,128)(2,1)S(1)} %collective-permute-done.3.refs_2_) | copy-start | bytes 1474564
  35.1 16.2 %copy-start.16 = (s32[32]{0:T(128)S(1)}, s32[32]{0:T(128)}, u32[]{:S(2)}) copy-start(s32[32]{0:T(128)} %lengths.1) | copy-start | bytes 388
  35.1 16.2 %copy-start.9 = (s32[32,4]{0,1:T(4,128)S(1)}, s32[32,4]{0,1:T(4,128)}, u32[]{:S(2)}) copy-start(s32[32,4]{0,1:T(4,128)} %param.18) | copy-start | bytes 1540
  35.1 18.3 %copy-start.8 = (s32[32,24]{0,1:T(8,128)S(1)}, s32[32,24]{0,1:T(8,128)}, u32[]{:S(2)}) copy-start(s32[32,24]{0,1:T(8,128)} %param.17) | copy-start | bytes 9220
  35.1 12.0 %collective-permute-start.5 = (bf16[4,480,128]{2,1,0:T(8,128)(2,1)S(1)}, bf16[4,480,128]{2,1,0:T(8,128)(2,1)S(1)}, u32[]{:S(2)}, u32[]{:S(2)}) collective-permute-start(bf16[4,480,128]{2,1,0:T(8,128)(2,1)S(1)} %collective-permute-done.3.refs_2_), channel_id=1, source_target_pairs={{0,7},{1,0},{2,1},{3,2},{4,3},{5,4},{6,5},{7,6},{8,15},{9,8},{10,9... | collective-permute-start | bytes 1474568 | tf_op jit(solution)/shard_map/ppermute | solution.py:531
  36.7 11.8 %collective-permute-start.4 = (bf16[4,480,128]{2,1,0:T(8,128)(2,1)}, bf16[4,480,128]{2,1,0:T(8,128)(2,1)S(1)}, u32[]{:S(2)}, u32[]{:S(2)}) collective-permute-start(bf16[4,480,128]{2,1,0:T(8,128)(2,1)} %collective-permute-done.2.refs_6_), channel_id=1, source_target_pairs={{0,1},{1,2},{2,3},{3,4},{4,5},{5,6},{6,7},{7,0},{8,9},{9,10},{10,1... | collective-permute-start | bytes 1474568 | tf_op jit(solution)/shard_map/ppermute | solution.py:527
  36.7 77.5 %all-to-all-start = ((bf16[32,160,512]{2,1,0:T(8,128)(2,1)}), bf16[32,160,512]{2,1,0:T(8,128)(2,1)}, u32[]{:S(2)}, u32[]{:S(2)}) async-start(bf16[32,160,512]{2,1,0:T(8,128)(2,1)} %order_cache.1), calls=%async_computation | async-start | bytes 10485760 | tf_op jit(solution)/shard_map/all_to_all | solution.py:523
  47.2 9.5 %copy-start.5 = (bf16[4,480,128]{2,1,0:T(8,128)(2,1)}, bf16[4,480,128]{2,1,0:T(8,128)(2,1)S(1)}, u32[]{:S(2)}) copy-start(bf16[4,480,128]{2,1,0:T(8,128)(2,1)S(1)} %collective-permute-done.5.refs_3_) | copy-start | bytes 1474564
  48.5 8.2 %copy-start.6 = (bf16[4,480,128]{2,1,0:T(8,128)(2,1)}, bf16[4,480,128]{2,1,0:T(8,128)(2,1)S(1)}, u32[]{:S(2)}) copy-start(bf16[4,480,128]{2,1,0:T(8,128)(2,1)S(1)} %collective-permute-done.4.refs_5_) | copy-start | bytes 1474564
  48.5 8.2 %collective-permute-start.6 = (bf16[2,480,128]{2,1,0:T(8,128)(2,1)S(1)}, bf16[2,480,128]{2,1,0:T(8,128)(2,1)S(1)}, u32[]{:S(2)}, u32[]{:S(2)}) collective-permute-start(bf16[2,480,128]{2,1,0:T(8,128)(2,1)S(1)} %slice.12), channel_id=1, source_target_pairs={{0,1},{1,2},{2,3},{3,4},{4,5},{5,6},{6,7},{7,0},{8,9},{9,10},{10,1... | collective-permute-start | bytes 737288 | tf_op jit(solution)/shard_map/ppermute | solution.py:527
  48.6 8.1 %collective-permute-start.7 = (bf16[2,480,128]{2,1,0:T(8,128)(2,1)S(1)}, bf16[2,480,128]{2,1,0:T(8,128)(2,1)}, u32[]{:S(2)}, u32[]{:S(2)}) collective-permute-start(bf16[2,480,128]{2,1,0:T(8,128)(2,1)S(1)} %slice.13), channel_id=1, source_target_pairs={{0,7},{1,0},{2,1},{3,2},{4,3},{5,4},{6,5},{7,6},{8,15},{9,8},{10,9... | collective-permute-start | bytes 737288 | tf_op jit(solution)/shard_map/ppermute | solution.py:531
  56.7 0.7 copy-start.14
  82.8 20.5 %copy-start.3 = (bf16[4,480,128]{2,1,0:T(8,128)(2,1)S(1)}, bf16[4,480,128]{2,1,0:T(8,128)(2,1)}, u32[]{:S(2)}) copy-start(bf16[4,480,128]{2,1,0:T(8,128)(2,1)} %get-tuple-element.55) | copy-start | bytes 1474564
  82.8 26.3 %copy-start.2 = (bf16[4,480,128]{2,1,0:T(8,128)(2,1)S(1)}, bf16[4,480,128]{2,1,0:T(8,128)(2,1)}, u32[]{:S(2)}) copy-start(bf16[4,480,128]{2,1,0:T(8,128)(2,1)} %get-tuple-element.58) | copy-start | bytes 1474564
  82.9 5.7 %collective-permute-start.11 = (bf16[2,480,128]{2,1,0:T(8,128)(2,1)}, bf16[2,480,128]{2,1,0:T(8,128)(2,1)S(1)}, u32[]{:S(2)}, u32[]{:S(2)}) collective-permute-start(bf16[2,480,128]{2,1,0:T(8,128)(2,1)} %get-tuple-element.61), channel_id=1, source_target_pairs={{0,7},{1,0},{2,1},{3,2},{4,3},{5,4},{6,5},{7,6},{8,15},{9,8},{10,9... | collective-permute-start | bytes 737288 | tf_op jit(solution)/shard_map/ppermute | solution.py:531
  83.5 8.6 %collective-permute-start.8 = (bf16[2,480,128]{2,1,0:T(8,128)(2,1)}, bf16[2,480,128]{2,1,0:T(8,128)(2,1)S(1)}, u32[]{:S(2)}, u32[]{:S(2)}) collective-permute-start(bf16[2,480,128]{2,1,0:T(8,128)(2,1)} %get-tuple-element.57), channel_id=1, source_target_pairs={{0,1},{1,2},{2,3},{3,4},{4,5},{5,6},{6,7},{7,0},{8,9},{9,10},{10,1... | collective-permute-start | bytes 737288 | tf_op jit(solution)/shard_map/ppermute | solution.py:527
  90.3 23.8 %copy-start.1 = (bf16[4,480,128]{2,1,0:T(8,128)(2,1)S(1)}, bf16[4,480,128]{2,1,0:T(8,128)(2,1)}, u32[]{:S(2)}) copy-start(bf16[4,480,128]{2,1,0:T(8,128)(2,1)} %get-tuple-element.54) | copy-start | bytes 1474564
  90.3 8.4 %collective-permute-start.12 = (bf16[4,480,128]{2,1,0:T(8,128)(2,1)}, bf16[4,480,128]{2,1,0:T(8,128)(2,1)S(1)}, u32[]{:S(2)}, u32[]{:S(2)}) collective-permute-start(bf16[4,480,128]{2,1,0:T(8,128)(2,1)} %fusion.3), channel_id=1, source_target_pairs={{0,7},{1,0},{2,1},{3,2},{4,3},{5,4},{6,5},{7,6},{8,15},{9,8},{10,9... | collective-permute-start | bytes 1474568 | tf_op jit(solution)/shard_map/ppermute | solution.py:531
  93.9 9.5 %collective-permute-start.9 = (bf16[4,480,128]{2,1,0:T(8,128)(2,1)}, bf16[4,480,128]{2,1,0:T(8,128)(2,1)S(1)}, u32[]{:S(2)}, u32[]{:S(2)}) collective-permute-start(bf16[4,480,128]{2,1,0:T(8,128)(2,1)} %fusion.2), channel_id=1, source_target_pairs={{0,1},{1,2},{2,3},{3,4},{4,5},{5,6},{6,7},{7,0},{8,9},{9,10},{10,1... | collective-permute-start | bytes 1474568 | tf_op jit(solution)/shard_map/ppermute | solution.py:527
  98.7 18.3 %copy-start.7 = (bf16[32,8,128]{2,1,0:T(8,128)(2,1)S(1)}, bf16[32,8,128]{2,1,0:T(8,128)(2,1)}, u32[]{:S(2)}) copy-start(bf16[32,8,128]{2,1,0:T(8,128)(2,1)} %get-tuple-element.67) | copy-start | bytes 196612
  99.9 9.2 %collective-permute-start.13 = (bf16[4,480,128]{2,1,0:T(8,128)(2,1)S(1)}, bf16[4,480,128]{2,1,0:T(8,128)(2,1)S(1)}, u32[]{:S(2)}, u32[]{:S(2)}) collective-permute-start(bf16[4,480,128]{2,1,0:T(8,128)(2,1)S(1)} %add_convert_fusion.1), channel_id=1, source_target_pairs={{0,7},{1,0},{2,1},{3,2},{4,3},{5,4},{6,5},{7,6},{8,15},{9,8},{10,9... | collective-permute-start | bytes 1474568 | tf_op jit(solution)/shard_map/ppermute | solution.py:531
  103.5 10.7 %collective-permute-start.10 = (bf16[4,480,128]{2,1,0:T(8,128)(2,1)S(1)}, bf16[4,480,128]{2,1,0:T(8,128)(2,1)S(1)}, u32[]{:S(2)}, u32[]{:S(2)}) collective-permute-start(bf16[4,480,128]{2,1,0:T(8,128)(2,1)S(1)} %add_convert_fusion.3), channel_id=1, source_target_pairs={{0,1},{1,2},{2,3},{3,4},{4,5},{5,6},{6,7},{7,0},{8,9},{9,10},{10,1... | collective-permute-start | bytes 1474568 | tf_op jit(solution)/shard_map/ppermute | solution.py:527
  114.3 36.5 %collective-permute-start.14 = (bf16[4,480,128]{2,1,0:T(8,128)(2,1)S(1)}, bf16[4,480,128]{2,1,0:T(8,128)(2,1)S(1)}, u32[]{:S(2)}, u32[]{:S(2)}) collective-permute-start(bf16[4,480,128]{2,1,0:T(8,128)(2,1)S(1)} %add_convert_fusion.2), channel_id=1, source_target_pairs={{0,1},{1,2},{2,3},{3,4},{4,5},{5,6},{6,7},{7,0},{8,9},{9,10},{10,1... | collective-permute-start | bytes 1474568 | tf_op jit(solution)/shard_map/ppermute | solution.py:527
  114.4 36.4 %collective-permute-start.15 = (bf16[4,480,128]{2,1,0:T(8,128)(2,1)S(1)}, bf16[4,480,128]{2,1,0:T(8,128)(2,1)}, u32[]{:S(2)}, u32[]{:S(2)}) collective-permute-start(bf16[4,480,128]{2,1,0:T(8,128)(2,1)S(1)} %add_convert_fusion), channel_id=1, source_target_pairs={{0,7},{1,0},{2,1},{3,2},{4,3},{5,4},{6,5},{7,6},{8,15},{9,8},{10,9... | collective-permute-start | bytes 1474568 | tf_op jit(solution)/shard_map/ppermute | solution.py:531
  150.8 0.8 copy-start.4
